TPU v7x, 32 devices: a whole 2x2x4 slice. The times are simulated.
32 devices in a mesh: rec: 8 (over z, core), frame: 4 (over y, x).
Axes of the slice: x: 2, y: 2, z: 4, core: 2. Of those that a mesh axis runs over, the one named last changes fastest.
Arguments:
- frames: bfloat16 [8, 6144, 256], P('rec', 'frame'), may hold values from -10 to 10
- texts: bfloat16 [16, 224, 256], P('rec', 'frame'), may hold values from -100 to 100
- pair_rec: int32 [16, 1], replicated, may hold values from 0 to 7, as said below
- pair_text: int32 [16], replicated, may hold values from 0 to 15, as said below
- pair_label: int32 [16], replicated, may hold values 0 or 1
Outputs:
- loss: float32 [], replicated
- grad_frames: bfloat16 [8, 6144, 256], P('rec', 'frame')
- grad_texts: bfloat16 [16, 224, 256], P('rec', 'frame')
Inputs may be any that keep to these rules, and one draw needn't show every extreme that they name: `pair_rec`: no recording is named by more than 6 pairs, some recording by exactly 6, and every recording by at least one. A pair's text is held by the index of rec one after, one before, or 4 after its recording (counted round): pair_text // 2 = (pair_rec + k) mod 8 with k one of 1, 7, 4.
All inputs are finite; a program needn't handle non-finite values.
Results may differ from a plain program's by a relative error of at most 0.0085.
Values may be sent and summed in bfloat16 or wider, within the bound.
No kernel may reach another device: no remote copies, remote signals or barrier semaphores. Data moves between devices by JAX's collectives and lax.ppermute only.
A program may use at most 64 MiB of HBM per device.

v0:
```python
import functools

import jax
import jax.numpy as jnp
from jax import lax
from jax.experimental import pallas as pl
from jax.experimental.pallas import tpu as pltpu
from jax.sharding import PartitionSpec as P

MOST = 6
EPS = 1e-06
TEMP = 10.0
BIAS = -1.0
LOSS_SCALE = 2048.0

F32 = jnp.float32
BF16 = jnp.bfloat16
EXTRA = 16
LINES = 8
AXES = ("rec", "frame")
VMEM = pl.BlockSpec(memory_space=pltpu.VMEM)
SMEM = pl.BlockSpec(memory_space=pltpu.SMEM)


def nt(a, b):
    return lax.dot_general(a, b, (((1,), (1,)), ((), ())), preferred_element_type=F32)


def nn(a, b):
    return lax.dot_general(a, b, (((1,), (0,)), ((), ())), preferred_element_type=F32)


def slot_tables(pair_rec, pair_text, pair_label, here, most):
    record = pair_rec[:, 0]
    count = record.shape[0]
    order = jnp.arange(count, dtype=jnp.int32)
    same = (record[:, None] == record[None, :]).astype(jnp.int32)
    earlier = (order[None, :] < order[:, None]).astype(jnp.int32)
    rank = jnp.sum(same * earlier, axis=1)
    places = jnp.arange(most, dtype=jnp.int32)
    chosen = ((record[None, :] == here) & (rank[None, :] == places[:, None])).astype(jnp.int32)
    valid = jnp.sum(chosen, axis=1)
    slot_text = jnp.sum(chosen * pair_text[None, :], axis=1)
    sign = jnp.sum(chosen * (2 * pair_label[None, :] - 1), axis=1)
    return (valid, slot_text, sign)


def pair_terms(score, valid, sign, tokens):
    margin = -sign * (TEMP * score + BIAS)
    loss_part = valid * jax.nn.softplus(margin)
    grad_cos = -LOSS_SCALE * TEMP * valid * sign * jax.nn.sigmoid(margin) / tokens
    return (loss_part, grad_cos)


def general_body(frames, texts, pair_rec, pair_text, pair_label):
    here = lax.axis_index("rec")
    part = lax.axis_index("frame")
    owned, width_rows, width = texts.shape
    tokens = width_rows * lax.axis_size("frame")
    n_text = owned * lax.axis_size("rec")
    valid, slot_text, sign = slot_tables(pair_rec, pair_text, pair_label, here, MOST)
    valid_f = valid.astype(jnp.float32)
    sign_f = sign.astype(jnp.float32)
    picks = (
        (slot_text[:, None] == jnp.arange(n_text, dtype=jnp.int32)[None, :]) & (valid[:, None] > 0)
    ).astype(jnp.bfloat16)
    local = jnp.einsum(
        "jc,cgx->jgx",
        picks,
        lax.all_gather(texts, "rec", axis=0, tiled=True),
        preferred_element_type=jnp.float32,
    ).astype(jnp.bfloat16)
    query_vectors = lax.all_gather(local, "frame", axis=1, tiled=True)
    upstream_signal = frames[0]
    logit_scale = width ** (-0.5)
    pair_scores = (
        jnp.einsum(
            "ype,je->ypj", query_vectors, upstream_signal, preferred_element_type=jnp.float32
        )
        * logit_scale
    )
    local_max = jnp.max(pair_scores, axis=2)
    row_max = lax.pmax(local_max, "frame")
    expo = jnp.exp(pair_scores - row_max[..., None])
    batch_weights = expo.astype(jnp.bfloat16)
    value_partial = jnp.einsum(
        "pqx,xh->pqh", batch_weights, upstream_signal, preferred_element_type=jnp.float32
    )
    query_f = query_vectors.astype(jnp.float32)
    q_norm = lax.rsqrt(jnp.sum(query_f * query_f, axis=2) + EPS)
    q_unit = query_f * q_norm[..., None]
    context = lax.psum(value_partial, "frame")
    c_norm = lax.rsqrt(jnp.sum(context * context, axis=2) + EPS)
    c_unit = context * c_norm[..., None]
    cos = jnp.sum(q_unit * c_unit, axis=2)
    score = jnp.mean(cos, axis=1)
    loss_part, grad_cos = pair_terms(score, valid_f, sign_f, tokens)
    weight = grad_cos[:, None, None]
    d_context = weight * (q_unit - cos[..., None] * c_unit) * c_norm[..., None]
    direct = weight * (c_unit - cos[..., None] * q_unit) * q_norm[..., None]
    direct_own = lax.dynamic_slice_in_dim(direct, part * width_rows, width_rows, 1)
    context_batch_gradient = d_context.astype(jnp.bfloat16)
    weight_gradient = jnp.einsum(
        "ype,je->ypj", context_batch_gradient, upstream_signal, preferred_element_type=jnp.float32
    )
    score_gradient = (expo * weight_gradient * logit_scale).astype(jnp.bfloat16)
    d_query = lax.psum_scatter(
        jnp.einsum(
            "slf,fd->lsd", score_gradient, upstream_signal, preferred_element_type=jnp.float32
        ),
        "frame",
        scatter_dimension=0,
        tiled=True,
    )
    d_query = d_query + jnp.transpose(direct_own, (1, 0, 2))
    text_term = jnp.einsum(
        "st,lsd->tld", picks.astype(jnp.float32), d_query, precision=lax.Precision.HIGHEST
    )
    grad_texts = lax.psum_scatter(text_term, "rec", scatter_dimension=0, tiled=True).astype(
        jnp.bfloat16
    )
    frame_loss_piece = jnp.einsum(
        "cvm,cvz->mz", score_gradient, query_vectors, preferred_element_type=jnp.float32
    )
    frame_loss_piece = frame_loss_piece + jnp.einsum(
        "cvm,cvz->mz", batch_weights, context_batch_gradient, preferred_element_type=jnp.float32
    )
    grad_frames = frame_loss_piece.astype(jnp.bfloat16)[None]
    loss = lax.psum(jnp.sum(loss_part), "rec")
    return (loss, grad_frames, grad_texts)


def split(line):
    pieces = []
    for _ in range(3):
        piece = line.astype(BF16)
        pieces.append(piece)
        line = line - piece.astype(F32)
    return pieces


def stack(lines, count, width):
    n = lines[0].shape[1]
    place = lax.broadcasted_iota(jnp.int32, (count, n), 0)
    out = jnp.zeros((count, n), F32)
    for at, line in enumerate(lines):
        out = jnp.where(place == at, line, out)
    if n < width:
        out = jnp.concatenate([out, jnp.zeros((count, width - n), F32)], axis=1)
    return out


def unpack(extra, i, n):
    got = [extra[3 * i + j : 3 * i + j + 1, :n] for j in range(3)]
    return (got[0] + got[1]) + got[2]


def diagonal(n):
    r = lax.broadcasted_iota(jnp.int32, (n, n), 0)
    c = lax.broadcasted_iota(jnp.int32, (n, n), 1)
    return r == c


def eye(n):
    return jnp.where(diagonal(n), 1.0, 0.0).astype(BF16)


def to_column(line, one, lanes):
    n = line.shape[1]
    out = None
    for piece in split(line):
        term = nt(one, jnp.broadcast_to(piece, (lanes, n)))
        out = term if out is None else out + term
    return out


def turned(x, one):
    high = x.astype(BF16)
    low = (x - high.astype(F32)).astype(BF16)
    return nt(one, high) + nt(one, low)


def table_kernel(rec_ref, text_ref, label_ref, out_ref, seen_ref, count_ref, *, recs, owned):
    here = lax.axis_index("rec")
    odd = lax.rem(here, 2)
    far, cross = lax.rem(here + 2 * odd + recs - 1, recs), lax.rem(here + recs // 2, recs)
    n_cand = 3 * owned
    for i in range(2 * n_cand):
        out_ref[i] = 0
    for r in range(recs):
        seen_ref[r] = 0
        count_ref[r] = 0

    def pair(p, most):
        rec, text, label = rec_ref[p], text_ref[p], label_ref[p]
        seen, bit = seen_ref[rec], lax.shift_left(jnp.int32(1), text)
        n = count_ref[rec] + jnp.where((seen & bit) == 0, 1, 0)
        seen_ref[rec] = seen | bit
        count_ref[rec] = n
        owner = lax.div(text, owned)
        which = jnp.where(owner == far, 1, jnp.where(owner == cross, 2, 0))
        at = which * owned + text - owner * owned + (1 - label) * n_cand
        at = jnp.where(rec == here, at, 4 * n_cand + 1)
        out_ref[at] = out_ref[at] + 1
        return jnp.maximum(most, n)

    out_ref[4 * n_cand + 1] = 0
    out_ref[4 * n_cand] = lax.fori_loop(0, text_ref.shape[0], pair, jnp.int32(0))
    for s in range(n_cand):
        out_ref[3 * n_cand + s] = -1
    at = jnp.int32(0)
    for c in range(n_cand):
        used = (out_ref[c] + out_ref[n_cand + c]) > 0
        out_ref[2 * n_cand + c] = jnp.where(used, at, -1)

        @pl.when(used)
        def _(at=at, c=c):
            out_ref[3 * n_cand + at] = c

        at = at + jnp.where(used, 1, 0)


def select_kernel(table_ref, a_ref, b_ref, c_ref, *out_refs, n_cand, order):
    owned = a_ref.shape[0]
    me = lax.axis_index("frame")
    half = out_refs[0].shape[0]
    for at, out_ref in enumerate(out_refs):
        for i in range(half):
            s = i if len(out_refs) == 1 else me ^ (at // 2) ^ order[at % 2 * half + i]
            c = table_ref[3 * n_cand + s]
            out_ref[i] = jnp.zeros(out_ref.shape[1:], out_ref.dtype)
            for k, ref in enumerate((a_ref, b_ref, c_ref)):

                @pl.when((c >= k * owned) & (c < (k + 1) * owned))
                def _(ref=ref, k=k, i=i, c=c, out_ref=out_ref):
                    out_ref[i] = ref[c - k * owned]


def prepare_kernel(f_ref, out_ref):
    out_ref[...] = nt(eye(f_ref.shape[1]), f_ref[...]).astype(BF16)


def forward_kernel(f_ref, ft_ref, *refs, unit, first, group, scale, place):
    q_refs, (out_ref, weights_ref, top_ref, q_out_ref, q_ref) = refs[:group], refs[group:]
    me = lax.axis_index("frame")
    held, w, width = q_refs[0].shape
    slot = first + (me ^ unit)
    rows = group * w
    for j in range(group):
        if place is None:
            block = q_refs[j][jnp.minimum(slot, held - 1)].astype(F32)
            q_ref[me ^ j] = jnp.where(slot < held, block, 0.0)
        else:
            q_ref[me ^ j] = q_refs[j][place].astype(F32)
    q = q_ref[...].reshape(rows, width).astype(BF16)
    q_out_ref[...] = q
    s = nt(f_ref[...], q) * scale
    top = jnp.max(s, axis=0, keepdims=True)
    weights = jnp.exp(s - top)
    weights_ref[...] = weights
    top_ref[...] = top
    out_ref[:rows] = turned(nn(ft_ref[...], weights.astype(BF16)), eye(rows))
    out_ref[rows:] = stack([top], LINES, width)


def token_kernel(table_ref, q_ref, *refs, first, group, tokens, n_cand):
    in_refs, (out_ref, direct_ref) = refs[:group], refs[group:]
    rows, width = q_ref.shape
    one = eye(rows)
    tops = [ref[rows : rows + 1, :rows] for ref in in_refs]
    m = functools.reduce(jnp.maximum, tops)
    context = jnp.zeros((rows, width), F32)
    for top, ref in zip(tops, in_refs):
        share = to_column(jnp.exp(top - m), one, 128)
        context = context + jnp.concatenate([share] * (width // 128), axis=1) * ref[:rows]
    q = q_ref[...].astype(F32)
    q_norm = lax.rsqrt(jnp.sum(q * q, axis=1, keepdims=True) + EPS)
    c_norm = lax.rsqrt(jnp.sum(context * context, axis=1, keepdims=True) + EPS)
    q_unit, c_unit = q * q_norm, context * c_norm
    cos = jnp.sum(q_unit * c_unit, axis=1, keepdims=True)
    score = jnp.sum(cos, axis=0, keepdims=True) / tokens
    logit = TEMP * score + BIAS
    slot = first + lax.axis_index("frame")
    c = jnp.where(slot < n_cand, table_ref[3 * n_cand + jnp.minimum(slot, n_cand - 1)], -1)
    used = jnp.where(c >= 0, 1, 0)
    pos = (used * table_ref[jnp.maximum(c, 0)]).astype(F32)
    neg = (used * table_ref[n_cand + jnp.maximum(c, 0)]).astype(F32)
    tail = jnp.log1p(jnp.exp(-jnp.abs(logit)))
    loss = pos * (jnp.maximum(-logit, 0.0) + tail) + neg * (jnp.maximum(logit, 0.0) + tail)
    grad_pos = (-LOSS_SCALE * TEMP / tokens) * jax.nn.sigmoid(-logit)
    grad_neg = (LOSS_SCALE * TEMP / tokens) * jax.nn.sigmoid(logit)
    side = q_unit - cos * c_unit
    d_pos = (grad_pos * side * c_norm).astype(BF16).astype(F32)
    d_neg = (grad_neg * side * c_norm).astype(BF16).astype(F32)
    out_ref[:rows] = (pos * d_pos + neg * d_neg).astype(BF16)
    extra = split(m) + split(jnp.broadcast_to(loss, (1, rows)))
    out_ref[rows:] = stack([x.astype(F32) for x in extra], EXTRA, width).astype(BF16)
    direct_ref[...] = (pos * grad_pos + neg * grad_neg) * (c_unit - cos * q_unit) * q_norm


def backward_kernel(f_ref, ft_ref, weights_ref, top_ref, d_ref, *refs, unit, group, scale):
    if unit == 0:
        direct_ref, refs = refs[0], refs[1:]
    dq_ref, ds_ref, w_ref = refs
    width = f_ref.shape[1]
    rows = top_ref.shape[1]
    m = unpack(d_ref[rows:].astype(F32), 0, rows)
    weights = weights_ref[...] * jnp.exp(top_ref[...] - m)
    w_ref[...] = weights.astype(BF16)
    ds = (weights * nt(f_ref[...], d_ref[:rows]) * scale).astype(BF16)
    ds_ref[...] = ds
    dqt = nn(ft_ref[...], ds)
    dq = turned(dqt, eye(rows)) + direct_ref[...] if unit == 0 else nt(eye(rows), dqt.astype(BF16))
    dq_ref[...] = dq.reshape(group, rows // group, width)


def spread_kernel(*refs, units, group):
    in_refs, out_refs = refs[:units], refs[units:]
    me = lax.axis_index("frame")
    for i in range(units):
        slot = (i // group) * group + (me ^ (i % group))
        for j, ref in enumerate(out_refs):
            if units == group:
                ref[slot] = in_refs[i][me ^ j].astype(ref.dtype)
            else:

                @pl.when(slot < ref.shape[0])
                def _(ref=ref, i=i, j=j, slot=slot):
                    ref[slot] = in_refs[i][me ^ j].astype(ref.dtype)


def frames_kernel(*refs, units):
    ds_refs, q_refs, w_refs, d_refs = [refs[k * units : (k + 1) * units] for k in range(4)]
    rows = q_refs[0].shape[0]
    total = None
    for i in range(units):
        term = nn(ds_refs[i][...], q_refs[i][...]) + nn(w_refs[i][...], d_refs[i][:rows])
        total = term if total is None else total + term
    refs[-1][...] = total


def last_frames_kernel(*refs, units):
    ds_refs, q_refs, w_refs, d_refs = [refs[k * units : (k + 1) * units] for k in range(4)]
    before_ref, out_ref, held_ref, sems = refs[4 * units :]
    rows, depth = q_refs[0].shape[0], before_ref.shape[0]
    blocks = sems.shape[0]
    size = depth // blocks
    copies = []
    for b in range(blocks):
        at = pl.ds(b * size, size)
        total = before_ref[at]
        for i in range(units):
            total = total + nn(ds_refs[i][at], q_refs[i][...]) + nn(w_refs[i][at], d_refs[i][:rows])
        held_ref[at] = total.astype(BF16)
        copies.append(pltpu.make_async_copy(held_ref.at[at], out_ref.at[0, at], sems.at[b]))
        copies[-1].start()
    for copy in copies:
        copy.wait()


def finish_kernel(table_ref, loss_ref, *refs, n_cand):
    in_refs, outs = refs[:-3], refs[-3:]
    owned = n_cand // 3
    w, width = in_refs[0].shape[1:]
    for c in range(n_cand):
        s = table_ref[2 * n_cand + c]
        k, j = c // owned, c % owned
        at = jnp.maximum(s, 0)
        total = functools.reduce(jnp.add, [x[at].astype(F32) for x in in_refs])
        total = jnp.where(s >= 0, total, 0.0).astype(BF16)
        if k < 2:
            outs[k][j] = total
        else:
            outs[k][j * w : (j + 1) * w] = total
    pieces = [x.astype(F32) for x in split(loss_ref[...])]
    outs[2][owned * w :] = stack(pieces, EXTRA, width).astype(BF16)


def close_kernel(loss_ref, near_ref, far_ref, cross_ref, out_ref, total_ref):
    owned, w, _ = near_ref.shape
    for j in range(owned):
        total = near_ref[j].astype(F32) + far_ref[j].astype(F32)
        out_ref[j] = (total + cross_ref[j * w : (j + 1) * w].astype(F32)).astype(BF16)
    total_ref[...] = loss_ref[...] + unpack(cross_ref[owned * w :].astype(F32), 0, total_ref.shape[1])


def call(kernel, out_shape, in_specs, *args, scratch=(), flops=0, nbytes=1 << 20, vmem=16, out_specs=None):
    many = isinstance(out_shape, (list, tuple))
    return pl.pallas_call(
        kernel,
        out_shape=out_shape,
        in_specs=in_specs,
        out_specs=out_specs or ([VMEM] * len(out_shape) if many else VMEM),
        scratch_shapes=list(scratch),
        compiler_params=pltpu.CompilerParams(vmem_limit_bytes=vmem << 20),
        cost_estimate=pl.CostEstimate(flops=flops, bytes_accessed=nbytes, transcendentals=0),
    )(*args)


def permute(x, recs, group, move, sends=None):
    pairs = []
    for r in range(recs):
        for f in range(group):
            to_r, to_f = move(r, f)
            if sends is None or sends(f, to_f):
                pairs.append((r * group + f, to_r * group + to_f))
    return lax.ppermute(x, AXES, pairs)


def near_of(r, recs):
    return r ^ 1


def far_of(r, recs):
    return (r - 1) % recs if r % 2 == 0 else (r + 1) % recs


def cross_of(r, recs):
    return (r + recs // 2) % recs


def slot_body(slots, frames, near, far, cross, table, *, tokens, recs, group):
    owned, w, width = near.shape
    n_cand = 3 * owned
    rows = group * w
    depth = frames.shape[1]
    f = frames[0]
    scale = width ** (-0.5)
    rounds = -(-slots // group)
    units = rounds * group
    cost = 2 * rows * depth * width
    shape = jax.ShapeDtypeStruct
    xor = [lambda r, g, j=j: (r, g ^ j) for j in range(group)]
    order = [3, 1, 2, 0]

    halves = 2 if slots == group else 1
    q = call(
        functools.partial(select_kernel, n_cand=n_cand, order=order),
        [shape((slots // halves, w, width), BF16)] * (2 * group if halves == 2 else 1),
        [SMEM, VMEM, VMEM, VMEM],
        table, near, far, cross,
    )
    qs = []
    for h in range(halves):
        part = [q[2 * j + h] if halves == 2 else q[0] for j in range(group)]
        qs.append(part[:1] + [permute(part[j], recs, group, xor[j]) for j in range(1, group)])
    ft = call(prepare_kernel, shape((width, depth), BF16), [VMEM], f, flops=cost)
    made, sent = {}, {}
    for r in range(rounds):
        for i in order:
            made[r, i] = call(
                functools.partial(
                    forward_kernel,
                    unit=i,
                    first=r * group,
                    group=group,
                    scale=scale,
                    place=order.index(i) % 2 if halves == 2 else None,
                ),
                [
                    shape((rows + LINES, width), F32),
                    shape((depth, rows), F32),
                    shape((1, rows), F32),
                    shape((rows, width), BF16),
                ],
                [VMEM] * (2 + group),
                f, ft, *qs[order.index(i) // 2 if halves == 2 else 0],
                scratch=[pltpu.VMEM((group, w, width), F32)],
                flops=2 * cost,
            )
            sent[r, i] = made[r, i][0]
            if i:
                sent[r, i] = permute(
                    sent[r, i], recs, group, xor[i], lambda a, b, r=r: r * group + b < slots
                )
    ds, directs = {}, {}
    for r in range(rounds):
        d, directs[r] = call(
            functools.partial(token_kernel, first=r * group, group=group, tokens=tokens, n_cand=n_cand),
            [shape((rows + EXTRA, width), BF16), shape((rows, width), F32)],
            [SMEM] + [VMEM] * (1 + group),
            table, made[r, 0][3], *[sent[r, i] for i in range(group)],
        )
        for i in order:
            ds[r, i] = d
            if i:
                ds[r, i] = permute(d, recs, group, xor[i], lambda a, b, r=r: r * group + a < slots)
    back = {}
    for r in range(rounds):
        for i in order:
            back[r, i] = call(
                functools.partial(backward_kernel, unit=i, group=group, scale=scale),
                [shape((group, w, width), F32), shape((depth, rows), BF16), shape((depth, rows), BF16)],
                [VMEM] * (6 if i == 0 else 5),
                f, ft, made[r, i][1], made[r, i][2], ds[r, i], *([directs[r]] if i == 0 else []),
                flops=2 * cost,
            )
    keys = [(r, i) for r in range(rounds) for i in range(group)]
    dqs = call(
        functools.partial(spread_kernel, units=units, group=group),
        [shape((slots, w, width), BF16)] * group,
        [VMEM] * units,
        *[back[k][0] for k in keys],
    )

    loss = 0
    for k in keys:
        loss = loss + jnp.sum(ds[k][rows + 3 : rows + 6, :128].astype(F32), axis=0, keepdims=True)
    *dqs, loss = lax.optimization_barrier((*dqs, loss))
    dqs = [dqs[0]] + [permute(dqs[j], recs, group, xor[j]) for j in range(1, group)]
    step, total, half = 1, None, units // 2
    for n, some in enumerate((keys[:half], keys[half:])):
        if step < recs // 2:
            other = permute(loss, recs, group, lambda r, g, k=step: (r ^ k, g))
        args = [back[k][1] for k in some] + [made[k][3] for k in some]
        args += [back[k][2] for k in some] + [ds[k] for k in some]
        if n == 0:
            total = call(
                functools.partial(frames_kernel, units=half),
                shape(frames.shape[1:], F32),
                [VMEM] * len(args),
                *args,
                flops=2 * half * cost,
            )
        else:
            blocks = 3 if depth % 384 == 0 else 1
            total = call(
                functools.partial(last_frames_kernel, units=half),
                shape(frames.shape, BF16),
                [VMEM] * (len(args) + 1),
                *args, total,
                out_specs=pl.BlockSpec(memory_space=pltpu.HBM),
                scratch=[pltpu.VMEM((depth, width), BF16), pltpu.SemaphoreType.DMA((blocks,))],
                flops=2 * half * cost,
            )
        if step < recs // 2:
            if n == 0:
                total, other = lax.optimization_barrier((total, other))
            loss = loss + other
            step *= 2
    while step < recs // 2:
        loss = loss + permute(loss, recs, group, lambda r, g, k=step: (r ^ k, g))
        step *= 2
    home = call(
        functools.partial(finish_kernel, n_cand=n_cand),
        [shape((owned, w, width), BF16)] * 2 + [shape((owned * w + EXTRA, width), BF16)],
        [SMEM] + [VMEM] * (1 + group),
        table, loss, *dqs,
    )
    got = []
    for x, where in zip(home, (near_of, far_of, cross_of)):
        got.append(permute(x, recs, group, lambda r, g: (where(r, recs), g)))
    texts, loss = call(
        close_kernel,
        [shape((owned, w, width), BF16), shape((1, 128), F32)],
        [VMEM] * 4,
        loss, *got,
    )
    return loss[0, 0], total, texts


def body(frames, texts, pair_rec, pair_text, pair_label):
    recs, group = lax.axis_size("rec"), lax.axis_size("frame")
    owned, w, _ = texts.shape
    if group != 4 or w % 8 or recs < 4 or recs & (recs - 1) or 3 * owned > 2 * group or owned * recs > 32:
        return general_body(frames, texts, pair_rec, pair_text, pair_label)
    near, far, cross = [
        permute(texts, recs, group, lambda r, g, to=to: (to(r, recs), g)) for to in (near_of, far_of, cross_of)
    ]
    n_cand = 3 * owned
    table = pl.pallas_call(
        functools.partial(table_kernel, recs=recs, owned=owned),
        name="table",
        out_shape=jax.ShapeDtypeStruct((4 * n_cand + 2,), jnp.int32),
        in_specs=[SMEM] * 3,
        out_specs=SMEM,
        scratch_shapes=[pltpu.SMEM((recs,), jnp.int32)] * 2,
    )(pair_rec[:, 0], pair_text, pair_label)

    def run(slots, *args):
        return slot_body(slots, *args, tokens=w * group, recs=recs, group=group)

    args = (frames, near, far, cross, table)
    return lax.cond(
        table[4 * n_cand] <= group, functools.partial(run, group), functools.partial(run, n_cand), *args
    )


def solution(mesh):
    return jax.shard_map(
        body,
        mesh=mesh,
        in_specs=(P("rec", "frame", None), P("rec", "frame", None), P(), P(), P()),
        out_specs=(P(), P("rec", "frame", None), P("rec", "frame", None)),
        check_vma=False,
    )
```

profile of v0, /device:TPU:0, one launch (start us, length us, event | category | flops | bytes accessed | tf_op | source)
XLA Modules:
  0.0 66.5 jit_solution(10815227323538185637)
XLA Ops:
  0.6 0.6 collective-permute-start.43
  1.2 4.7 %collective-permute-start.44 = (bf16[2,56,256]{2,1,0:T(8,128)(2,1)}, bf16[2,56,256]{2,1,0:T(8,128)(2,1)S(1)}, u32[]{:S(2)}, u32[]{:S(2)}) collective-permute-start(bf16[2,56,256]{2,1,0:T(8,128)(2,1)} %param.8), channel_id=1, source_target_pairs={{0,28},{1,29},{2,30},{3,31},{4,8},{5,9},{6,10},{7,11},{8,4},{9,5},... | collective-permute-start | bytes 172040 | tf_op jit(solution)/shard_map/ppermute | solution.py:407
  5.9 0.0 collective-permute-start.45
  5.9 1.6 %table.1 = s32[26]{0:T(128)S(1)} custom-call(s32[16]{0:T(128)} %bitcast.38, s32[16]{0:T(128)} %text_ref.1, s32[16]{0:T(128)} %label_ref.1), custom_call_target="tpu_custom_call" | custom-call | tf_op jit(solution)/shard_map/table/pallas_call | solution.py:571
  7.5 0.6 slice.45
  8.7 0.0 collective-permute-done.43
  8.8 0.0 collective-permute-done.44
  8.8 2.4 %collective-permute-done.45 = bf16[2,56,256]{2,1,0:T(8,128)(2,1)S(1)} collective-permute-done((bf16[2,56,256]{2,1,0:T(8,128)(2,1)}, bf16[2,56,256]{2,1,0:T(8,128)(2,1)S(1)}, u32[]{:S(2)}, u32[]{:S(2)}) %collective-permute-start.45) | collective-permute-done | bytes 57376 | tf_op jit(solution)/shard_map/ppermute | solution.py:407
  11.2 54.5 %conditional.1 = (bf16[2,56,256]{2,1,0:T(8,128)(2,1)}, f32[]{:T(128)}, bf16[1,1536,256]{2,1,0:T(8,128)(2,1)S(1)}) conditional(s32[]{:T(128)} %bitcast.7, (bf16[1,1536,256]{2,1,0:T(8,128)(2,1)}, s32[26]{0:T(128)S(1)}, bf16[2,56,256]{2,1,0:T(8,128)(2,1)S(1)}, bf16[2,56,256]{2,1,0:T(8,128)(2,1)S(1)}, bf16[2,56,256]{2,1,0:T(8,128)(2,1)S(1)}) %tuple.19, ...), branch_computations={%region_0.0_spmd, %region_9.0_spmd} | conditional | flops 8631883776 | bytes 42883532 | solution.py:584
  11.2 0.9 %branch_1_fun.17 = (bf16[2,56,256]{2,1,0:T(8,128)(2,1)S(1)}, bf16[2,56,256]{2,1,0:T(8,128)(2,1)S(1)}, bf16[2,56,256]{2,1,0:T(8,128)(2,1)S(1)}, bf16[2,56,256]{2,...) custom-call(s32[26]{0:T(128)S(1)} %get-tuple-element.102.table_ref, ...), custom_call_target="tpu_custom_call" | custom-call | bytes 1048576 | tf_op jit(solution)/shard_map/cond/branch_1_fun/pallas_call | solution.py:389
  12.1 1.6 %collective-permute-start.26 = (bf16[2,56,256]{2,1,0:T(8,128)(2,1)S(1)}, bf16[2,56,256]{2,1,0:T(8,128)(2,1)S(1)}, u32[]{:S(2)}, u32[]{:S(2)}) collective-permute-start(bf16[2,56,256]{2,1,0:T(8,128)(2,1)S(1)} %get-tuple-element.115), channel_id=1, source_target_pairs={{0,1},{1,0},{2,3},{3,2},{4,5},{5,4},{6,7},{7,6},{8,9},{9,8},{10,11... | collective-permute-start | bytes 172040 | tf_op jit(solution)/shard_map/cond/branch_1_fun/ppermute | solution.py:407
  13.6 1.5 %collective-permute-start.27 = (bf16[2,56,256]{2,1,0:T(8,128)(2,1)S(1)}, bf16[2,56,256]{2,1,0:T(8,128)(2,1)S(1)}, u32[]{:S(2)}, u32[]{:S(2)}) collective-permute-start(bf16[2,56,256]{2,1,0:T(8,128)(2,1)S(1)} %get-tuple-element.116), channel_id=1, source_target_pairs={{0,2},{1,3},{2,0},{3,1},{4,6},{5,7},{6,4},{7,5},{8,10},{9,11},{10,... | collective-permute-start | bytes 172040 | tf_op jit(solution)/shard_map/cond/branch_1_fun/ppermute | solution.py:407
  15.2 0.5 collective-permute-start.28
  15.6 1.5 %collective-permute-start.23 = (bf16[2,56,256]{2,1,0:T(8,128)(2,1)S(1)}, bf16[2,56,256]{2,1,0:T(8,128)(2,1)S(1)}, u32[]{:S(2)}, u32[]{:S(2)}) collective-permute-start(bf16[2,56,256]{2,1,0:T(8,128)(2,1)S(1)} %get-tuple-element.107), channel_id=1, source_target_pairs={{0,1},{1,0},{2,3},{3,2},{4,5},{5,4},{6,7},{7,6},{8,9},{9,8},{10,11... | collective-permute-start | bytes 172040 | tf_op jit(solution)/shard_map/cond/branch_1_fun/ppermute | solution.py:407
  17.1 1.5 %collective-permute-start.24 = (bf16[2,56,256]{2,1,0:T(8,128)(2,1)S(1)}, bf16[2,56,256]{2,1,0:T(8,128)(2,1)S(1)}, u32[]{:S(2)}, u32[]{:S(2)}) collective-permute-start(bf16[2,56,256]{2,1,0:T(8,128)(2,1)S(1)} %get-tuple-element.108), channel_id=1, source_target_pairs={{0,2},{1,3},{2,0},{3,1},{4,6},{5,7},{6,4},{7,5},{8,10},{9,11},{10,... | collective-permute-start | bytes 172040 | tf_op jit(solution)/shard_map/cond/branch_1_fun/ppermute | solution.py:407
  18.6 0.0 collective-permute-done.26.refs_1_
  18.6 0.5 collective-permute-start.25
  19.1 1.5 %branch_1_fun.16.ft_ref = bf16[256,1536]{1,0:T(8,128)(2,1)S(1)} custom-call(bf16[1536,256]{1,0:T(8,128)(2,1)} %bitcast.29), custom_call_target="tpu_custom_call" | custom-call | flops 176160768 | bytes 1048576 | tf_op jit(solution)/shard_map/cond/branch_1_fun/pallas_call | solution.py:389
  20.7 0.0 collective-permute-done.27.refs_2_
  20.7 0.1 collective-permute-done.28.refs_3_
  20.8 1.6 %branch_1_fun.19 = (f32[232,256]{1,0:T(8,128)S(1)}, f32[1536,224]{1,0:T(8,128)S(1)}, f32[1,224]{1,0:T(1,128)S(1)}, bf16[224,256]{1,0:T(8,128)(2,1)S(1)}) custom-call(bf16[1536,256]{1,0:T(8,128)(2,1)S(1)} %bitcast.30, bf16[256,1536]{1,0:T(8,128)(2,1)S(1)} %branch_1_fun.16.ft_ref, bf16[2,56,256]{2,1,0:T(8,128)(2,1)S(1)} %get-tuple-element.114.refs_0_, ...), custom_call_target="tpu_custom_call" | custom-call | flops 352321536 | bytes 1048576 | tf_op jit(solution)/shard_map/cond/branch_1_fun/pallas_call | solution.py:389
  22.3 1.5 %collective-permute-start.29 = (f32[232,256]{1,0:T(8,128)S(1)}, f32[232,256]{1,0:T(8,128)S(1)}, u32[]{:S(2)}, u32[]{:S(2)}) collective-permute-start(f32[232,256]{1,0:T(8,128)S(1)} %get-tuple-element.118), channel_id=1, source_target_pairs={{0,1},{1,0},{2,3},{3,2},{4,5},{5,4},{6,7},{7,6},{8,9},{9,8},{10,11... | collective-permute-start | bytes 712712 | tf_op jit(solution)/shard_map/cond/branch_1_fun/ppermute | solution.py:407
  23.8 0.0 collective-permute-done.23.refs_1_
  23.8 0.0 collective-permute-done.24.refs_2_
  23.8 0.5 collective-permute-done.25.refs_3_
  24.3 1.6 %branch_1_fun.20 = (f32[232,256]{1,0:T(8,128)S(1)}, f32[1536,224]{1,0:T(8,128)S(1)}, f32[1,224]{1,0:T(1,128)S(1)}, bf16[224,256]{1,0:T(8,128)(2,1)S(1)}) custom-call(bf16[1536,256]{1,0:T(8,128)(2,1)S(1)} %bitcast.31, bf16[256,1536]{1,0:T(8,128)(2,1)S(1)} %branch_1_fun.16.ft_ref, bf16[2,56,256]{2,1,0:T(8,128)(2,1)S(1)} %get-tuple-element.106.refs_0_, ...), custom_call_target="tpu_custom_call" | custom-call | flops 352321536 | bytes 1048576 | tf_op jit(solution)/shard_map/cond/branch_1_fun/pallas_call | solution.py:389
  25.9 1.1 %collective-permute-start.30 = (f32[232,256]{1,0:T(8,128)S(1)}, f32[232,256]{1,0:T(8,128)S(1)}, u32[]{:S(2)}, u32[]{:S(2)}) collective-permute-start(f32[232,256]{1,0:T(8,128)S(1)} %get-tuple-element.119), channel_id=1, source_target_pairs={{0,2},{1,3},{2,0},{3,1},{4,6},{5,7},{6,4},{7,5},{8,10},{9,11},{10,... | collective-permute-start | bytes 712712 | tf_op jit(solution)/shard_map/cond/branch_1_fun/ppermute | solution.py:407
  27.0 1.6 %branch_1_fun.21 = (f32[232,256]{1,0:T(8,128)S(1)}, f32[1536,224]{1,0:T(8,128)S(1)}, f32[1,224]{1,0:T(1,128)S(1)}, bf16[224,256]{1,0:T(8,128)(2,1)S(1)}) custom-call(bf16[1536,256]{1,0:T(8,128)(2,1)S(1)} %bitcast.32, bf16[256,1536]{1,0:T(8,128)(2,1)S(1)} %branch_1_fun.16.ft_ref, bf16[2,56,256]{2,1,0:T(8,128)(2,1)S(1)} %get-tuple-element.114.refs_0_, ...), custom_call_target="tpu_custom_call" | custom-call | flops 352321536 | bytes 1048576 | tf_op jit(solution)/shard_map/cond/branch_1_fun/pallas_call | solution.py:389
  28.6 0.6 collective-permute-start.31
  29.1 1.6 %branch_1_fun.18 = (f32[232,256]{1,0:T(8,128)S(1)}, f32[1536,224]{1,0:T(8,128)S(1)}, f32[1,224]{1,0:T(1,128)S(1)}, bf16[224,256]{1,0:T(8,128)(2,1)S(1)}) custom-call(bf16[1536,256]{1,0:T(8,128)(2,1)S(1)} %bitcast.33, bf16[256,1536]{1,0:T(8,128)(2,1)S(1)} %branch_1_fun.16.ft_ref, bf16[2,56,256]{2,1,0:T(8,128)(2,1)S(1)} %get-tuple-element.106.refs_0_, ...), custom_call_target="tpu_custom_call" | custom-call | flops 352321536 | bytes 1048576 | tf_op jit(solution)/shard_map/cond/branch_1_fun/pallas_call | solution.py:389
  30.7 0.0 collective-permute-done.29.refs_1_
  30.7 6.0 %collective-permute-done.30.refs_2_ = f32[232,256]{1,0:T(8,128)S(1)} collective-permute-done((f32[232,256]{1,0:T(8,128)S(1)}, f32[232,256]{1,0:T(8,128)S(1)}, u32[]{:S(2)}, u32[]{:S(2)}) %collective-permute-start.30) | collective-permute-done | bytes 237600 | tf_op jit(solution)/shard_map/cond/branch_1_fun/ppermute | solution.py:407
  36.7 0.0 collective-permute-done.31.refs_3_
  36.7 1.4 %branch_1_fun.22 = (bf16[240,256]{1,0:T(8,128)(2,1)S(1)}, f32[224,256]{1,0:T(8,128)S(1)}) custom-call(s32[26]{0:T(128)S(1)} %get-tuple-element.102.table_ref, bf16[224,256]{1,0:T(8,128)(2,1)S(1)} %get-tuple-element.112.q_ref.refs_2_, f32[232,256]{1,0:T(8,128)S(1)} %get-tuple-element.113.refs_0_, f32[232,256]{1,0:T(8,128)S(1)} %collective-permute-done.29.refs_1_, ...), custom_call_target="tpu_custom_call" | custom-call | bytes 1048576 | tf_op jit(solution)/shard_map/cond/branch_1_fun/pallas_call | solution.py:389
  38.1 0.4 collective-permute-start.32
  38.5 2.0 %collective-permute-start.34 = (bf16[240,256]{1,0:T(8,128)(2,1)S(1)}, bf16[240,256]{1,0:T(8,128)(2,1)S(1)}, u32[]{:S(2)}, u32[]{:S(2)}) collective-permute-start(bf16[240,256]{1,0:T(8,128)(2,1)S(1)} %get-tuple-element.121.d_ref.refs_6_), channel_id=1, source_target_pairs={{0,3},{1,2},{2,1},{3,0},{4,7},{5,6},{6,5},{7,4},{8,11},{9,10},{10,... | collective-permute-start | bytes 368648 | tf_op jit(solution)/shard_map/cond/branch_1_fun/ppermute | solution.py:407
  40.5 1.2 %collective-permute-start.33 = (bf16[240,256]{1,0:T(8,128)(2,1)S(1)}, bf16[240,256]{1,0:T(8,128)(2,1)S(1)}, u32[]{:S(2)}, u32[]{:S(2)}) collective-permute-start(bf16[240,256]{1,0:T(8,128)(2,1)S(1)} %get-tuple-element.121.d_ref.refs_6_), channel_id=1, source_target_pairs={{0,2},{1,3},{2,0},{3,1},{4,6},{5,7},{6,4},{7,5},{8,10},{9,11},{10,... | collective-permute-start | bytes 368648 | tf_op jit(solution)/shard_map/cond/branch_1_fun/ppermute | solution.py:407
  41.7 1.0 %branch_1_fun.23 = (f32[4,56,256]{2,1,0:T(8,128)S(1)}, bf16[1536,224]{1,0:T(8,128)(2,1)S(1)}, bf16[1536,224]{1,0:T(8,128)(2,1)S(1)}) custom-call(bf16[1536,256]{1,0:T(8,128)(2,1)S(1)} %bitcast.34, bf16[256,1536]{1,0:T(8,128)(2,1)S(1)} %branch_1_fun.16.ft_ref, f32[1536,224]{1,0:T(8,128)S(1)} %get-tuple-element.110.weights_ref, ...), custom_call_target="tpu_custom_call" | custom-call | flops 352321536 | bytes 1048576 | tf_op jit(solution)/shard_map/cond/branch_1_fun/pallas_call | solution.py:389
  42.7 0.4 collective-permute-done.32.d_ref.refs_7_
  43.1 1.6 %collective-permute-done.34.d_ref.refs_7_ = bf16[240,256]{1,0:T(8,128)(2,1)S(1)} collective-permute-done((bf16[240,256]{1,0:T(8,128)(2,1)S(1)}, bf16[240,256]{1,0:T(8,128)(2,1)S(1)}, u32[]{:S(2)}, u32[]{:S(2)}) %collective-permute-start.34) | collective-permute-done | bytes 122912 | tf_op jit(solution)/shard_map/cond/branch_1_fun/ppermute | solution.py:407
  44.8 1.2 %collective-permute-done.33.d_ref.refs_6_ = bf16[240,256]{1,0:T(8,128)(2,1)S(1)} collective-permute-done((bf16[240,256]{1,0:T(8,128)(2,1)S(1)}, bf16[240,256]{1,0:T(8,128)(2,1)S(1)}, u32[]{:S(2)}, u32[]{:S(2)}) %collective-permute-start.33) | collective-permute-done | bytes 122912 | tf_op jit(solution)/shard_map/cond/branch_1_fun/ppermute | solution.py:407
  46.0 1.0 %branch_1_fun.24 = (f32[4,56,256]{2,1,0:T(8,128)S(1)}, bf16[1536,224]{1,0:T(8,128)(2,1)S(1)}, bf16[1536,224]{1,0:T(8,128)(2,1)S(1)}) custom-call(bf16[1536,256]{1,0:T(8,128)(2,1)S(1)} %bitcast.35, bf16[256,1536]{1,0:T(8,128)(2,1)S(1)} %branch_1_fun.16.ft_ref, f32[1536,224]{1,0:T(8,128)S(1)} %get-tuple-element.124.weights_ref, ...), custom_call_target="tpu_custom_call" | custom-call | flops 352321536 | bytes 1048576 | tf_op jit(solution)/shard_map/cond/branch_1_fun/pallas_call | solution.py:389
  47.0 1.0 %branch_1_fun.26 = (f32[4,56,256]{2,1,0:T(8,128)S(1)}, bf16[1536,224]{1,0:T(8,128)(2,1)S(1)}, bf16[1536,224]{1,0:T(8,128)(2,1)S(1)}) custom-call(bf16[1536,256]{1,0:T(8,128)(2,1)S(1)} %bitcast.36, bf16[256,1536]{1,0:T(8,128)(2,1)S(1)} %branch_1_fun.16.ft_ref, f32[1536,224]{1,0:T(8,128)S(1)} %get-tuple-element.130.weights_ref, ...), custom_call_target="tpu_custom_call" | custom-call | flops 352321536 | bytes 1048576 | tf_op jit(solution)/shard_map/cond/branch_1_fun/pallas_call | solution.py:389
  48.0 1.0 %branch_1_fun.25 = (f32[4,56,256]{2,1,0:T(8,128)S(1)}, bf16[1536,224]{1,0:T(8,128)(2,1)S(1)}, bf16[1536,224]{1,0:T(8,128)(2,1)S(1)}) custom-call(bf16[1536,256]{1,0:T(8,128)(2,1)S(1)} %bitcast.37, bf16[256,1536]{1,0:T(8,128)(2,1)S(1)} %branch_1_fun.16.ft_ref, f32[1536,224]{1,0:T(8,128)S(1)} %get-tuple-element.127.weights_ref, ...), custom_call_target="tpu_custom_call" | custom-call | flops 352321536 | bytes 1048576 | tf_op jit(solution)/shard_map/cond/branch_1_fun/pallas_call | solution.py:389
  48.9 0.1 branch_1_fun.27
  49.0 1.3 %collective-permute-start.37 = (bf16[4,56,256]{2,1,0:T(8,128)(2,1)S(1)}, bf16[4,56,256]{2,1,0:T(8,128)(2,1)S(1)}, u32[]{:S(2)}, u32[]{:S(2)}) collective-permute-start(bf16[4,56,256]{2,1,0:T(8,128)(2,1)S(1)} %get-tuple-element.145), channel_id=1, source_target_pairs={{0,1},{1,0},{2,3},{3,2},{4,5},{5,4},{6,7},{7,6},{8,9},{9,8},{10,11... | collective-permute-start | bytes 344072 | tf_op jit(solution)/shard_map/cond/branch_1_fun/ppermute | solution.py:407
  50.3 0.9 %collective-permute-start.38 = (bf16[4,56,256]{2,1,0:T(8,128)(2,1)S(1)}, bf16[4,56,256]{2,1,0:T(8,128)(2,1)S(1)}, u32[]{:S(2)}, u32[]{:S(2)}) collective-permute-start(bf16[4,56,256]{2,1,0:T(8,128)(2,1)S(1)} %get-tuple-element.146), channel_id=1, source_target_pairs={{0,2},{1,3},{2,0},{3,1},{4,6},{5,7},{6,4},{7,5},{8,10},{9,11},{10,... | collective-permute-start | bytes 344072 | tf_op jit(solution)/shard_map/cond/branch_1_fun/ppermute | solution.py:407
  51.3 1.3 %collective-permute-start.39 = (bf16[4,56,256]{2,1,0:T(8,128)(2,1)S(1)}, bf16[4,56,256]{2,1,0:T(8,128)(2,1)S(1)}, u32[]{:S(2)}, u32[]{:S(2)}) collective-permute-start(bf16[4,56,256]{2,1,0:T(8,128)(2,1)S(1)} %get-tuple-element.147), channel_id=1, source_target_pairs={{0,3},{1,2},{2,1},{3,0},{4,7},{5,6},{6,5},{7,4},{8,11},{9,10},{10,... | collective-permute-start | bytes 344072 | tf_op jit(solution)/shard_map/cond/branch_1_fun/ppermute | solution.py:407
  52.6 0.0 collective-permute-start.35
  52.6 1.0 %branch_1_fun.28.refs_8_ = f32[1536,256]{1,0:T(8,128)S(1)} custom-call(bf16[1536,224]{1,0:T(8,128)(2,1)S(1)} %get-tuple-element.138.refs_0_, bf16[1536,224]{1,0:T(8,128)(2,1)S(1)} %get-tuple-element.139.refs_1_, bf16[224,256]{1,0:T(8,128)(2,1)S(1)} %get-tuple-element.112.q_ref.refs_2_, bf16[224,256]{1,0:T(8,128)(2,1)S(1)} %get-tuple-element.140.refs_3_, ...), custom_call_target="tpu_custom_call" | custom-call | flops 704643072 | bytes 1048576 | tf_op jit(solution)/shard_map/cond/branch_1_fun/pallas_call | solution.py:389
  53.6 0.2 collective-permute-done.35
  53.7 0.0 collective-permute-start.36
  53.7 3.6 %collective-permute-done.36 = f32[1,128]{1,0:T(1,128)S(1)} collective-permute-done((f32[1,128]{1,0:T(1,128)S(1)}, f32[1,128]{1,0:T(1,128)S(1)}, u32[]{:S(2)}, u32[]{:S(2)}) %collective-permute-start.36) | collective-permute-done | bytes 544 | tf_op jit(solution)/shard_map/cond/branch_1_fun/ppermute | solution.py:407
  57.3 0.0 collective-permute-done.37.refs_1_
  57.3 0.0 collective-permute-done.38.refs_2_
  57.3 0.0 collective-permute-done.39.refs_3_
  57.3 0.7 branch_1_fun.29
  58.0 1.2 %collective-permute-start.42 = (bf16[128,256]{1,0:T(8,128)(2,1)S(1)}, bf16[128,256]{1,0:T(8,128)(2,1)S(1)}, u32[]{:S(2)}, u32[]{:S(2)}) collective-permute-start(bf16[128,256]{1,0:T(8,128)(2,1)S(1)} %get-tuple-element.150), channel_id=1, source_target_pairs={{0,16},{1,17},{2,18},{3,19},{4,20},{5,21},{6,22},{7,23},{8,24},{9,... | collective-permute-start | bytes 196616 | tf_op jit(solution)/shard_map/cond/branch_1_fun/ppermute | solution.py:407
  59.2 1.4 %collective-permute-start.41 = (bf16[2,56,256]{2,1,0:T(8,128)(2,1)S(1)}, bf16[2,56,256]{2,1,0:T(8,128)(2,1)S(1)}, u32[]{:S(2)}, u32[]{:S(2)}) collective-permute-start(bf16[2,56,256]{2,1,0:T(8,128)(2,1)S(1)} %get-tuple-element.149), channel_id=1, source_target_pairs={{0,28},{1,29},{2,30},{3,31},{4,8},{5,9},{6,10},{7,11},{8,4},{9,5},... | collective-permute-start | bytes 172040 | tf_op jit(solution)/shard_map/cond/branch_1_fun/ppermute | solution.py:407
  60.6 1.9 %branch_1_fun.31 = bf16[1,1536,256]{2,1,0:T(8,128)(2,1)S(1)} custom-call(bf16[1536,224]{1,0:T(8,128)(2,1)S(1)} %get-tuple-element.152.refs_0_, bf16[1536,224]{1,0:T(8,128)(2,1)S(1)} %get-tuple-element.153.refs_1_, bf16[224,256]{1,0:T(8,128)(2,1)S(1)} %get-tuple-element.154.refs_2_, bf16[224,256]{1,0:T(8,128)(2,1)S(1)} %get-tuple-element.155.refs_3_, ...), custom_call_target="tpu_custom_call" | custom-call | flops 704643072 | bytes 1048576 | tf_op jit(solution)/shard_map/cond/branch_1_fun/pallas_call | solution.py:389
  62.5 0.0 collective-permute-done.40.near_ref
  62.5 2.5 %collective-permute-done.41.far_ref = bf16[2,56,256]{2,1,0:T(8,128)(2,1)S(1)} collective-permute-done((bf16[2,56,256]{2,1,0:T(8,128)(2,1)S(1)}, bf16[2,56,256]{2,1,0:T(8,128)(2,1)S(1)}, u32[]{:S(2)}, u32[]{:S(2)}) %collective-permute-start.41) | collective-permute-done | bytes 57376 | tf_op jit(solution)/shard_map/cond/branch_1_fun/ppermute | solution.py:407
  65.0 0.7 branch_1_fun.30
  65.7 0.9 %copy-done.2 = bf16[1,1536,256]{2,1,0:T(8,128)(2,1)} copy-done((bf16[1,1536,256]{2,1,0:T(8,128)(2,1)}, bf16[1,1536,256]{2,1,0:T(8,128)(2,1)S(1)}, u32[]{:S(2)}) %copy-start.2) | copy-done | bytes 786456
  (12 shorter events, 0.1 us)
Async XLA Ops:
  0.6 8.1 %collective-permute-start.43 = (bf16[2,56,256]{2,1,0:T(8,128)(2,1)}, bf16[2,56,256]{2,1,0:T(8,128)(2,1)S(1)}, u32[]{:S(2)}, u32[]{:S(2)}) collective-permute-start(bf16[2,56,256]{2,1,0:T(8,128)(2,1)} %param.8), channel_id=1, source_target_pairs={{0,4},{1,5},{2,6},{3,7},{4,0},{5,1},{6,2},{7,3},{8,12},{9,13},{10,... | collective-permute-start | bytes 172040 | tf_op jit(solution)/shard_map/ppermute | solution.py:407
  1.2 7.6 %collective-permute-start.44 = (bf16[2,56,256]{2,1,0:T(8,128)(2,1)}, bf16[2,56,256]{2,1,0:T(8,128)(2,1)S(1)}, u32[]{:S(2)}, u32[]{:S(2)}) collective-permute-start(bf16[2,56,256]{2,1,0:T(8,128)(2,1)} %param.8), channel_id=1, source_target_pairs={{0,28},{1,29},{2,30},{3,31},{4,8},{5,9},{6,10},{7,11},{8,4},{9,5},... | collective-permute-start | bytes 172040 | tf_op jit(solution)/shard_map/ppermute | solution.py:407
  5.9 5.3 %collective-permute-start.45 = (bf16[2,56,256]{2,1,0:T(8,128)(2,1)}, bf16[2,56,256]{2,1,0:T(8,128)(2,1)S(1)}, u32[]{:S(2)}, u32[]{:S(2)}) collective-permute-start(bf16[2,56,256]{2,1,0:T(8,128)(2,1)} %param.8), channel_id=1, source_target_pairs={{0,16},{1,17},{2,18},{3,19},{4,20},{5,21},{6,22},{7,23},{8,24},{9,... | collective-permute-start | bytes 172040 | tf_op jit(solution)/shard_map/ppermute | solution.py:407
  11.2 9.6 %copy-start.1 = (bf16[1,1536,256]{2,1,0:T(8,128)(2,1)S(1)}, bf16[1,1536,256]{2,1,0:T(8,128)(2,1)}, u32[]{:S(2)}) copy-start(bf16[1,1536,256]{2,1,0:T(8,128)(2,1)} %get-tuple-element.168) | copy-start | bytes 2359300 | tf_op jit(solution)/shard_map/cond
  12.1 6.6 %collective-permute-start.26 = (bf16[2,56,256]{2,1,0:T(8,128)(2,1)S(1)}, bf16[2,56,256]{2,1,0:T(8,128)(2,1)S(1)}, u32[]{:S(2)}, u32[]{:S(2)}) collective-permute-start(bf16[2,56,256]{2,1,0:T(8,128)(2,1)S(1)} %get-tuple-element.115), channel_id=1, source_target_pairs={{0,1},{1,0},{2,3},{3,2},{4,5},{5,4},{6,7},{7,6},{8,9},{9,8},{10,11... | collective-permute-start | bytes 172040 | tf_op jit(solution)/shard_map/cond/branch_1_fun/ppermute | solution.py:407
  13.6 7.0 %collective-permute-start.27 = (bf16[2,56,256]{2,1,0:T(8,128)(2,1)S(1)}, bf16[2,56,256]{2,1,0:T(8,128)(2,1)S(1)}, u32[]{:S(2)}, u32[]{:S(2)}) collective-permute-start(bf16[2,56,256]{2,1,0:T(8,128)(2,1)S(1)} %get-tuple-element.116), channel_id=1, source_target_pairs={{0,2},{1,3},{2,0},{3,1},{4,6},{5,7},{6,4},{7,5},{8,10},{9,11},{10,... | collective-permute-start | bytes 172040 | tf_op jit(solution)/shard_map/cond/branch_1_fun/ppermute | solution.py:407
  15.2 5.6 %collective-permute-start.28 = (bf16[2,56,256]{2,1,0:T(8,128)(2,1)S(1)}, bf16[2,56,256]{2,1,0:T(8,128)(2,1)S(1)}, u32[]{:S(2)}, u32[]{:S(2)}) collective-permute-start(bf16[2,56,256]{2,1,0:T(8,128)(2,1)S(1)} %get-tuple-element.117), channel_id=1, source_target_pairs={{0,3},{1,2},{2,1},{3,0},{4,7},{5,6},{6,5},{7,4},{8,11},{9,10},{10,... | collective-permute-start | bytes 172040 | tf_op jit(solution)/shard_map/cond/branch_1_fun/ppermute | solution.py:407
  15.6 8.2 %collective-permute-start.23 = (bf16[2,56,256]{2,1,0:T(8,128)(2,1)S(1)}, bf16[2,56,256]{2,1,0:T(8,128)(2,1)S(1)}, u32[]{:S(2)}, u32[]{:S(2)}) collective-permute-start(bf16[2,56,256]{2,1,0:T(8,128)(2,1)S(1)} %get-tuple-element.107), channel_id=1, source_target_pairs={{0,1},{1,0},{2,3},{3,2},{4,5},{5,4},{6,7},{7,6},{8,9},{9,8},{10,11... | collective-permute-start | bytes 172040 | tf_op jit(solution)/shard_map/cond/branch_1_fun/ppermute | solution.py:407
  17.1 6.7 %collective-permute-start.24 = (bf16[2,56,256]{2,1,0:T(8,128)(2,1)S(1)}, bf16[2,56,256]{2,1,0:T(8,128)(2,1)S(1)}, u32[]{:S(2)}, u32[]{:S(2)}) collective-permute-start(bf16[2,56,256]{2,1,0:T(8,128)(2,1)S(1)} %get-tuple-element.108), channel_id=1, source_target_pairs={{0,2},{1,3},{2,0},{3,1},{4,6},{5,7},{6,4},{7,5},{8,10},{9,11},{10,... | collective-permute-start | bytes 172040 | tf_op jit(solution)/shard_map/cond/branch_1_fun/ppermute | solution.py:407
  18.6 5.7 %collective-permute-start.25 = (bf16[2,56,256]{2,1,0:T(8,128)(2,1)S(1)}, bf16[2,56,256]{2,1,0:T(8,128)(2,1)S(1)}, u32[]{:S(2)}, u32[]{:S(2)}) collective-permute-start(bf16[2,56,256]{2,1,0:T(8,128)(2,1)S(1)} %get-tuple-element.109), channel_id=1, source_target_pairs={{0,3},{1,2},{2,1},{3,0},{4,7},{5,6},{6,5},{7,4},{8,11},{9,10},{10,... | collective-permute-start | bytes 172040 | tf_op jit(solution)/shard_map/cond/branch_1_fun/ppermute | solution.py:407
  22.3 8.4 %collective-permute-start.29 = (f32[232,256]{1,0:T(8,128)S(1)}, f32[232,256]{1,0:T(8,128)S(1)}, u32[]{:S(2)}, u32[]{:S(2)}) collective-permute-start(f32[232,256]{1,0:T(8,128)S(1)} %get-tuple-element.118), channel_id=1, source_target_pairs={{0,1},{1,0},{2,3},{3,2},{4,5},{5,4},{6,7},{7,6},{8,9},{9,8},{10,11... | collective-permute-start | bytes 712712 | tf_op jit(solution)/shard_map/cond/branch_1_fun/ppermute | solution.py:407
  25.9 10.8 %collective-permute-start.30 = (f32[232,256]{1,0:T(8,128)S(1)}, f32[232,256]{1,0:T(8,128)S(1)}, u32[]{:S(2)}, u32[]{:S(2)}) collective-permute-start(f32[232,256]{1,0:T(8,128)S(1)} %get-tuple-element.119), channel_id=1, source_target_pairs={{0,2},{1,3},{2,0},{3,1},{4,6},{5,7},{6,4},{7,5},{8,10},{9,11},{10,... | collective-permute-start | bytes 712712 | tf_op jit(solution)/shard_map/cond/branch_1_fun/ppermute | solution.py:407
  28.6 8.2 %collective-permute-start.31 = (f32[232,256]{1,0:T(8,128)S(1)}, f32[232,256]{1,0:T(8,128)S(1)}, u32[]{:S(2)}, u32[]{:S(2)}) collective-permute-start(f32[232,256]{1,0:T(8,128)S(1)} %get-tuple-element.120), channel_id=1, source_target_pairs={{0,3},{1,2},{2,1},{3,0},{4,7},{5,6},{6,5},{7,4},{8,11},{9,10},{10,... | collective-permute-start | bytes 712712 | tf_op jit(solution)/shard_map/cond/branch_1_fun/ppermute | solution.py:407
  38.1 4.9 %collective-permute-start.32 = (bf16[240,256]{1,0:T(8,128)(2,1)S(1)}, bf16[240,256]{1,0:T(8,128)(2,1)S(1)}, u32[]{:S(2)}, u32[]{:S(2)}) collective-permute-start(bf16[240,256]{1,0:T(8,128)(2,1)S(1)} %get-tuple-element.121.d_ref.refs_6_), channel_id=1, source_target_pairs={{0,1},{1,0},{2,3},{3,2},{4,5},{5,4},{6,7},{7,6},{8,9},{9,8},{10,11... | collective-permute-start | bytes 368648 | tf_op jit(solution)/shard_map/cond/branch_1_fun/ppermute | solution.py:407
  38.5 6.2 %collective-permute-start.34 = (bf16[240,256]{1,0:T(8,128)(2,1)S(1)}, bf16[240,256]{1,0:T(8,128)(2,1)S(1)}, u32[]{:S(2)}, u32[]{:S(2)}) collective-permute-start(bf16[240,256]{1,0:T(8,128)(2,1)S(1)} %get-tuple-element.121.d_ref.refs_6_), channel_id=1, source_target_pairs={{0,3},{1,2},{2,1},{3,0},{4,7},{5,6},{6,5},{7,4},{8,11},{9,10},{10,... | collective-permute-start | bytes 368648 | tf_op jit(solution)/shard_map/cond/branch_1_fun/ppermute | solution.py:407
  40.5 5.5 %collective-permute-start.33 = (bf16[240,256]{1,0:T(8,128)(2,1)S(1)}, bf16[240,256]{1,0:T(8,128)(2,1)S(1)}, u32[]{:S(2)}, u32[]{:S(2)}) collective-permute-start(bf16[240,256]{1,0:T(8,128)(2,1)S(1)} %get-tuple-element.121.d_ref.refs_6_), channel_id=1, source_target_pairs={{0,2},{1,3},{2,0},{3,1},{4,6},{5,7},{6,4},{7,5},{8,10},{9,11},{10,... | collective-permute-start | bytes 368648 | tf_op jit(solution)/shard_map/cond/branch_1_fun/ppermute | solution.py:407
  49.0 8.3 %collective-permute-start.37 = (bf16[4,56,256]{2,1,0:T(8,128)(2,1)S(1)}, bf16[4,56,256]{2,1,0:T(8,128)(2,1)S(1)}, u32[]{:S(2)}, u32[]{:S(2)}) collective-permute-start(bf16[4,56,256]{2,1,0:T(8,128)(2,1)S(1)} %get-tuple-element.145), channel_id=1, source_target_pairs={{0,1},{1,0},{2,3},{3,2},{4,5},{5,4},{6,7},{7,6},{8,9},{9,8},{10,11... | collective-permute-start | bytes 344072 | tf_op jit(solution)/shard_map/cond/branch_1_fun/ppermute | solution.py:407
  50.3 7.0 %collective-permute-start.38 = (bf16[4,56,256]{2,1,0:T(8,128)(2,1)S(1)}, bf16[4,56,256]{2,1,0:T(8,128)(2,1)S(1)}, u32[]{:S(2)}, u32[]{:S(2)}) collective-permute-start(bf16[4,56,256]{2,1,0:T(8,128)(2,1)S(1)} %get-tuple-element.146), channel_id=1, source_target_pairs={{0,2},{1,3},{2,0},{3,1},{4,6},{5,7},{6,4},{7,5},{8,10},{9,11},{10,... | collective-permute-start | bytes 344072 | tf_op jit(solution)/shard_map/cond/branch_1_fun/ppermute | solution.py:407
  51.3 6.1 %collective-permute-start.39 = (bf16[4,56,256]{2,1,0:T(8,128)(2,1)S(1)}, bf16[4,56,256]{2,1,0:T(8,128)(2,1)S(1)}, u32[]{:S(2)}, u32[]{:S(2)}) collective-permute-start(bf16[4,56,256]{2,1,0:T(8,128)(2,1)S(1)} %get-tuple-element.147), channel_id=1, source_target_pairs={{0,3},{1,2},{2,1},{3,0},{4,7},{5,6},{6,5},{7,4},{8,11},{9,10},{10,... | collective-permute-start | bytes 344072 | tf_op jit(solution)/shard_map/cond/branch_1_fun/ppermute | solution.py:407
  52.6 1.2 %collective-permute-start.35 = (f32[1,128]{1,0:T(1,128)S(1)}, f32[1,128]{1,0:T(1,128)S(1)}, u32[]{:S(2)}, u32[]{:S(2)}) collective-permute-start(f32[1,128]{1,0:T(1,128)S(1)} %add_bitcast_fusion.1), channel_id=1, source_target_pairs={{0,4},{1,5},{2,6},{3,7},{4,0},{5,1},{6,2},{7,3},{8,12},{9,13},{10,... | collective-permute-start | bytes 1544 | tf_op jit(solution)/shard_map/cond/branch_1_fun/ppermute | solution.py:407
  53.7 3.6 %collective-permute-start.36 = (f32[1,128]{1,0:T(1,128)S(1)}, f32[1,128]{1,0:T(1,128)S(1)}, u32[]{:S(2)}, u32[]{:S(2)}) collective-permute-start(f32[1,128]{1,0:T(1,128)S(1)} %add.131), channel_id=1, source_target_pairs={{0,8},{1,9},{2,10},{3,11},{4,12},{5,13},{6,14},{7,15},{8,0},{9,1},... | collective-permute-start | bytes 1544 | tf_op jit(solution)/shard_map/cond/branch_1_fun/ppermute | solution.py:407
  58.0 7.0 %collective-permute-start.42 = (bf16[128,256]{1,0:T(8,128)(2,1)S(1)}, bf16[128,256]{1,0:T(8,128)(2,1)S(1)}, u32[]{:S(2)}, u32[]{:S(2)}) collective-permute-start(bf16[128,256]{1,0:T(8,128)(2,1)S(1)} %get-tuple-element.150), channel_id=1, source_target_pairs={{0,16},{1,17},{2,18},{3,19},{4,20},{5,21},{6,22},{7,23},{8,24},{9,... | collective-permute-start | bytes 196616 | tf_op jit(solution)/shard_map/cond/branch_1_fun/ppermute | solution.py:407
  59.2 3.4 %collective-permute-start.40 = (bf16[2,56,256]{2,1,0:T(8,128)(2,1)S(1)}, bf16[2,56,256]{2,1,0:T(8,128)(2,1)S(1)}, u32[]{:S(2)}, u32[]{:S(2)}) collective-permute-start(bf16[2,56,256]{2,1,0:T(8,128)(2,1)S(1)} %get-tuple-element.148), channel_id=1, source_target_pairs={{0,4},{1,5},{2,6},{3,7},{4,0},{5,1},{6,2},{7,3},{8,12},{9,13},{10,... | collective-permute-start | bytes 172040 | tf_op jit(solution)/shard_map/cond/branch_1_fun/ppermute | solution.py:407
  59.2 5.9 %collective-permute-start.41 = (bf16[2,56,256]{2,1,0:T(8,128)(2,1)S(1)}, bf16[2,56,256]{2,1,0:T(8,128)(2,1)S(1)}, u32[]{:S(2)}, u32[]{:S(2)}) collective-permute-start(bf16[2,56,256]{2,1,0:T(8,128)(2,1)S(1)} %get-tuple-element.149), channel_id=1, source_target_pairs={{0,28},{1,29},{2,30},{3,31},{4,8},{5,9},{6,10},{7,11},{8,4},{9,5},... | collective-permute-start | bytes 172040 | tf_op jit(solution)/shard_map/cond/branch_1_fun/ppermute | solution.py:407
  65.7 0.9 %copy-start.2 = (bf16[1,1536,256]{2,1,0:T(8,128)(2,1)}, bf16[1,1536,256]{2,1,0:T(8,128)(2,1)S(1)}, u32[]{:S(2)}) copy-start(bf16[1,1536,256]{2,1,0:T(8,128)(2,1)S(1)} %get-tuple-element.164) | copy-start | bytes 2359300
where the time goes:
time: 66.7 us; the launch traced here: 66.5 us
  starting transfers between devices  25.2 us (38%)
  Pallas kernels  19.9 us (30%)
  waiting for transfers between devices  18.5 us (28%)
  local copies, waits for them, and re-layouts  1.46 us (2%)
  between operations  1.31 us (2%)
    ppermute x23, starting transfers between devices, permute(): return lax.ppermute(x, AXES, pairs)  25.2 us
    ppermute x23, waiting for transfers between devices, permute(): return lax.ppermute(x, AXES, pairs)  18.5 us
    pallas_call x16, Pallas kernels, call(): pl.pallas_call(kernel, out_shape=out_shape, in_specs=in_specs, out_specs=...  18.3 us
    pallas_call x1, Pallas kernels, body(): pl.pallas_call(functools.partial(table_kernel, recs=recs, owned=owned), n...  1.61 us
  transfers between devices with their start and end apart: 23, of which 10 were waited for; matrix products, arithmetic and copies ran while one was open for 1% of the time, Pallas kernels for 20%

commit v1 on v0

--- a/solution.py
+++ b/solution.py
@@ -220,38 +220,31 @@
         at = at + jnp.where(used, 1, 0)
 
 
-def select_kernel(table_ref, a_ref, b_ref, c_ref, *out_refs, n_cand, order):
-    owned = a_ref.shape[0]
-    me = lax.axis_index("frame")
-    half = out_refs[0].shape[0]
-    for at, out_ref in enumerate(out_refs):
-        for i in range(half):
-            s = i if len(out_refs) == 1 else me ^ (at // 2) ^ order[at % 2 * half + i]
-            c = table_ref[3 * n_cand + s]
-            out_ref[i] = jnp.zeros(out_ref.shape[1:], out_ref.dtype)
-            for k, ref in enumerate((a_ref, b_ref, c_ref)):
-
-                @pl.when((c >= k * owned) & (c < (k + 1) * owned))
-                def _(ref=ref, k=k, i=i, c=c, out_ref=out_ref):
-                    out_ref[i] = ref[c - k * owned]
+def select_kernel(table_ref, a_ref, b_ref, c_ref, out_ref, *, slots, n_cand):
+    owned, _, _ = a_ref.shape
+    for s in range(slots):
+        c = table_ref[3 * n_cand + s]
+        out_ref[s] = jnp.zeros(out_ref.shape[1:], out_ref.dtype)
+        for i, ref in enumerate((a_ref, b_ref, c_ref)):
+
+            @pl.when((c >= i * owned) & (c < (i + 1) * owned))
+            def _(ref=ref, i=i, s=s, c=c):
+                out_ref[s] = ref[c - i * owned]
 
 
 def prepare_kernel(f_ref, out_ref):
     out_ref[...] = nt(eye(f_ref.shape[1]), f_ref[...]).astype(BF16)
 
 
-def forward_kernel(f_ref, ft_ref, *refs, unit, first, group, scale, place):
+def forward_kernel(f_ref, ft_ref, *refs, unit, first, group, scale):
     q_refs, (out_ref, weights_ref, top_ref, q_out_ref, q_ref) = refs[:group], refs[group:]
     me = lax.axis_index("frame")
     held, w, width = q_refs[0].shape
     slot = first + (me ^ unit)
     rows = group * w
     for j in range(group):
-        if place is None:
-            block = q_refs[j][jnp.minimum(slot, held - 1)].astype(F32)
-            q_ref[me ^ j] = jnp.where(slot < held, block, 0.0)
-        else:
-            q_ref[me ^ j] = q_refs[j][place].astype(F32)
+        block = q_refs[j][jnp.minimum(slot, held - 1)].astype(F32)
+        q_ref[me ^ j] = jnp.where(slot < held, block, 0.0)
     q = q_ref[...].reshape(rows, width).astype(BF16)
     q_out_ref[...] = q
     s = nt(f_ref[...], q) * scale
@@ -315,18 +308,23 @@
 
 
 def spread_kernel(*refs, units, group):
-    in_refs, out_refs = refs[:units], refs[units:]
+    in_refs, d_refs, out_refs, loss_ref = refs[:units], refs[units : 2 * units], refs[2 * units : -1], refs[-1]
     me = lax.axis_index("frame")
+    rows = d_refs[0].shape[0] - EXTRA
+    loss = jnp.zeros(loss_ref.shape, F32)
     for i in range(units):
+        loss = loss + unpack(d_refs[i][rows:].astype(F32), 1, loss_ref.shape[1])
         slot = (i // group) * group + (me ^ (i % group))
         for j, ref in enumerate(out_refs):
-            if units == group:
+            if ref.shape[0] == units:
                 ref[slot] = in_refs[i][me ^ j].astype(ref.dtype)
             else:
 
                 @pl.when(slot < ref.shape[0])
                 def _(ref=ref, i=i, j=j, slot=slot):
                     ref[slot] = in_refs[i][me ^ j].astype(ref.dtype)
+
+    loss_ref[...] = loss
 
 
 def frames_kernel(*refs, units):
@@ -358,30 +356,31 @@
         copy.wait()
 
 
-def finish_kernel(table_ref, loss_ref, *refs, n_cand):
+def finish_kernel(table_ref, pair_ref, across_ref, *refs, n_cand):
     in_refs, outs = refs[:-3], refs[-3:]
     owned = n_cand // 3
     w, width = in_refs[0].shape[1:]
     for c in range(n_cand):
         s = table_ref[2 * n_cand + c]
-        k, j = c // owned, c % owned
+        j = c % owned
         at = jnp.maximum(s, 0)
         total = functools.reduce(jnp.add, [x[at].astype(F32) for x in in_refs])
-        total = jnp.where(s >= 0, total, 0.0).astype(BF16)
-        if k < 2:
-            outs[k][j] = total
-        else:
-            outs[k][j * w : (j + 1) * w] = total
-    pieces = [x.astype(F32) for x in split(loss_ref[...])]
-    outs[2][owned * w :] = stack(pieces, EXTRA, width).astype(BF16)
-
-
-def close_kernel(loss_ref, near_ref, far_ref, cross_ref, out_ref, total_ref):
-    owned, w, _ = near_ref.shape
+        outs[c // owned][j * w : (j + 1) * w] = jnp.where(s >= 0, total, 0.0).astype(BF16)
+    for ref, loss_ref in zip(outs, (across_ref, across_ref, pair_ref)):
+        pieces = [x.astype(F32) for x in split(loss_ref[...])]
+        ref[owned * w :] = stack(pieces, EXTRA, width).astype(BF16)
+
+
+def close_kernel(pair_ref, near_ref, far_ref, cross_ref, out_ref, total_ref):
+    owned, w, _ = out_ref.shape
+    loss = pair_ref[...]
+    for ref in (near_ref, far_ref, cross_ref):
+        loss = loss + unpack(ref[owned * w :].astype(F32), 0, total_ref.shape[1])
+    total_ref[...] = loss
     for j in range(owned):
-        total = near_ref[j].astype(F32) + far_ref[j].astype(F32)
-        out_ref[j] = (total + cross_ref[j * w : (j + 1) * w].astype(F32)).astype(BF16)
-    total_ref[...] = loss_ref[...] + unpack(cross_ref[owned * w :].astype(F32), 0, total_ref.shape[1])
+        at = slice(j * w, (j + 1) * w)
+        total = near_ref[at].astype(F32) + far_ref[at].astype(F32)
+        out_ref[j] = (total + cross_ref[at].astype(F32)).astype(BF16)
 
 
 def call(kernel, out_shape, in_specs, *args, scratch=(), flops=0, nbytes=1 << 20, vmem=16, out_specs=None):
@@ -433,30 +432,19 @@
     xor = [lambda r, g, j=j: (r, g ^ j) for j in range(group)]
     order = [3, 1, 2, 0]
 
-    halves = 2 if slots == group else 1
     q = call(
-        functools.partial(select_kernel, n_cand=n_cand, order=order),
-        [shape((slots // halves, w, width), BF16)] * (2 * group if halves == 2 else 1),
+        functools.partial(select_kernel, slots=slots, n_cand=n_cand),
+        shape((slots, w, width), BF16),
         [SMEM, VMEM, VMEM, VMEM],
         table, near, far, cross,
     )
-    qs = []
-    for h in range(halves):
-        part = [q[2 * j + h] if halves == 2 else q[0] for j in range(group)]
-        qs.append(part[:1] + [permute(part[j], recs, group, xor[j]) for j in range(1, group)])
+    qs = [q] + [permute(q, recs, group, xor[j]) for j in range(1, group)]
     ft = call(prepare_kernel, shape((width, depth), BF16), [VMEM], f, flops=cost)
     made, sent = {}, {}
     for r in range(rounds):
         for i in order:
             made[r, i] = call(
-                functools.partial(
-                    forward_kernel,
-                    unit=i,
-                    first=r * group,
-                    group=group,
-                    scale=scale,
-                    place=order.index(i) % 2 if halves == 2 else None,
-                ),
+functools.partial(forward_kernel, unit=i, first=r * group, group=group, scale=scale),
                 [
                     shape((rows + LINES, width), F32),
                     shape((depth, rows), F32),
@@ -464,7 +452,7 @@
                     shape((rows, width), BF16),
                 ],
                 [VMEM] * (2 + group),
-                f, ft, *qs[order.index(i) // 2 if halves == 2 else 0],
+                f, ft, *qs,
                 scratch=[pltpu.VMEM((group, w, width), F32)],
                 flops=2 * cost,
             )
@@ -496,22 +484,17 @@
                 flops=2 * cost,
             )
     keys = [(r, i) for r in range(rounds) for i in range(group)]
-    dqs = call(
+    *dqs, loss = call(
         functools.partial(spread_kernel, units=units, group=group),
-        [shape((slots, w, width), BF16)] * group,
-        [VMEM] * units,
-        *[back[k][0] for k in keys],
-    )
-
-    loss = 0
-    for k in keys:
-        loss = loss + jnp.sum(ds[k][rows + 3 : rows + 6, :128].astype(F32), axis=0, keepdims=True)
-    *dqs, loss = lax.optimization_barrier((*dqs, loss))
+        [shape((slots, w, width), BF16)] * group + [shape((1, 128), F32)],
+        [VMEM] * (2 * units),
+        *[back[k][0] for k in keys], *[ds[k] for k in keys],
+    )
     dqs = [dqs[0]] + [permute(dqs[j], recs, group, xor[j]) for j in range(1, group)]
-    step, total, half = 1, None, units // 2
+    pair = loss + permute(loss, recs, group, lambda r, g: (r ^ 2, g))
+    across = loss + permute(loss, recs, group, lambda r, g: (cross_of(r, recs), g))
+    total, half = None, units // 2
     for n, some in enumerate((keys[:half], keys[half:])):
-        if step < recs // 2:
-            other = permute(loss, recs, group, lambda r, g, k=step: (r ^ k, g))
         args = [back[k][1] for k in some] + [made[k][3] for k in some]
         args += [back[k][2] for k in some] + [ds[k] for k in some]
         if n == 0:
@@ -526,26 +509,19 @@
             blocks = 3 if depth % 384 == 0 else 1
             total = call(
                 functools.partial(last_frames_kernel, units=half),
-                shape(frames.shape, BF16),
+                pltpu.HBM(frames.shape, BF16),
                 [VMEM] * (len(args) + 1),
                 *args, total,
                 out_specs=pl.BlockSpec(memory_space=pltpu.HBM),
                 scratch=[pltpu.VMEM((depth, width), BF16), pltpu.SemaphoreType.DMA((blocks,))],
                 flops=2 * half * cost,
             )
-        if step < recs // 2:
-            if n == 0:
-                total, other = lax.optimization_barrier((total, other))
-            loss = loss + other
-            step *= 2
-    while step < recs // 2:
-        loss = loss + permute(loss, recs, group, lambda r, g, k=step: (r ^ k, g))
-        step *= 2
+    pair, across, *dqs = lax.optimization_barrier((pair, across, *dqs))
     home = call(
         functools.partial(finish_kernel, n_cand=n_cand),
-        [shape((owned, w, width), BF16)] * 2 + [shape((owned * w + EXTRA, width), BF16)],
-        [SMEM] + [VMEM] * (1 + group),
-        table, loss, *dqs,
+        [shape((owned * w + EXTRA, width), BF16)] * 3,
+        [SMEM] + [VMEM] * (2 + group),
+        table, pair, across, *dqs,
     )
     got = []
     for x, where in zip(home, (near_of, far_of, cross_of)):
@@ -554,7 +530,7 @@
         close_kernel,
         [shape((owned, w, width), BF16), shape((1, 128), F32)],
         [VMEM] * 4,
-        loss, *got,
+        pair, *got,
     )
     return loss[0, 0], total, texts
 
@@ -562,11 +538,12 @@
 def body(frames, texts, pair_rec, pair_text, pair_label):
     recs, group = lax.axis_size("rec"), lax.axis_size("frame")
     owned, w, _ = texts.shape
-    if group != 4 or w % 8 or recs < 4 or recs & (recs - 1) or 3 * owned > 2 * group or owned * recs > 32:
+    if group != 4 or w % 8 or recs != 8 or 3 * owned > 2 * group or owned * recs > 32:
         return general_body(frames, texts, pair_rec, pair_text, pair_label)
-    near, far, cross = [
-        permute(texts, recs, group, lambda r, g, to=to: (to(r, recs), g)) for to in (near_of, far_of, cross_of)
-    ]
+    fetched = []
+    for to in (near_of, far_of, cross_of):
+        fetched.append(permute(texts, recs, group, lambda r, g: (to(r, recs), g)))
+    near, far, cross = fetched
     n_cand = 3 * owned
     table = pl.pallas_call(
         functools.partial(table_kernel, recs=recs, owned=owned),

time: 66.7 us -> 66.1 us (level)
  waiting for transfers between devices: 18.5 us -> 20.1 us
  starting transfers between devices: 25.2 us -> 24.3 us
  local copies, waits for them, and re-layouts: 1.46 us -> 0.59 us
    ppermute x23 -> x20, waiting for transfers between devices: 18.5 us -> 20.1 us  [permute(): return lax.ppermute(x, AXES, pairs)]
    ppermute x23 -> x20, starting transfers between devices: 25.2 us -> 24.3 us  [permute(): return lax.ppermute(x, AXES, pairs)]
    unnamed x2 -> x0, local copies, waits for them, and re-layouts: 0.88 us -> none
  transfers between devices with their start and end apart: 23 -> 20, of which waited for: 10 -> 13; matrix products, arithmetic and copies ran while one was open for 1% -> 1% of each run, Pallas kernels for 20% -> 21%
where the time goes in v1:
time: 66.1 us; the launch traced here: 65.9 us
  starting transfers between devices  24.3 us (37%)
  waiting for transfers between devices  20.1 us (30%)
  Pallas kernels  19.5 us (30%)
  between operations  1.31 us (2%)
    ppermute x20, starting transfers between devices, permute(): return lax.ppermute(x, AXES, pairs)  24.3 us
    ppermute x20, waiting for transfers between devices, permute(): return lax.ppermute(x, AXES, pairs)  20.1 us
    pallas_call x16, Pallas kernels, call(): pl.pallas_call(kernel, out_shape=out_shape, in_specs=in_specs, out_specs=...  17.9 us
    pallas_call x1, Pallas kernels, body(): pl.pallas_call(functools.partial(table_kernel, recs=recs, owned=owned), n...  1.61 us
  transfers between devices with their start and end apart: 20, of which 13 were waited for; matrix products, arithmetic and copies ran while one was open for 1% of the time, Pallas kernels for 21%

profile of v1, /device:TPU:0, one launch (start us, length us, event | category | flops | bytes accessed | tf_op | source)
XLA Modules:
  0.0 65.9 jit_solution(17186010158193958956)
XLA Ops:
  0.6 0.6 collective-permute-start.40
  1.2 4.7 %collective-permute-start.41 = (bf16[2,56,256]{2,1,0:T(8,128)(2,1)}, bf16[2,56,256]{2,1,0:T(8,128)(2,1)S(1)}, u32[]{:S(2)}, u32[]{:S(2)}) collective-permute-start(bf16[2,56,256]{2,1,0:T(8,128)(2,1)} %param.8), channel_id=1, source_target_pairs={{0,28},{1,29},{2,30},{3,31},{4,8},{5,9},{6,10},{7,11},{8,4},{9,5},... | collective-permute-start | bytes 172040 | tf_op jit(solution)/shard_map/ppermute | solution.py:406
  5.9 0.0 collective-permute-start.42
  5.9 1.6 %table.1 = s32[26]{0:T(128)S(1)} custom-call(s32[16]{0:T(128)} %bitcast.34, s32[16]{0:T(128)} %text_ref.1, s32[16]{0:T(128)} %label_ref.1), custom_call_target="tpu_custom_call" | custom-call | tf_op jit(solution)/shard_map/table/pallas_call | solution.py:548
  7.5 0.6 slice.9
  8.7 0.0 collective-permute-done.40
  8.8 0.0 collective-permute-done.41
  8.8 2.4 %collective-permute-done.42 = bf16[2,56,256]{2,1,0:T(8,128)(2,1)S(1)} collective-permute-done((bf16[2,56,256]{2,1,0:T(8,128)(2,1)}, bf16[2,56,256]{2,1,0:T(8,128)(2,1)S(1)}, u32[]{:S(2)}, u32[]{:S(2)}) %collective-permute-start.42) | collective-permute-done | bytes 57376 | tf_op jit(solution)/shard_map/ppermute | solution.py:406
  11.2 54.8 %conditional.1 = (bf16[2,56,256]{2,1,0:T(8,128)(2,1)}, f32[]{:T(128)}, bf16[1,1536,256]{2,1,0:T(8,128)(2,1)}) conditional(s32[]{:T(128)} %bitcast.5, (bf16[1,1536,256]{2,1,0:T(8,128)(2,1)}, s32[26]{0:T(128)S(1)}, bf16[2,56,256]{2,1,0:T(8,128)(2,1)S(1)}, bf16[2,56,256]{2,1,0:T(8,128)(2,1)S(1)}, bf16[2,56,256]{2,1,0:T(8,128)(2,1)S(1)}) %tuple.17, ...), branch_computations={%region_0.0_spmd, %region_1.0_spmd} | conditional | flops 8631877632 | bytes 42933708 | solution.py:561
  11.2 0.0 copy-start.1
  11.2 0.6 branch_1_fun.17.refs_0_
  11.8 1.6 %collective-permute-start.23 = (bf16[4,56,256]{2,1,0:T(8,128)(2,1)S(1)}, bf16[4,56,256]{2,1,0:T(8,128)(2,1)S(1)}, u32[]{:S(2)}, u32[]{:S(2)}) collective-permute-start(bf16[4,56,256]{2,1,0:T(8,128)(2,1)S(1)} %branch_1_fun.17.refs_0_), channel_id=1, source_target_pairs={{0,1},{1,0},{2,3},{3,2},{4,5},{5,4},{6,7},{7,6},{8,9},{9,8},{10,11... | collective-permute-start | bytes 344072 | tf_op jit(solution)/shard_map/cond/branch_1_fun/ppermute | solution.py:406
  13.4 1.5 %collective-permute-start.24 = (bf16[4,56,256]{2,1,0:T(8,128)(2,1)S(1)}, bf16[4,56,256]{2,1,0:T(8,128)(2,1)S(1)}, u32[]{:S(2)}, u32[]{:S(2)}) collective-permute-start(bf16[4,56,256]{2,1,0:T(8,128)(2,1)S(1)} %branch_1_fun.17.refs_0_), channel_id=1, source_target_pairs={{0,2},{1,3},{2,0},{3,1},{4,6},{5,7},{6,4},{7,5},{8,10},{9,11},{10,... | collective-permute-start | bytes 344072 | tf_op jit(solution)/shard_map/cond/branch_1_fun/ppermute | solution.py:406
  14.9 0.5 collective-permute-start.25
  15.4 1.5 %branch_1_fun.16.ft_ref = bf16[256,1536]{1,0:T(8,128)(2,1)S(1)} custom-call(bf16[1536,256]{1,0:T(8,128)(2,1)} %bitcast.25), custom_call_target="tpu_custom_call" | custom-call | flops 176160768 | bytes 1048576 | tf_op jit(solution)/shard_map/cond/branch_1_fun/pallas_call | solution.py:388
  16.9 0.8 %collective-permute-done.23.refs_1_ = bf16[4,56,256]{2,1,0:T(8,128)(2,1)S(1)} collective-permute-done((bf16[4,56,256]{2,1,0:T(8,128)(2,1)S(1)}, bf16[4,56,256]{2,1,0:T(8,128)(2,1)S(1)}, u32[]{:S(2)}, u32[]{:S(2)}) %collective-permute-start.23) | collective-permute-done | bytes 114720 | tf_op jit(solution)/shard_map/cond/branch_1_fun/ppermute | solution.py:406
  17.7 1.5 %collective-permute-done.24.refs_2_ = bf16[4,56,256]{2,1,0:T(8,128)(2,1)S(1)} collective-permute-done((bf16[4,56,256]{2,1,0:T(8,128)(2,1)S(1)}, bf16[4,56,256]{2,1,0:T(8,128)(2,1)S(1)}, u32[]{:S(2)}, u32[]{:S(2)}) %collective-permute-start.24) | collective-permute-done | bytes 114720 | tf_op jit(solution)/shard_map/cond/branch_1_fun/ppermute | solution.py:406
  19.2 1.4 %collective-permute-done.25.refs_3_ = bf16[4,56,256]{2,1,0:T(8,128)(2,1)S(1)} collective-permute-done((bf16[4,56,256]{2,1,0:T(8,128)(2,1)S(1)}, bf16[4,56,256]{2,1,0:T(8,128)(2,1)S(1)}, u32[]{:S(2)}, u32[]{:S(2)}) %collective-permute-start.25) | collective-permute-done | bytes 114720 | tf_op jit(solution)/shard_map/cond/branch_1_fun/ppermute | solution.py:406
  20.6 0.0 copy-done.1
  20.6 1.6 %branch_1_fun.19 = (f32[232,256]{1,0:T(8,128)S(1)}, f32[1536,224]{1,0:T(8,128)S(1)}, f32[1,224]{1,0:T(1,128)S(1)}, bf16[224,256]{1,0:T(8,128)(2,1)S(1)}) custom-call(bf16[1536,256]{1,0:T(8,128)(2,1)S(1)} %bitcast.26, bf16[256,1536]{1,0:T(8,128)(2,1)S(1)} %branch_1_fun.16.ft_ref, bf16[4,56,256]{2,1,0:T(8,128)(2,1)S(1)} %branch_1_fun.17.refs_0_, ...), custom_call_target="tpu_custom_call" | custom-call | flops 352321536 | bytes 1048576 | tf_op jit(solution)/shard_map/cond/branch_1_fun/pallas_call | solution.py:388
  22.2 0.6 collective-permute-start.26
  22.7 1.6 %branch_1_fun.20 = (f32[232,256]{1,0:T(8,128)S(1)}, f32[1536,224]{1,0:T(8,128)S(1)}, f32[1,224]{1,0:T(1,128)S(1)}, bf16[224,256]{1,0:T(8,128)(2,1)S(1)}) custom-call(bf16[1536,256]{1,0:T(8,128)(2,1)S(1)} %bitcast.27, bf16[256,1536]{1,0:T(8,128)(2,1)S(1)} %branch_1_fun.16.ft_ref, bf16[4,56,256]{2,1,0:T(8,128)(2,1)S(1)} %branch_1_fun.17.refs_0_, ...), custom_call_target="tpu_custom_call" | custom-call | flops 352321536 | bytes 1048576 | tf_op jit(solution)/shard_map/cond/branch_1_fun/pallas_call | solution.py:388
  24.3 0.6 collective-permute-start.27
  24.9 1.6 %branch_1_fun.21 = (f32[232,256]{1,0:T(8,128)S(1)}, f32[1536,224]{1,0:T(8,128)S(1)}, f32[1,224]{1,0:T(1,128)S(1)}, bf16[224,256]{1,0:T(8,128)(2,1)S(1)}) custom-call(bf16[1536,256]{1,0:T(8,128)(2,1)S(1)} %bitcast.28, bf16[256,1536]{1,0:T(8,128)(2,1)S(1)} %branch_1_fun.16.ft_ref, bf16[4,56,256]{2,1,0:T(8,128)(2,1)S(1)} %branch_1_fun.17.refs_0_, ...), custom_call_target="tpu_custom_call" | custom-call | flops 352321536 | bytes 1048576 | tf_op jit(solution)/shard_map/cond/branch_1_fun/pallas_call | solution.py:388
  26.5 2.5 %collective-permute-start.28 = (f32[232,256]{1,0:T(8,128)S(1)}, f32[232,256]{1,0:T(8,128)S(1)}, u32[]{:S(2)}, u32[]{:S(2)}) collective-permute-start(f32[232,256]{1,0:T(8,128)S(1)} %get-tuple-element.112), channel_id=1, source_target_pairs={{0,3},{1,2},{2,1},{3,0},{4,7},{5,6},{6,5},{7,4},{8,11},{9,10},{10,... | collective-permute-start | bytes 712712 | tf_op jit(solution)/shard_map/cond/branch_1_fun/ppermute | solution.py:406
  28.9 1.6 %branch_1_fun.18 = (f32[232,256]{1,0:T(8,128)S(1)}, f32[1536,224]{1,0:T(8,128)S(1)}, f32[1,224]{1,0:T(1,128)S(1)}, bf16[224,256]{1,0:T(8,128)(2,1)S(1)}) custom-call(bf16[1536,256]{1,0:T(8,128)(2,1)S(1)} %bitcast.29, bf16[256,1536]{1,0:T(8,128)(2,1)S(1)} %branch_1_fun.16.ft_ref, bf16[4,56,256]{2,1,0:T(8,128)(2,1)S(1)} %branch_1_fun.17.refs_0_, ...), custom_call_target="tpu_custom_call" | custom-call | flops 352321536 | bytes 1048576 | tf_op jit(solution)/shard_map/cond/branch_1_fun/pallas_call | solution.py:388
  30.5 0.0 collective-permute-done.26.refs_1_
  30.5 4.8 %collective-permute-done.27.refs_2_ = f32[232,256]{1,0:T(8,128)S(1)} collective-permute-done((f32[232,256]{1,0:T(8,128)S(1)}, f32[232,256]{1,0:T(8,128)S(1)}, u32[]{:S(2)}, u32[]{:S(2)}) %collective-permute-start.27) | collective-permute-done | bytes 237600 | tf_op jit(solution)/shard_map/cond/branch_1_fun/ppermute | solution.py:406
  35.3 0.0 collective-permute-done.28.refs_3_
  35.3 1.4 %branch_1_fun.22 = (bf16[240,256]{1,0:T(8,128)(2,1)S(1)}, f32[224,256]{1,0:T(8,128)S(1)}) custom-call(s32[26]{0:T(128)S(1)} %get-tuple-element.102.table_ref, bf16[224,256]{1,0:T(8,128)(2,1)S(1)} %get-tuple-element.108.q_ref.refs_2_, f32[232,256]{1,0:T(8,128)S(1)} %get-tuple-element.109.refs_0_, f32[232,256]{1,0:T(8,128)S(1)} %collective-permute-done.26.refs_1_, ...), custom_call_target="tpu_custom_call" | custom-call | bytes 1048576 | tf_op jit(solution)/shard_map/cond/branch_1_fun/pallas_call | solution.py:388
  36.7 1.5 %collective-permute-start.29 = (bf16[240,256]{1,0:T(8,128)(2,1)S(1)}, bf16[240,256]{1,0:T(8,128)(2,1)S(1)}, u32[]{:S(2)}, u32[]{:S(2)}) collective-permute-start(bf16[240,256]{1,0:T(8,128)(2,1)S(1)} %get-tuple-element.113.d_ref.refs_4_.refs_6_), channel_id=1, source_target_pairs={{0,1},{1,0},{2,3},{3,2},{4,5},{5,4},{6,7},{7,6},{8,9},{9,8},{10,11... | collective-permute-start | bytes 368648 | tf_op jit(solution)/shard_map/cond/branch_1_fun/ppermute | solution.py:406
  38.2 0.8 %collective-permute-start.31 = (bf16[240,256]{1,0:T(8,128)(2,1)S(1)}, bf16[240,256]{1,0:T(8,128)(2,1)S(1)}, u32[]{:S(2)}, u32[]{:S(2)}) collective-permute-start(bf16[240,256]{1,0:T(8,128)(2,1)S(1)} %get-tuple-element.113.d_ref.refs_4_.refs_6_), channel_id=1, source_target_pairs={{0,3},{1,2},{2,1},{3,0},{4,7},{5,6},{6,5},{7,4},{8,11},{9,10},{10,... | collective-permute-start | bytes 368648 | tf_op jit(solution)/shard_map/cond/branch_1_fun/ppermute | solution.py:406
  39.0 1.3 %collective-permute-start.30 = (bf16[240,256]{1,0:T(8,128)(2,1)S(1)}, bf16[240,256]{1,0:T(8,128)(2,1)S(1)}, u32[]{:S(2)}, u32[]{:S(2)}) collective-permute-start(bf16[240,256]{1,0:T(8,128)(2,1)S(1)} %get-tuple-element.113.d_ref.refs_4_.refs_6_), channel_id=1, source_target_pairs={{0,2},{1,3},{2,0},{3,1},{4,6},{5,7},{6,4},{7,5},{8,10},{9,11},{10,... | collective-permute-start | bytes 368648 | tf_op jit(solution)/shard_map/cond/branch_1_fun/ppermute | solution.py:406
  40.3 1.0 %branch_1_fun.23 = (f32[4,56,256]{2,1,0:T(8,128)S(1)}, bf16[1536,224]{1,0:T(8,128)(2,1)S(1)}, bf16[1536,224]{1,0:T(8,128)(2,1)S(1)}) custom-call(bf16[1536,256]{1,0:T(8,128)(2,1)S(1)} %bitcast.30, bf16[256,1536]{1,0:T(8,128)(2,1)S(1)} %branch_1_fun.16.ft_ref, f32[1536,224]{1,0:T(8,128)S(1)} %get-tuple-element.106.weights_ref, ...), custom_call_target="tpu_custom_call" | custom-call | flops 352321536 | bytes 1048576 | tf_op jit(solution)/shard_map/cond/branch_1_fun/pallas_call | solution.py:388
  41.3 0.4 collective-permute-done.29.d_ref.refs_5_.refs_7_
  41.7 1.0 %branch_1_fun.24 = (f32[4,56,256]{2,1,0:T(8,128)S(1)}, bf16[1536,224]{1,0:T(8,128)(2,1)S(1)}, bf16[1536,224]{1,0:T(8,128)(2,1)S(1)}) custom-call(bf16[1536,256]{1,0:T(8,128)(2,1)S(1)} %bitcast.31, bf16[256,1536]{1,0:T(8,128)(2,1)S(1)} %branch_1_fun.16.ft_ref, f32[1536,224]{1,0:T(8,128)S(1)} %get-tuple-element.116.weights_ref, ...), custom_call_target="tpu_custom_call" | custom-call | flops 352321536 | bytes 1048576 | tf_op jit(solution)/shard_map/cond/branch_1_fun/pallas_call | solution.py:388
  42.7 1.5 %collective-permute-done.31.d_ref.refs_7_ = bf16[240,256]{1,0:T(8,128)(2,1)S(1)} collective-permute-done((bf16[240,256]{1,0:T(8,128)(2,1)S(1)}, bf16[240,256]{1,0:T(8,128)(2,1)S(1)}, u32[]{:S(2)}, u32[]{:S(2)}) %collective-permute-start.31) | collective-permute-done | bytes 122912 | tf_op jit(solution)/shard_map/cond/branch_1_fun/ppermute | solution.py:406
  44.1 1.0 %branch_1_fun.26 = (f32[4,56,256]{2,1,0:T(8,128)S(1)}, bf16[1536,224]{1,0:T(8,128)(2,1)S(1)}, bf16[1536,224]{1,0:T(8,128)(2,1)S(1)}) custom-call(bf16[1536,256]{1,0:T(8,128)(2,1)S(1)} %bitcast.32, bf16[256,1536]{1,0:T(8,128)(2,1)S(1)} %branch_1_fun.16.ft_ref, f32[1536,224]{1,0:T(8,128)S(1)} %get-tuple-element.122.weights_ref, ...), custom_call_target="tpu_custom_call" | custom-call | flops 352321536 | bytes 1048576 | tf_op jit(solution)/shard_map/cond/branch_1_fun/pallas_call | solution.py:388
  45.1 0.1 collective-permute-done.30.d_ref.refs_6_
  45.2 1.0 %branch_1_fun.25 = (f32[4,56,256]{2,1,0:T(8,128)S(1)}, bf16[1536,224]{1,0:T(8,128)(2,1)S(1)}, bf16[1536,224]{1,0:T(8,128)(2,1)S(1)}) custom-call(bf16[1536,256]{1,0:T(8,128)(2,1)S(1)} %bitcast.33, bf16[256,1536]{1,0:T(8,128)(2,1)S(1)} %branch_1_fun.16.ft_ref, f32[1536,224]{1,0:T(8,128)S(1)} %get-tuple-element.119.weights_ref, ...), custom_call_target="tpu_custom_call" | custom-call | flops 352321536 | bytes 1048576 | tf_op jit(solution)/shard_map/cond/branch_1_fun/pallas_call | solution.py:388
  46.2 0.1 branch_1_fun.27
  46.3 0.1 collective-permute-start.32
  46.4 2.9 %collective-permute-start.33 = (f32[1,128]{1,0:T(1,128)S(1)}, f32[1,128]{1,0:T(1,128)S(1)}, u32[]{:S(2)}, u32[]{:S(2)}) collective-permute-start(f32[1,128]{1,0:T(1,128)S(1)} %get-tuple-element.125), channel_id=1, source_target_pairs={{0,16},{1,17},{2,18},{3,19},{4,20},{5,21},{6,22},{7,23},{8,24},{9,... | collective-permute-start | bytes 1544 | tf_op jit(solution)/shard_map/cond/branch_1_fun/ppermute | solution.py:406
  49.2 1.1 %collective-permute-start.34 = (bf16[4,56,256]{2,1,0:T(8,128)(2,1)S(1)}, bf16[4,56,256]{2,1,0:T(8,128)(2,1)S(1)}, u32[]{:S(2)}, u32[]{:S(2)}) collective-permute-start(bf16[4,56,256]{2,1,0:T(8,128)(2,1)S(1)} %get-tuple-element.127), channel_id=1, source_target_pairs={{0,1},{1,0},{2,3},{3,2},{4,5},{5,4},{6,7},{7,6},{8,9},{9,8},{10,11... | collective-permute-start | bytes 344072 | tf_op jit(solution)/shard_map/cond/branch_1_fun/ppermute | solution.py:406
  50.4 0.8 %collective-permute-start.35 = (bf16[4,56,256]{2,1,0:T(8,128)(2,1)S(1)}, bf16[4,56,256]{2,1,0:T(8,128)(2,1)S(1)}, u32[]{:S(2)}, u32[]{:S(2)}) collective-permute-start(bf16[4,56,256]{2,1,0:T(8,128)(2,1)S(1)} %get-tuple-element.128), channel_id=1, source_target_pairs={{0,2},{1,3},{2,0},{3,1},{4,6},{5,7},{6,4},{7,5},{8,10},{9,11},{10,... | collective-permute-start | bytes 344072 | tf_op jit(solution)/shard_map/cond/branch_1_fun/ppermute | solution.py:406
  51.2 1.5 %collective-permute-start.36 = (bf16[4,56,256]{2,1,0:T(8,128)(2,1)S(1)}, bf16[4,56,256]{2,1,0:T(8,128)(2,1)S(1)}, u32[]{:S(2)}, u32[]{:S(2)}) collective-permute-start(bf16[4,56,256]{2,1,0:T(8,128)(2,1)S(1)} %get-tuple-element.129), channel_id=1, source_target_pairs={{0,3},{1,2},{2,1},{3,0},{4,7},{5,6},{6,5},{7,4},{8,11},{9,10},{10,... | collective-permute-start | bytes 344072 | tf_op jit(solution)/shard_map/cond/branch_1_fun/ppermute | solution.py:406
  52.7 1.0 %branch_1_fun.30.refs_8_ = f32[1536,256]{1,0:T(8,128)S(1)} custom-call(bf16[1536,224]{1,0:T(8,128)(2,1)S(1)} %get-tuple-element.146.refs_0_, bf16[1536,224]{1,0:T(8,128)(2,1)S(1)} %get-tuple-element.147.refs_1_, bf16[224,256]{1,0:T(8,128)(2,1)S(1)} %get-tuple-element.108.q_ref.refs_2_, bf16[224,256]{1,0:T(8,128)(2,1)S(1)} %get-tuple-element.148.refs_3_, ...), custom_call_target="tpu_custom_call" | custom-call | flops 704643072 | bytes 1048576 | tf_op jit(solution)/shard_map/cond/branch_1_fun/pallas_call | solution.py:388
  53.7 0.0 collective-permute-done.32
  53.7 0.0 collective-permute-done.33
  53.8 0.3 collective-permute-done.34.refs_1_
  54.0 1.1 %collective-permute-done.35.refs_2_ = bf16[4,56,256]{2,1,0:T(8,128)(2,1)S(1)} collective-permute-done((bf16[4,56,256]{2,1,0:T(8,128)(2,1)S(1)}, bf16[4,56,256]{2,1,0:T(8,128)(2,1)S(1)}, u32[]{:S(2)}, u32[]{:S(2)}) %collective-permute-start.35) | collective-permute-done | bytes 114720 | tf_op jit(solution)/shard_map/cond/branch_1_fun/ppermute | solution.py:406
  55.2 1.7 %collective-permute-done.36.refs_3_ = bf16[4,56,256]{2,1,0:T(8,128)(2,1)S(1)} collective-permute-done((bf16[4,56,256]{2,1,0:T(8,128)(2,1)S(1)}, bf16[4,56,256]{2,1,0:T(8,128)(2,1)S(1)}, u32[]{:S(2)}, u32[]{:S(2)}) %collective-permute-start.36) | collective-permute-done | bytes 114720 | tf_op jit(solution)/shard_map/cond/branch_1_fun/ppermute | solution.py:406
  56.9 0.7 branch_1_fun.28
  57.6 0.1 collective-permute-start.37
  57.6 1.6 %collective-permute-start.38 = (bf16[128,256]{1,0:T(8,128)(2,1)S(1)}, bf16[128,256]{1,0:T(8,128)(2,1)S(1)}, u32[]{:S(2)}, u32[]{:S(2)}) collective-permute-start(bf16[128,256]{1,0:T(8,128)(2,1)S(1)} %get-tuple-element.137), channel_id=1, source_target_pairs={{0,28},{1,29},{2,30},{3,31},{4,8},{5,9},{6,10},{7,11},{8,4},{9,5},... | collective-permute-start | bytes 196616 | tf_op jit(solution)/shard_map/cond/branch_1_fun/ppermute | solution.py:406
  59.3 0.1 collective-permute-start.39
  59.4 1.8 %branch_1_fun.31 = bf16[1,1536,256]{2,1,0:T(8,128)(2,1)} custom-call(bf16[1536,224]{1,0:T(8,128)(2,1)S(1)} %get-tuple-element.140.refs_0_, bf16[1536,224]{1,0:T(8,128)(2,1)S(1)} %get-tuple-element.141.refs_1_, bf16[224,256]{1,0:T(8,128)(2,1)S(1)} %get-tuple-element.142.refs_2_, bf16[224,256]{1,0:T(8,128)(2,1)S(1)} %get-tuple-element.143.refs_3_, ...), custom_call_target="tpu_custom_call" | custom-call | flops 704643072 | bytes 1048576 | tf_op jit(solution)/shard_map/cond/branch_1_fun/pallas_call | solution.py:388
  61.2 0.0 collective-permute-done.37.near_ref
  61.2 2.0 %collective-permute-done.38.far_ref = bf16[128,256]{1,0:T(8,128)(2,1)S(1)} collective-permute-done((bf16[128,256]{1,0:T(8,128)(2,1)S(1)}, bf16[128,256]{1,0:T(8,128)(2,1)S(1)}, u32[]{:S(2)}, u32[]{:S(2)}) %collective-permute-start.38) | collective-permute-done | bytes 65568 | tf_op jit(solution)/shard_map/cond/branch_1_fun/ppermute | solution.py:406
  63.2 2.1 %collective-permute-done.39.cross_ref = bf16[128,256]{1,0:T(8,128)(2,1)S(1)} collective-permute-done((bf16[128,256]{1,0:T(8,128)(2,1)S(1)}, bf16[128,256]{1,0:T(8,128)(2,1)S(1)}, u32[]{:S(2)}, u32[]{:S(2)}) %collective-permute-start.39) | collective-permute-done | bytes 65568 | tf_op jit(solution)/shard_map/cond/branch_1_fun/ppermute | solution.py:406
  65.3 0.7 branch_1_fun.29
  (1 shorter events, 0.0 us)
Async XLA Ops:
  0.6 8.1 %collective-permute-start.40 = (bf16[2,56,256]{2,1,0:T(8,128)(2,1)}, bf16[2,56,256]{2,1,0:T(8,128)(2,1)S(1)}, u32[]{:S(2)}, u32[]{:S(2)}) collective-permute-start(bf16[2,56,256]{2,1,0:T(8,128)(2,1)} %param.8), channel_id=1, source_target_pairs={{0,4},{1,5},{2,6},{3,7},{4,0},{5,1},{6,2},{7,3},{8,12},{9,13},{10,... | collective-permute-start | bytes 172040 | tf_op jit(solution)/shard_map/ppermute | solution.py:406
  1.2 7.6 %collective-permute-start.41 = (bf16[2,56,256]{2,1,0:T(8,128)(2,1)}, bf16[2,56,256]{2,1,0:T(8,128)(2,1)S(1)}, u32[]{:S(2)}, u32[]{:S(2)}) collective-permute-start(bf16[2,56,256]{2,1,0:T(8,128)(2,1)} %param.8), channel_id=1, source_target_pairs={{0,28},{1,29},{2,30},{3,31},{4,8},{5,9},{6,10},{7,11},{8,4},{9,5},... | collective-permute-start | bytes 172040 | tf_op jit(solution)/shard_map/ppermute | solution.py:406
  5.9 5.3 %collective-permute-start.42 = (bf16[2,56,256]{2,1,0:T(8,128)(2,1)}, bf16[2,56,256]{2,1,0:T(8,128)(2,1)S(1)}, u32[]{:S(2)}, u32[]{:S(2)}) collective-permute-start(bf16[2,56,256]{2,1,0:T(8,128)(2,1)} %param.8), channel_id=1, source_target_pairs={{0,16},{1,17},{2,18},{3,19},{4,20},{5,21},{6,22},{7,23},{8,24},{9,... | collective-permute-start | bytes 172040 | tf_op jit(solution)/shard_map/ppermute | solution.py:406
  11.2 9.4 %copy-start.1 = (bf16[1,1536,256]{2,1,0:T(8,128)(2,1)S(1)}, bf16[1,1536,256]{2,1,0:T(8,128)(2,1)}, u32[]{:S(2)}) copy-start(bf16[1,1536,256]{2,1,0:T(8,128)(2,1)} %get-tuple-element.160) | copy-start | bytes 2359300 | tf_op jit(solution)/shard_map/cond
  11.8 5.9 %collective-permute-start.23 = (bf16[4,56,256]{2,1,0:T(8,128)(2,1)S(1)}, bf16[4,56,256]{2,1,0:T(8,128)(2,1)S(1)}, u32[]{:S(2)}, u32[]{:S(2)}) collective-permute-start(bf16[4,56,256]{2,1,0:T(8,128)(2,1)S(1)} %branch_1_fun.17.refs_0_), channel_id=1, source_target_pairs={{0,1},{1,0},{2,3},{3,2},{4,5},{5,4},{6,7},{7,6},{8,9},{9,8},{10,11... | collective-permute-start | bytes 344072 | tf_op jit(solution)/shard_map/cond/branch_1_fun/ppermute | solution.py:406
  13.4 5.9 %collective-permute-start.24 = (bf16[4,56,256]{2,1,0:T(8,128)(2,1)S(1)}, bf16[4,56,256]{2,1,0:T(8,128)(2,1)S(1)}, u32[]{:S(2)}, u32[]{:S(2)}) collective-permute-start(bf16[4,56,256]{2,1,0:T(8,128)(2,1)S(1)} %branch_1_fun.17.refs_0_), channel_id=1, source_target_pairs={{0,2},{1,3},{2,0},{3,1},{4,6},{5,7},{6,4},{7,5},{8,10},{9,11},{10,... | collective-permute-start | bytes 344072 | tf_op jit(solution)/shard_map/cond/branch_1_fun/ppermute | solution.py:406
  14.9 5.7 %collective-permute-start.25 = (bf16[4,56,256]{2,1,0:T(8,128)(2,1)S(1)}, bf16[4,56,256]{2,1,0:T(8,128)(2,1)S(1)}, u32[]{:S(2)}, u32[]{:S(2)}) collective-permute-start(bf16[4,56,256]{2,1,0:T(8,128)(2,1)S(1)} %branch_1_fun.17.refs_0_), channel_id=1, source_target_pairs={{0,3},{1,2},{2,1},{3,0},{4,7},{5,6},{6,5},{7,4},{8,11},{9,10},{10,... | collective-permute-start | bytes 344072 | tf_op jit(solution)/shard_map/cond/branch_1_fun/ppermute | solution.py:406
  22.2 8.4 %collective-permute-start.26 = (f32[232,256]{1,0:T(8,128)S(1)}, f32[232,256]{1,0:T(8,128)S(1)}, u32[]{:S(2)}, u32[]{:S(2)}) collective-permute-start(f32[232,256]{1,0:T(8,128)S(1)} %get-tuple-element.110), channel_id=1, source_target_pairs={{0,1},{1,0},{2,3},{3,2},{4,5},{5,4},{6,7},{7,6},{8,9},{9,8},{10,11... | collective-permute-start | bytes 712712 | tf_op jit(solution)/shard_map/cond/branch_1_fun/ppermute | solution.py:406
  24.3 11.0 %collective-permute-start.27 = (f32[232,256]{1,0:T(8,128)S(1)}, f32[232,256]{1,0:T(8,128)S(1)}, u32[]{:S(2)}, u32[]{:S(2)}) collective-permute-start(f32[232,256]{1,0:T(8,128)S(1)} %get-tuple-element.111), channel_id=1, source_target_pairs={{0,2},{1,3},{2,0},{3,1},{4,6},{5,7},{6,4},{7,5},{8,10},{9,11},{10,... | collective-permute-start | bytes 712712 | tf_op jit(solution)/shard_map/cond/branch_1_fun/ppermute | solution.py:406
  26.5 8.9 %collective-permute-start.28 = (f32[232,256]{1,0:T(8,128)S(1)}, f32[232,256]{1,0:T(8,128)S(1)}, u32[]{:S(2)}, u32[]{:S(2)}) collective-permute-start(f32[232,256]{1,0:T(8,128)S(1)} %get-tuple-element.112), channel_id=1, source_target_pairs={{0,3},{1,2},{2,1},{3,0},{4,7},{5,6},{6,5},{7,4},{8,11},{9,10},{10,... | collective-permute-start | bytes 712712 | tf_op jit(solution)/shard_map/cond/branch_1_fun/ppermute | solution.py:406
  36.7 4.9 %collective-permute-start.29 = (bf16[240,256]{1,0:T(8,128)(2,1)S(1)}, bf16[240,256]{1,0:T(8,128)(2,1)S(1)}, u32[]{:S(2)}, u32[]{:S(2)}) collective-permute-start(bf16[240,256]{1,0:T(8,128)(2,1)S(1)} %get-tuple-element.113.d_ref.refs_4_.refs_6_), channel_id=1, source_target_pairs={{0,1},{1,0},{2,3},{3,2},{4,5},{5,4},{6,7},{7,6},{8,9},{9,8},{10,11... | collective-permute-start | bytes 368648 | tf_op jit(solution)/shard_map/cond/branch_1_fun/ppermute | solution.py:406
  38.2 5.9 %collective-permute-start.31 = (bf16[240,256]{1,0:T(8,128)(2,1)S(1)}, bf16[240,256]{1,0:T(8,128)(2,1)S(1)}, u32[]{:S(2)}, u32[]{:S(2)}) collective-permute-start(bf16[240,256]{1,0:T(8,128)(2,1)S(1)} %get-tuple-element.113.d_ref.refs_4_.refs_6_), channel_id=1, source_target_pairs={{0,3},{1,2},{2,1},{3,0},{4,7},{5,6},{6,5},{7,4},{8,11},{9,10},{10,... | collective-permute-start | bytes 368648 | tf_op jit(solution)/shard_map/cond/branch_1_fun/ppermute | solution.py:406
  39.0 6.2 %collective-permute-start.30 = (bf16[240,256]{1,0:T(8,128)(2,1)S(1)}, bf16[240,256]{1,0:T(8,128)(2,1)S(1)}, u32[]{:S(2)}, u32[]{:S(2)}) collective-permute-start(bf16[240,256]{1,0:T(8,128)(2,1)S(1)} %get-tuple-element.113.d_ref.refs_4_.refs_6_), channel_id=1, source_target_pairs={{0,2},{1,3},{2,0},{3,1},{4,6},{5,7},{6,4},{7,5},{8,10},{9,11},{10,... | collective-permute-start | bytes 368648 | tf_op jit(solution)/shard_map/cond/branch_1_fun/ppermute | solution.py:406
  46.3 7.4 %collective-permute-start.32 = (f32[1,128]{1,0:T(1,128)S(1)}, f32[1,128]{1,0:T(1,128)S(1)}, u32[]{:S(2)}, u32[]{:S(2)}) collective-permute-start(f32[1,128]{1,0:T(1,128)S(1)} %get-tuple-element.125), channel_id=1, source_target_pairs={{0,8},{1,9},{2,10},{3,11},{4,12},{5,13},{6,14},{7,15},{8,0},{9,1},... | collective-permute-start | bytes 1544 | tf_op jit(solution)/shard_map/cond/branch_1_fun/ppermute | solution.py:406
  46.4 7.4 %collective-permute-start.33 = (f32[1,128]{1,0:T(1,128)S(1)}, f32[1,128]{1,0:T(1,128)S(1)}, u32[]{:S(2)}, u32[]{:S(2)}) collective-permute-start(f32[1,128]{1,0:T(1,128)S(1)} %get-tuple-element.125), channel_id=1, source_target_pairs={{0,16},{1,17},{2,18},{3,19},{4,20},{5,21},{6,22},{7,23},{8,24},{9,... | collective-permute-start | bytes 1544 | tf_op jit(solution)/shard_map/cond/branch_1_fun/ppermute | solution.py:406
  49.2 4.8 %collective-permute-start.34 = (bf16[4,56,256]{2,1,0:T(8,128)(2,1)S(1)}, bf16[4,56,256]{2,1,0:T(8,128)(2,1)S(1)}, u32[]{:S(2)}, u32[]{:S(2)}) collective-permute-start(bf16[4,56,256]{2,1,0:T(8,128)(2,1)S(1)} %get-tuple-element.127), channel_id=1, source_target_pairs={{0,1},{1,0},{2,3},{3,2},{4,5},{5,4},{6,7},{7,6},{8,9},{9,8},{10,11... | collective-permute-start | bytes 344072 | tf_op jit(solution)/shard_map/cond/branch_1_fun/ppermute | solution.py:406
  50.4 4.8 %collective-permute-start.35 = (bf16[4,56,256]{2,1,0:T(8,128)(2,1)S(1)}, bf16[4,56,256]{2,1,0:T(8,128)(2,1)S(1)}, u32[]{:S(2)}, u32[]{:S(2)}) collective-permute-start(bf16[4,56,256]{2,1,0:T(8,128)(2,1)S(1)} %get-tuple-element.128), channel_id=1, source_target_pairs={{0,2},{1,3},{2,0},{3,1},{4,6},{5,7},{6,4},{7,5},{8,10},{9,11},{10,... | collective-permute-start | bytes 344072 | tf_op jit(solution)/shard_map/cond/branch_1_fun/ppermute | solution.py:406
  51.2 5.7 %collective-permute-start.36 = (bf16[4,56,256]{2,1,0:T(8,128)(2,1)S(1)}, bf16[4,56,256]{2,1,0:T(8,128)(2,1)S(1)}, u32[]{:S(2)}, u32[]{:S(2)}) collective-permute-start(bf16[4,56,256]{2,1,0:T(8,128)(2,1)S(1)} %get-tuple-element.129), channel_id=1, source_target_pairs={{0,3},{1,2},{2,1},{3,0},{4,7},{5,6},{6,5},{7,4},{8,11},{9,10},{10,... | collective-permute-start | bytes 344072 | tf_op jit(solution)/shard_map/cond/branch_1_fun/ppermute | solution.py:406
  57.6 3.6 %collective-permute-start.37 = (bf16[128,256]{1,0:T(8,128)(2,1)S(1)}, bf16[128,256]{1,0:T(8,128)(2,1)S(1)}, u32[]{:S(2)}, u32[]{:S(2)}) collective-permute-start(bf16[128,256]{1,0:T(8,128)(2,1)S(1)} %get-tuple-element.136), channel_id=1, source_target_pairs={{0,4},{1,5},{2,6},{3,7},{4,0},{5,1},{6,2},{7,3},{8,12},{9,13},{10,... | collective-permute-start | bytes 196616 | tf_op jit(solution)/shard_map/cond/branch_1_fun/ppermute | solution.py:406
  57.6 5.6 %collective-permute-start.38 = (bf16[128,256]{1,0:T(8,128)(2,1)S(1)}, bf16[128,256]{1,0:T(8,128)(2,1)S(1)}, u32[]{:S(2)}, u32[]{:S(2)}) collective-permute-start(bf16[128,256]{1,0:T(8,128)(2,1)S(1)} %get-tuple-element.137), channel_id=1, source_target_pairs={{0,28},{1,29},{2,30},{3,31},{4,8},{5,9},{6,10},{7,11},{8,4},{9,5},... | collective-permute-start | bytes 196616 | tf_op jit(solution)/shard_map/cond/branch_1_fun/ppermute | solution.py:406
  59.3 6.0 %collective-permute-start.39 = (bf16[128,256]{1,0:T(8,128)(2,1)S(1)}, bf16[128,256]{1,0:T(8,128)(2,1)S(1)}, u32[]{:S(2)}, u32[]{:S(2)}) collective-permute-start(bf16[128,256]{1,0:T(8,128)(2,1)S(1)} %get-tuple-element.138), channel_id=1, source_target_pairs={{0,16},{1,17},{2,18},{3,19},{4,20},{5,21},{6,22},{7,23},{8,24},{9,... | collective-permute-start | bytes 196616 | tf_op jit(solution)/shard_map/cond/branch_1_fun/ppermute | solution.py:406

commit v2 on v1

--- a/solution.py
+++ b/solution.py
@@ -329,26 +329,17 @@
 
 def frames_kernel(*refs, units):
     ds_refs, q_refs, w_refs, d_refs = [refs[k * units : (k + 1) * units] for k in range(4)]
-    rows = q_refs[0].shape[0]
-    total = None
-    for i in range(units):
-        term = nn(ds_refs[i][...], q_refs[i][...]) + nn(w_refs[i][...], d_refs[i][:rows])
-        total = term if total is None else total + term
-    refs[-1][...] = total
-
-
-def last_frames_kernel(*refs, units):
-    ds_refs, q_refs, w_refs, d_refs = [refs[k * units : (k + 1) * units] for k in range(4)]
-    before_ref, out_ref, held_ref, sems = refs[4 * units :]
-    rows, depth = q_refs[0].shape[0], before_ref.shape[0]
+    out_ref, held_ref, sems = refs[4 * units :]
+    rows, depth = q_refs[0].shape[0], held_ref.shape[0]
     blocks = sems.shape[0]
     size = depth // blocks
     copies = []
     for b in range(blocks):
         at = pl.ds(b * size, size)
-        total = before_ref[at]
+        total = None
         for i in range(units):
-            total = total + nn(ds_refs[i][at], q_refs[i][...]) + nn(w_refs[i][at], d_refs[i][:rows])
+            term = nn(ds_refs[i][at], q_refs[i][...]) + nn(w_refs[i][at], d_refs[i][:rows])
+            total = term if total is None else total + term
         held_ref[at] = total.astype(BF16)
         copies.append(pltpu.make_async_copy(held_ref.at[at], out_ref.at[0, at], sems.at[b]))
         copies[-1].start()
@@ -493,30 +484,6 @@
     dqs = [dqs[0]] + [permute(dqs[j], recs, group, xor[j]) for j in range(1, group)]
     pair = loss + permute(loss, recs, group, lambda r, g: (r ^ 2, g))
     across = loss + permute(loss, recs, group, lambda r, g: (cross_of(r, recs), g))
-    total, half = None, units // 2
-    for n, some in enumerate((keys[:half], keys[half:])):
-        args = [back[k][1] for k in some] + [made[k][3] for k in some]
-        args += [back[k][2] for k in some] + [ds[k] for k in some]
-        if n == 0:
-            total = call(
-                functools.partial(frames_kernel, units=half),
-                shape(frames.shape[1:], F32),
-                [VMEM] * len(args),
-                *args,
-                flops=2 * half * cost,
-            )
-        else:
-            blocks = 3 if depth % 384 == 0 else 1
-            total = call(
-                functools.partial(last_frames_kernel, units=half),
-                pltpu.HBM(frames.shape, BF16),
-                [VMEM] * (len(args) + 1),
-                *args, total,
-                out_specs=pl.BlockSpec(memory_space=pltpu.HBM),
-                scratch=[pltpu.VMEM((depth, width), BF16), pltpu.SemaphoreType.DMA((blocks,))],
-                flops=2 * half * cost,
-            )
-    pair, across, *dqs = lax.optimization_barrier((pair, across, *dqs))
     home = call(
         functools.partial(finish_kernel, n_cand=n_cand),
         [shape((owned * w + EXTRA, width), BF16)] * 3,
@@ -526,6 +493,19 @@
     got = []
     for x, where in zip(home, (near_of, far_of, cross_of)):
         got.append(permute(x, recs, group, lambda r, g: (where(r, recs), g)))
+    args = [back[k][1] for k in keys]
+    args[0], _ = lax.optimization_barrier((args[0], home[0]))
+    args += [made[k][3] for k in keys] + [back[k][2] for k in keys] + [ds[k] for k in keys]
+    blocks = 6 if depth % 768 == 0 else 1
+    total = call(
+        functools.partial(frames_kernel, units=units),
+        pltpu.HBM(frames.shape, BF16),
+        [VMEM] * len(args),
+        *args,
+        out_specs=pl.BlockSpec(memory_space=pltpu.HBM),
+        scratch=[pltpu.VMEM((depth, width), BF16), pltpu.SemaphoreType.DMA((blocks,))],
+        flops=2 * units * cost,
+    )
     texts, loss = call(
         close_kernel,
         [shape((owned, w, width), BF16), shape((1, 128), F32)],

time: 66.1 us -> 67.6 us (1.023)
  starting transfers between devices: 24.3 us -> 27.2 us
  waiting for transfers between devices: 20.1 us -> 18.9 us
    ppermute x20, starting transfers between devices: 24.3 us -> 27.2 us  [permute(): return lax.ppermute(x, AXES, pairs)]
    ppermute x20, waiting for transfers between devices: 20.1 us -> 18.9 us  [permute(): return lax.ppermute(x, AXES, pairs)]
    pallas_call x16 -> x15, Pallas kernels: 17.9 us -> 17.7 us  [call(): pl.pallas_call(kernel, out_shape=out_shape, in_specs=in_specs, out_specs=...]
  transfers between devices with their start and end apart: 20 -> 20, of which waited for: 13 -> 15; matrix products, arithmetic and copies ran while one was open for 1% -> 1% of each run, Pallas kernels for 21% -> 20%
where the time goes in v2:
time: 67.6 us; the launch traced here: 67.4 us
  starting transfers between devices  27.2 us (40%)
  Pallas kernels  19.3 us (29%)
  waiting for transfers between devices  18.9 us (28%)
  between operations  1.3 us (2%)
    ppermute x20, starting transfers between devices, permute(): return lax.ppermute(x, AXES, pairs)  27.2 us
    ppermute x20, waiting for transfers between devices, permute(): return lax.ppermute(x, AXES, pairs)  18.9 us
    pallas_call x15, Pallas kernels, call(): pl.pallas_call(kernel, out_shape=out_shape, in_specs=in_specs, out_specs=...  17.7 us
    pallas_call x1, Pallas kernels, body(): pl.pallas_call(functools.partial(table_kernel, recs=recs, owned=owned), n...  1.61 us
  transfers between devices with their start and end apart: 20, of which 15 were waited for; matrix products, arithmetic and copies ran while one was open for 1% of the time, Pallas kernels for 20%

profile of v2, /device:TPU:0, one launch (start us, length us, event | category | flops | bytes accessed | tf_op | source)
XLA Modules:
  0.0 67.4 jit_solution(11066530687859116375)
XLA Ops:
  0.6 0.6 collective-permute-start.40
  1.2 3.6 %collective-permute-start.42 = (bf16[2,56,256]{2,1,0:T(8,128)(2,1)}, bf16[2,56,256]{2,1,0:T(8,128)(2,1)S(1)}, u32[]{:S(2)}, u32[]{:S(2)}) collective-permute-start(bf16[2,56,256]{2,1,0:T(8,128)(2,1)} %param.8), channel_id=1, source_target_pairs={{0,16},{1,17},{2,18},{3,19},{4,20},{5,21},{6,22},{7,23},{8,24},{9,... | collective-permute-start | bytes 172040 | tf_op jit(solution)/shard_map/ppermute | solution.py:397
  4.8 1.1 %collective-permute-start.41 = (bf16[2,56,256]{2,1,0:T(8,128)(2,1)}, bf16[2,56,256]{2,1,0:T(8,128)(2,1)S(1)}, u32[]{:S(2)}, u32[]{:S(2)}) collective-permute-start(bf16[2,56,256]{2,1,0:T(8,128)(2,1)} %param.8), channel_id=1, source_target_pairs={{0,28},{1,29},{2,30},{3,31},{4,8},{5,9},{6,10},{7,11},{8,4},{9,5},... | collective-permute-start | bytes 172040 | tf_op jit(solution)/shard_map/ppermute | solution.py:397
  5.9 1.6 %table.1 = s32[26]{0:T(128)S(1)} custom-call(s32[16]{0:T(128)} %bitcast.34, s32[16]{0:T(128)} %text_ref.1, s32[16]{0:T(128)} %label_ref.1), custom_call_target="tpu_custom_call" | custom-call | tf_op jit(solution)/shard_map/table/pallas_call | solution.py:528
  7.6 0.6 slice.9
  8.8 0.0 collective-permute-done.40
  8.8 0.1 collective-permute-done.42
  8.9 1.7 %collective-permute-done.41 = bf16[2,56,256]{2,1,0:T(8,128)(2,1)S(1)} collective-permute-done((bf16[2,56,256]{2,1,0:T(8,128)(2,1)}, bf16[2,56,256]{2,1,0:T(8,128)(2,1)S(1)}, u32[]{:S(2)}, u32[]{:S(2)}) %collective-permute-start.41) | collective-permute-done | bytes 57376 | tf_op jit(solution)/shard_map/ppermute | solution.py:397
  10.6 56.8 %conditional.1 = (bf16[2,56,256]{2,1,0:T(8,128)(2,1)}, f32[]{:T(128)}, bf16[1,1536,256]{2,1,0:T(8,128)(2,1)}) conditional(s32[]{:T(128)} %bitcast.5, (bf16[1,1536,256]{2,1,0:T(8,128)(2,1)}, s32[26]{0:T(128)S(1)}, bf16[2,56,256]{2,1,0:T(8,128)(2,1)S(1)}, bf16[2,56,256]{2,1,0:T(8,128)(2,1)S(1)}, bf16[2,56,256]{2,1,0:T(8,128)(2,1)S(1)}) %tuple.17, ...), branch_computations={%region_0.0_spmd, %region_1.0_spmd} | conditional | flops 8631877632 | bytes 41885132 | solution.py:541
  10.6 0.0 copy-start.1
  10.6 0.6 branch_1_fun.16.refs_0_
  11.2 2.5 %collective-permute-start.25 = (bf16[4,56,256]{2,1,0:T(8,128)(2,1)S(1)}, bf16[4,56,256]{2,1,0:T(8,128)(2,1)S(1)}, u32[]{:S(2)}, u32[]{:S(2)}) collective-permute-start(bf16[4,56,256]{2,1,0:T(8,128)(2,1)S(1)} %branch_1_fun.16.refs_0_), channel_id=1, source_target_pairs={{0,3},{1,2},{2,1},{3,0},{4,7},{5,6},{6,5},{7,4},{8,11},{9,10},{10,... | collective-permute-start | bytes 344072 | tf_op jit(solution)/shard_map/cond/branch_1_fun/ppermute | solution.py:397
  13.7 0.5 collective-permute-start.24
  14.2 0.5 collective-permute-start.23
  14.7 1.5 %branch_1_fun.15.ft_ref = bf16[256,1536]{1,0:T(8,128)(2,1)S(1)} custom-call(bf16[1536,256]{1,0:T(8,128)(2,1)} %bitcast.25), custom_call_target="tpu_custom_call" | custom-call | flops 176160768 | bytes 1048576 | tf_op jit(solution)/shard_map/cond/branch_1_fun/pallas_call | solution.py:379
  16.3 1.3 %collective-permute-done.25.refs_3_ = bf16[4,56,256]{2,1,0:T(8,128)(2,1)S(1)} collective-permute-done((bf16[4,56,256]{2,1,0:T(8,128)(2,1)S(1)}, bf16[4,56,256]{2,1,0:T(8,128)(2,1)S(1)}, u32[]{:S(2)}, u32[]{:S(2)}) %collective-permute-start.25) | collective-permute-done | bytes 114720 | tf_op jit(solution)/shard_map/cond/branch_1_fun/ppermute | solution.py:397
  17.6 1.2 %collective-permute-done.24.refs_2_ = bf16[4,56,256]{2,1,0:T(8,128)(2,1)S(1)} collective-permute-done((bf16[4,56,256]{2,1,0:T(8,128)(2,1)S(1)}, bf16[4,56,256]{2,1,0:T(8,128)(2,1)S(1)}, u32[]{:S(2)}, u32[]{:S(2)}) %collective-permute-start.24) | collective-permute-done | bytes 114720 | tf_op jit(solution)/shard_map/cond/branch_1_fun/ppermute | solution.py:397
  18.8 0.2 collective-permute-done.23.refs_1_
  19.0 0.0 copy-done.1
  19.0 1.6 %branch_1_fun.20 = (f32[232,256]{1,0:T(8,128)S(1)}, f32[1536,224]{1,0:T(8,128)S(1)}, f32[1,224]{1,0:T(1,128)S(1)}, bf16[224,256]{1,0:T(8,128)(2,1)S(1)}) custom-call(bf16[1536,256]{1,0:T(8,128)(2,1)S(1)} %bitcast.26, bf16[256,1536]{1,0:T(8,128)(2,1)S(1)} %branch_1_fun.15.ft_ref, bf16[4,56,256]{2,1,0:T(8,128)(2,1)S(1)} %branch_1_fun.16.refs_0_, ...), custom_call_target="tpu_custom_call" | custom-call | flops 352321536 | bytes 1048576 | tf_op jit(solution)/shard_map/cond/branch_1_fun/pallas_call | solution.py:379
  20.6 1.5 %collective-permute-start.28 = (f32[232,256]{1,0:T(8,128)S(1)}, f32[232,256]{1,0:T(8,128)S(1)}, u32[]{:S(2)}, u32[]{:S(2)}) collective-permute-start(f32[232,256]{1,0:T(8,128)S(1)} %get-tuple-element.107), channel_id=1, source_target_pairs={{0,3},{1,2},{2,1},{3,0},{4,7},{5,6},{6,5},{7,4},{8,11},{9,10},{10,... | collective-permute-start | bytes 712712 | tf_op jit(solution)/shard_map/cond/branch_1_fun/ppermute | solution.py:397
  22.2 1.6 %branch_1_fun.19 = (f32[232,256]{1,0:T(8,128)S(1)}, f32[1536,224]{1,0:T(8,128)S(1)}, f32[1,224]{1,0:T(1,128)S(1)}, bf16[224,256]{1,0:T(8,128)(2,1)S(1)}) custom-call(bf16[1536,256]{1,0:T(8,128)(2,1)S(1)} %bitcast.27, bf16[256,1536]{1,0:T(8,128)(2,1)S(1)} %branch_1_fun.15.ft_ref, bf16[4,56,256]{2,1,0:T(8,128)(2,1)S(1)} %branch_1_fun.16.refs_0_, ...), custom_call_target="tpu_custom_call" | custom-call | flops 352321536 | bytes 1048576 | tf_op jit(solution)/shard_map/cond/branch_1_fun/pallas_call | solution.py:379
  23.7 1.3 %collective-permute-start.27 = (f32[232,256]{1,0:T(8,128)S(1)}, f32[232,256]{1,0:T(8,128)S(1)}, u32[]{:S(2)}, u32[]{:S(2)}) collective-permute-start(f32[232,256]{1,0:T(8,128)S(1)} %get-tuple-element.106), channel_id=1, source_target_pairs={{0,2},{1,3},{2,0},{3,1},{4,6},{5,7},{6,4},{7,5},{8,10},{9,11},{10,... | collective-permute-start | bytes 712712 | tf_op jit(solution)/shard_map/cond/branch_1_fun/ppermute | solution.py:397
  25.1 1.6 %branch_1_fun.18 = (f32[232,256]{1,0:T(8,128)S(1)}, f32[1536,224]{1,0:T(8,128)S(1)}, f32[1,224]{1,0:T(1,128)S(1)}, bf16[224,256]{1,0:T(8,128)(2,1)S(1)}) custom-call(bf16[1536,256]{1,0:T(8,128)(2,1)S(1)} %bitcast.28, bf16[256,1536]{1,0:T(8,128)(2,1)S(1)} %branch_1_fun.15.ft_ref, bf16[4,56,256]{2,1,0:T(8,128)(2,1)S(1)} %branch_1_fun.16.refs_0_, ...), custom_call_target="tpu_custom_call" | custom-call | flops 352321536 | bytes 1048576 | tf_op jit(solution)/shard_map/cond/branch_1_fun/pallas_call | solution.py:379
  26.6 0.8 %collective-permute-start.26 = (f32[232,256]{1,0:T(8,128)S(1)}, f32[232,256]{1,0:T(8,128)S(1)}, u32[]{:S(2)}, u32[]{:S(2)}) collective-permute-start(f32[232,256]{1,0:T(8,128)S(1)} %get-tuple-element.105), channel_id=1, source_target_pairs={{0,1},{1,0},{2,3},{3,2},{4,5},{5,4},{6,7},{7,6},{8,9},{9,8},{10,11... | collective-permute-start | bytes 712712 | tf_op jit(solution)/shard_map/cond/branch_1_fun/ppermute | solution.py:397
  27.4 1.6 %branch_1_fun.17 = (f32[232,256]{1,0:T(8,128)S(1)}, f32[1536,224]{1,0:T(8,128)S(1)}, f32[1,224]{1,0:T(1,128)S(1)}, bf16[224,256]{1,0:T(8,128)(2,1)S(1)}) custom-call(bf16[1536,256]{1,0:T(8,128)(2,1)S(1)} %bitcast.29, bf16[256,1536]{1,0:T(8,128)(2,1)S(1)} %branch_1_fun.15.ft_ref, bf16[4,56,256]{2,1,0:T(8,128)(2,1)S(1)} %branch_1_fun.16.refs_0_, ...), custom_call_target="tpu_custom_call" | custom-call | flops 352321536 | bytes 1048576 | tf_op jit(solution)/shard_map/cond/branch_1_fun/pallas_call | solution.py:379
  29.0 0.0 collective-permute-done.28.refs_3_
  29.0 4.2 %collective-permute-done.27.refs_2_ = f32[232,256]{1,0:T(8,128)S(1)} collective-permute-done((f32[232,256]{1,0:T(8,128)S(1)}, f32[232,256]{1,0:T(8,128)S(1)}, u32[]{:S(2)}, u32[]{:S(2)}) %collective-permute-start.27) | collective-permute-done | bytes 237600 | tf_op jit(solution)/shard_map/cond/branch_1_fun/ppermute | solution.py:397
  33.2 0.2 collective-permute-done.26.refs_1_
  33.4 1.4 %branch_1_fun.21 = (bf16[240,256]{1,0:T(8,128)(2,1)S(1)}, f32[224,256]{1,0:T(8,128)S(1)}) custom-call(s32[26]{0:T(128)S(1)} %get-tuple-element.97.table_ref, bf16[224,256]{1,0:T(8,128)(2,1)S(1)} %get-tuple-element.103.q_ref.refs_4_, f32[232,256]{1,0:T(8,128)S(1)} %get-tuple-element.104.refs_0_, f32[232,256]{1,0:T(8,128)S(1)} %collective-permute-done.26.refs_1_, ...), custom_call_target="tpu_custom_call" | custom-call | bytes 1048576 | tf_op jit(solution)/shard_map/cond/branch_1_fun/pallas_call | solution.py:379
  34.8 1.1 %collective-permute-start.29 = (bf16[240,256]{1,0:T(8,128)(2,1)S(1)}, bf16[240,256]{1,0:T(8,128)(2,1)S(1)}, u32[]{:S(2)}, u32[]{:S(2)}) collective-permute-start(bf16[240,256]{1,0:T(8,128)(2,1)S(1)} %get-tuple-element.108.d_ref.refs_4_.refs_12_), channel_id=1, source_target_pairs={{0,1},{1,0},{2,3},{3,2},{4,5},{5,4},{6,7},{7,6},{8,9},{9,8},{10,11... | collective-permute-start | bytes 368648 | tf_op jit(solution)/shard_map/cond/branch_1_fun/ppermute | solution.py:397
  35.9 0.6 collective-permute-start.30
  36.5 1.9 %collective-permute-start.31 = (bf16[240,256]{1,0:T(8,128)(2,1)S(1)}, bf16[240,256]{1,0:T(8,128)(2,1)S(1)}, u32[]{:S(2)}, u32[]{:S(2)}) collective-permute-start(bf16[240,256]{1,0:T(8,128)(2,1)S(1)} %get-tuple-element.108.d_ref.refs_4_.refs_12_), channel_id=1, source_target_pairs={{0,3},{1,2},{2,1},{3,0},{4,7},{5,6},{6,5},{7,4},{8,11},{9,10},{10,... | collective-permute-start | bytes 368648 | tf_op jit(solution)/shard_map/cond/branch_1_fun/ppermute | solution.py:397
  38.4 1.0 %branch_1_fun.22 = (f32[4,56,256]{2,1,0:T(8,128)S(1)}, bf16[1536,224]{1,0:T(8,128)(2,1)S(1)}, bf16[1536,224]{1,0:T(8,128)(2,1)S(1)}) custom-call(bf16[1536,256]{1,0:T(8,128)(2,1)S(1)} %bitcast.30, bf16[256,1536]{1,0:T(8,128)(2,1)S(1)} %branch_1_fun.15.ft_ref, f32[1536,224]{1,0:T(8,128)S(1)} %get-tuple-element.101.weights_ref, ...), custom_call_target="tpu_custom_call" | custom-call | flops 352321536 | bytes 1048576 | tf_op jit(solution)/shard_map/cond/branch_1_fun/pallas_call | solution.py:379
  39.4 1.0 %collective-permute-done.29.d_ref.refs_5_.refs_13_ = bf16[240,256]{1,0:T(8,128)(2,1)S(1)} collective-permute-done((bf16[240,256]{1,0:T(8,128)(2,1)S(1)}, bf16[240,256]{1,0:T(8,128)(2,1)S(1)}, u32[]{:S(2)}, u32[]{:S(2)}) %collective-permute-start.29) | collective-permute-done | bytes 122912 | tf_op jit(solution)/shard_map/cond/branch_1_fun/ppermute | solution.py:397
  40.4 1.0 %branch_1_fun.23 = (f32[4,56,256]{2,1,0:T(8,128)S(1)}, bf16[1536,224]{1,0:T(8,128)(2,1)S(1)}, bf16[1536,224]{1,0:T(8,128)(2,1)S(1)}) custom-call(bf16[1536,256]{1,0:T(8,128)(2,1)S(1)} %bitcast.31, bf16[256,1536]{1,0:T(8,128)(2,1)S(1)} %branch_1_fun.15.ft_ref, f32[1536,224]{1,0:T(8,128)S(1)} %get-tuple-element.111.weights_ref, ...), custom_call_target="tpu_custom_call" | custom-call | flops 352321536 | bytes 1048576 | tf_op jit(solution)/shard_map/cond/branch_1_fun/pallas_call | solution.py:379
  41.4 0.3 collective-permute-done.30.d_ref.refs_6_.refs_14_
  41.7 1.0 %branch_1_fun.24 = (f32[4,56,256]{2,1,0:T(8,128)S(1)}, bf16[1536,224]{1,0:T(8,128)(2,1)S(1)}, bf16[1536,224]{1,0:T(8,128)(2,1)S(1)}) custom-call(bf16[1536,256]{1,0:T(8,128)(2,1)S(1)} %bitcast.32, bf16[256,1536]{1,0:T(8,128)(2,1)S(1)} %branch_1_fun.15.ft_ref, f32[1536,224]{1,0:T(8,128)S(1)} %get-tuple-element.114.weights_ref, ...), custom_call_target="tpu_custom_call" | custom-call | flops 352321536 | bytes 1048576 | tf_op jit(solution)/shard_map/cond/branch_1_fun/pallas_call | solution.py:379
  42.7 0.9 %collective-permute-done.31.d_ref.refs_7_.refs_15_ = bf16[240,256]{1,0:T(8,128)(2,1)S(1)} collective-permute-done((bf16[240,256]{1,0:T(8,128)(2,1)S(1)}, bf16[240,256]{1,0:T(8,128)(2,1)S(1)}, u32[]{:S(2)}, u32[]{:S(2)}) %collective-permute-start.31) | collective-permute-done | bytes 122912 | tf_op jit(solution)/shard_map/cond/branch_1_fun/ppermute | solution.py:397
  43.6 1.0 %branch_1_fun.25 = (f32[4,56,256]{2,1,0:T(8,128)S(1)}, bf16[1536,224]{1,0:T(8,128)(2,1)S(1)}, bf16[1536,224]{1,0:T(8,128)(2,1)S(1)}) custom-call(bf16[1536,256]{1,0:T(8,128)(2,1)S(1)} %bitcast.33, bf16[256,1536]{1,0:T(8,128)(2,1)S(1)} %branch_1_fun.15.ft_ref, f32[1536,224]{1,0:T(8,128)S(1)} %get-tuple-element.117.weights_ref, ...), custom_call_target="tpu_custom_call" | custom-call | flops 352321536 | bytes 1048576 | tf_op jit(solution)/shard_map/cond/branch_1_fun/pallas_call | solution.py:379
  44.6 0.1 branch_1_fun.26
  44.7 1.0 %collective-permute-start.33 = (f32[1,128]{1,0:T(1,128)S(1)}, f32[1,128]{1,0:T(1,128)S(1)}, u32[]{:S(2)}, u32[]{:S(2)}) collective-permute-start(f32[1,128]{1,0:T(1,128)S(1)} %get-tuple-element.120), channel_id=1, source_target_pairs={{0,16},{1,17},{2,18},{3,19},{4,20},{5,21},{6,22},{7,23},{8,24},{9,... | collective-permute-start | bytes 1544 | tf_op jit(solution)/shard_map/cond/branch_1_fun/ppermute | solution.py:397
  45.7 5.0 %collective-permute-start.32 = (f32[1,128]{1,0:T(1,128)S(1)}, f32[1,128]{1,0:T(1,128)S(1)}, u32[]{:S(2)}, u32[]{:S(2)}) collective-permute-start(f32[1,128]{1,0:T(1,128)S(1)} %get-tuple-element.120), channel_id=1, source_target_pairs={{0,8},{1,9},{2,10},{3,11},{4,12},{5,13},{6,14},{7,15},{8,0},{9,1},... | collective-permute-start | bytes 1544 | tf_op jit(solution)/shard_map/cond/branch_1_fun/ppermute | solution.py:397
  50.7 0.6 collective-permute-start.34
  51.2 1.5 %collective-permute-start.35 = (bf16[4,56,256]{2,1,0:T(8,128)(2,1)S(1)}, bf16[4,56,256]{2,1,0:T(8,128)(2,1)S(1)}, u32[]{:S(2)}, u32[]{:S(2)}) collective-permute-start(bf16[4,56,256]{2,1,0:T(8,128)(2,1)S(1)} %get-tuple-element.123), channel_id=1, source_target_pairs={{0,2},{1,3},{2,0},{3,1},{4,6},{5,7},{6,4},{7,5},{8,10},{9,11},{10,... | collective-permute-start | bytes 344072 | tf_op jit(solution)/shard_map/cond/branch_1_fun/ppermute | solution.py:397
  52.7 1.4 %collective-permute-start.36 = (bf16[4,56,256]{2,1,0:T(8,128)(2,1)S(1)}, bf16[4,56,256]{2,1,0:T(8,128)(2,1)S(1)}, u32[]{:S(2)}, u32[]{:S(2)}) collective-permute-start(bf16[4,56,256]{2,1,0:T(8,128)(2,1)S(1)} %get-tuple-element.124), channel_id=1, source_target_pairs={{0,3},{1,2},{2,1},{3,0},{4,7},{5,6},{6,5},{7,4},{8,11},{9,10},{10,... | collective-permute-start | bytes 344072 | tf_op jit(solution)/shard_map/cond/branch_1_fun/ppermute | solution.py:397
  54.2 0.0 collective-permute-done.33
  54.2 0.0 collective-permute-done.32
  54.2 1.3 %collective-permute-done.34.refs_1_ = bf16[4,56,256]{2,1,0:T(8,128)(2,1)S(1)} collective-permute-done((bf16[4,56,256]{2,1,0:T(8,128)(2,1)S(1)}, bf16[4,56,256]{2,1,0:T(8,128)(2,1)S(1)}, u32[]{:S(2)}, u32[]{:S(2)}) %collective-permute-start.34) | collective-permute-done | bytes 114720 | tf_op jit(solution)/shard_map/cond/branch_1_fun/ppermute | solution.py:397
  55.5 0.6 collective-permute-done.35.refs_2_
  56.0 2.4 %collective-permute-done.36.refs_3_ = bf16[4,56,256]{2,1,0:T(8,128)(2,1)S(1)} collective-permute-done((bf16[4,56,256]{2,1,0:T(8,128)(2,1)S(1)}, bf16[4,56,256]{2,1,0:T(8,128)(2,1)S(1)}, u32[]{:S(2)}, u32[]{:S(2)}) %collective-permute-start.36) | collective-permute-done | bytes 114720 | tf_op jit(solution)/shard_map/cond/branch_1_fun/ppermute | solution.py:397
  58.4 0.7 branch_1_fun.27
  59.1 0.1 collective-permute-start.37
  59.2 0.1 collective-permute-start.38
  59.3 1.5 %collective-permute-start.39 = (bf16[128,256]{1,0:T(8,128)(2,1)S(1)}, bf16[128,256]{1,0:T(8,128)(2,1)S(1)}, u32[]{:S(2)}, u32[]{:S(2)}) collective-permute-start(bf16[128,256]{1,0:T(8,128)(2,1)S(1)} %get-tuple-element.127), channel_id=1, source_target_pairs={{0,16},{1,17},{2,18},{3,19},{4,20},{5,21},{6,22},{7,23},{8,24},{9,... | collective-permute-start | bytes 196616 | tf_op jit(solution)/shard_map/cond/branch_1_fun/ppermute | solution.py:397
  60.8 2.6 %branch_1_fun.29 = bf16[1,1536,256]{2,1,0:T(8,128)(2,1)} custom-call(bf16[1536,224]{1,0:T(8,128)(2,1)S(1)} %get-tuple-element.130.refs_0_, bf16[1536,224]{1,0:T(8,128)(2,1)S(1)} %get-tuple-element.131.refs_1_, bf16[1536,224]{1,0:T(8,128)(2,1)S(1)} %get-tuple-element.132.refs_2_, bf16[1536,224]{1,0:T(8,128)(2,1)S(1)} %get-tuple-element.133.refs_3_, ...), custom_call_target="tpu_custom_call" | custom-call | flops 1409286144 | bytes 1048576 | tf_op jit(solution)/shard_map/cond/branch_1_fun/pallas_call | solution.py:379
  63.3 1.6 %collective-permute-done.38.far_ref = bf16[128,256]{1,0:T(8,128)(2,1)S(1)} collective-permute-done((bf16[128,256]{1,0:T(8,128)(2,1)S(1)}, bf16[128,256]{1,0:T(8,128)(2,1)S(1)}, u32[]{:S(2)}, u32[]{:S(2)}) %collective-permute-start.38) | collective-permute-done | bytes 65568 | tf_op jit(solution)/shard_map/cond/branch_1_fun/ppermute | solution.py:397
  64.9 1.8 %collective-permute-done.39.cross_ref = bf16[128,256]{1,0:T(8,128)(2,1)S(1)} collective-permute-done((bf16[128,256]{1,0:T(8,128)(2,1)S(1)}, bf16[128,256]{1,0:T(8,128)(2,1)S(1)}, u32[]{:S(2)}, u32[]{:S(2)}) %collective-permute-start.39) | collective-permute-done | bytes 65568 | tf_op jit(solution)/shard_map/cond/branch_1_fun/ppermute | solution.py:397
  66.7 0.0 collective-permute-done.37.near_ref
  66.7 0.7 branch_1_fun.28
  (1 shorter events, 0.0 us)
Async XLA Ops:
  0.6 8.2 %collective-permute-start.40 = (bf16[2,56,256]{2,1,0:T(8,128)(2,1)}, bf16[2,56,256]{2,1,0:T(8,128)(2,1)S(1)}, u32[]{:S(2)}, u32[]{:S(2)}) collective-permute-start(bf16[2,56,256]{2,1,0:T(8,128)(2,1)} %param.8), channel_id=1, source_target_pairs={{0,4},{1,5},{2,6},{3,7},{4,0},{5,1},{6,2},{7,3},{8,12},{9,13},{10,... | collective-permute-start | bytes 172040 | tf_op jit(solution)/shard_map/ppermute | solution.py:397
  1.2 7.7 %collective-permute-start.42 = (bf16[2,56,256]{2,1,0:T(8,128)(2,1)}, bf16[2,56,256]{2,1,0:T(8,128)(2,1)S(1)}, u32[]{:S(2)}, u32[]{:S(2)}) collective-permute-start(bf16[2,56,256]{2,1,0:T(8,128)(2,1)} %param.8), channel_id=1, source_target_pairs={{0,16},{1,17},{2,18},{3,19},{4,20},{5,21},{6,22},{7,23},{8,24},{9,... | collective-permute-start | bytes 172040 | tf_op jit(solution)/shard_map/ppermute | solution.py:397
  4.8 5.7 %collective-permute-start.41 = (bf16[2,56,256]{2,1,0:T(8,128)(2,1)}, bf16[2,56,256]{2,1,0:T(8,128)(2,1)S(1)}, u32[]{:S(2)}, u32[]{:S(2)}) collective-permute-start(bf16[2,56,256]{2,1,0:T(8,128)(2,1)} %param.8), channel_id=1, source_target_pairs={{0,28},{1,29},{2,30},{3,31},{4,8},{5,9},{6,10},{7,11},{8,4},{9,5},... | collective-permute-start | bytes 172040 | tf_op jit(solution)/shard_map/ppermute | solution.py:397
  10.6 8.5 %copy-start.1 = (bf16[1,1536,256]{2,1,0:T(8,128)(2,1)S(1)}, bf16[1,1536,256]{2,1,0:T(8,128)(2,1)}, u32[]{:S(2)}) copy-start(bf16[1,1536,256]{2,1,0:T(8,128)(2,1)} %get-tuple-element.150) | copy-start | bytes 2359300 | tf_op jit(solution)/shard_map/cond
  11.2 6.4 %collective-permute-start.25 = (bf16[4,56,256]{2,1,0:T(8,128)(2,1)S(1)}, bf16[4,56,256]{2,1,0:T(8,128)(2,1)S(1)}, u32[]{:S(2)}, u32[]{:S(2)}) collective-permute-start(bf16[4,56,256]{2,1,0:T(8,128)(2,1)S(1)} %branch_1_fun.16.refs_0_), channel_id=1, source_target_pairs={{0,3},{1,2},{2,1},{3,0},{4,7},{5,6},{6,5},{7,4},{8,11},{9,10},{10,... | collective-permute-start | bytes 344072 | tf_op jit(solution)/shard_map/cond/branch_1_fun/ppermute | solution.py:397
  13.7 5.1 %collective-permute-start.24 = (bf16[4,56,256]{2,1,0:T(8,128)(2,1)S(1)}, bf16[4,56,256]{2,1,0:T(8,128)(2,1)S(1)}, u32[]{:S(2)}, u32[]{:S(2)}) collective-permute-start(bf16[4,56,256]{2,1,0:T(8,128)(2,1)S(1)} %branch_1_fun.16.refs_0_), channel_id=1, source_target_pairs={{0,2},{1,3},{2,0},{3,1},{4,6},{5,7},{6,4},{7,5},{8,10},{9,11},{10,... | collective-permute-start | bytes 344072 | tf_op jit(solution)/shard_map/cond/branch_1_fun/ppermute | solution.py:397
  14.2 4.8 %collective-permute-start.23 = (bf16[4,56,256]{2,1,0:T(8,128)(2,1)S(1)}, bf16[4,56,256]{2,1,0:T(8,128)(2,1)S(1)}, u32[]{:S(2)}, u32[]{:S(2)}) collective-permute-start(bf16[4,56,256]{2,1,0:T(8,128)(2,1)S(1)} %branch_1_fun.16.refs_0_), channel_id=1, source_target_pairs={{0,1},{1,0},{2,3},{3,2},{4,5},{5,4},{6,7},{7,6},{8,9},{9,8},{10,11... | collective-permute-start | bytes 344072 | tf_op jit(solution)/shard_map/cond/branch_1_fun/ppermute | solution.py:397
  20.6 8.4 %collective-permute-start.28 = (f32[232,256]{1,0:T(8,128)S(1)}, f32[232,256]{1,0:T(8,128)S(1)}, u32[]{:S(2)}, u32[]{:S(2)}) collective-permute-start(f32[232,256]{1,0:T(8,128)S(1)} %get-tuple-element.107), channel_id=1, source_target_pairs={{0,3},{1,2},{2,1},{3,0},{4,7},{5,6},{6,5},{7,4},{8,11},{9,10},{10,... | collective-permute-start | bytes 712712 | tf_op jit(solution)/shard_map/cond/branch_1_fun/ppermute | solution.py:397
  23.7 9.4 %collective-permute-start.27 = (f32[232,256]{1,0:T(8,128)S(1)}, f32[232,256]{1,0:T(8,128)S(1)}, u32[]{:S(2)}, u32[]{:S(2)}) collective-permute-start(f32[232,256]{1,0:T(8,128)S(1)} %get-tuple-element.106), channel_id=1, source_target_pairs={{0,2},{1,3},{2,0},{3,1},{4,6},{5,7},{6,4},{7,5},{8,10},{9,11},{10,... | collective-permute-start | bytes 712712 | tf_op jit(solution)/shard_map/cond/branch_1_fun/ppermute | solution.py:397
  26.6 6.7 %collective-permute-start.26 = (f32[232,256]{1,0:T(8,128)S(1)}, f32[232,256]{1,0:T(8,128)S(1)}, u32[]{:S(2)}, u32[]{:S(2)}) collective-permute-start(f32[232,256]{1,0:T(8,128)S(1)} %get-tuple-element.105), channel_id=1, source_target_pairs={{0,1},{1,0},{2,3},{3,2},{4,5},{5,4},{6,7},{7,6},{8,9},{9,8},{10,11... | collective-permute-start | bytes 712712 | tf_op jit(solution)/shard_map/cond/branch_1_fun/ppermute | solution.py:397
  34.8 5.6 %collective-permute-start.29 = (bf16[240,256]{1,0:T(8,128)(2,1)S(1)}, bf16[240,256]{1,0:T(8,128)(2,1)S(1)}, u32[]{:S(2)}, u32[]{:S(2)}) collective-permute-start(bf16[240,256]{1,0:T(8,128)(2,1)S(1)} %get-tuple-element.108.d_ref.refs_4_.refs_12_), channel_id=1, source_target_pairs={{0,1},{1,0},{2,3},{3,2},{4,5},{5,4},{6,7},{7,6},{8,9},{9,8},{10,11... | collective-permute-start | bytes 368648 | tf_op jit(solution)/shard_map/cond/branch_1_fun/ppermute | solution.py:397
  35.9 5.8 %collective-permute-start.30 = (bf16[240,256]{1,0:T(8,128)(2,1)S(1)}, bf16[240,256]{1,0:T(8,128)(2,1)S(1)}, u32[]{:S(2)}, u32[]{:S(2)}) collective-permute-start(bf16[240,256]{1,0:T(8,128)(2,1)S(1)} %get-tuple-element.108.d_ref.refs_4_.refs_12_), channel_id=1, source_target_pairs={{0,2},{1,3},{2,0},{3,1},{4,6},{5,7},{6,4},{7,5},{8,10},{9,11},{10,... | collective-permute-start | bytes 368648 | tf_op jit(solution)/shard_map/cond/branch_1_fun/ppermute | solution.py:397
  36.5 7.1 %collective-permute-start.31 = (bf16[240,256]{1,0:T(8,128)(2,1)S(1)}, bf16[240,256]{1,0:T(8,128)(2,1)S(1)}, u32[]{:S(2)}, u32[]{:S(2)}) collective-permute-start(bf16[240,256]{1,0:T(8,128)(2,1)S(1)} %get-tuple-element.108.d_ref.refs_4_.refs_12_), channel_id=1, source_target_pairs={{0,3},{1,2},{2,1},{3,0},{4,7},{5,6},{6,5},{7,4},{8,11},{9,10},{10,... | collective-permute-start | bytes 368648 | tf_op jit(solution)/shard_map/cond/branch_1_fun/ppermute | solution.py:397
  44.7 9.5 %collective-permute-start.33 = (f32[1,128]{1,0:T(1,128)S(1)}, f32[1,128]{1,0:T(1,128)S(1)}, u32[]{:S(2)}, u32[]{:S(2)}) collective-permute-start(f32[1,128]{1,0:T(1,128)S(1)} %get-tuple-element.120), channel_id=1, source_target_pairs={{0,16},{1,17},{2,18},{3,19},{4,20},{5,21},{6,22},{7,23},{8,24},{9,... | collective-permute-start | bytes 1544 | tf_op jit(solution)/shard_map/cond/branch_1_fun/ppermute | solution.py:397
  45.7 8.5 %collective-permute-start.32 = (f32[1,128]{1,0:T(1,128)S(1)}, f32[1,128]{1,0:T(1,128)S(1)}, u32[]{:S(2)}, u32[]{:S(2)}) collective-permute-start(f32[1,128]{1,0:T(1,128)S(1)} %get-tuple-element.120), channel_id=1, source_target_pairs={{0,8},{1,9},{2,10},{3,11},{4,12},{5,13},{6,14},{7,15},{8,0},{9,1},... | collective-permute-start | bytes 1544 | tf_op jit(solution)/shard_map/cond/branch_1_fun/ppermute | solution.py:397
  50.7 4.8 %collective-permute-start.34 = (bf16[4,56,256]{2,1,0:T(8,128)(2,1)S(1)}, bf16[4,56,256]{2,1,0:T(8,128)(2,1)S(1)}, u32[]{:S(2)}, u32[]{:S(2)}) collective-permute-start(bf16[4,56,256]{2,1,0:T(8,128)(2,1)S(1)} %get-tuple-element.122), channel_id=1, source_target_pairs={{0,1},{1,0},{2,3},{3,2},{4,5},{5,4},{6,7},{7,6},{8,9},{9,8},{10,11... | collective-permute-start | bytes 344072 | tf_op jit(solution)/shard_map/cond/branch_1_fun/ppermute | solution.py:397
  51.2 4.8 %collective-permute-start.35 = (bf16[4,56,256]{2,1,0:T(8,128)(2,1)S(1)}, bf16[4,56,256]{2,1,0:T(8,128)(2,1)S(1)}, u32[]{:S(2)}, u32[]{:S(2)}) collective-permute-start(bf16[4,56,256]{2,1,0:T(8,128)(2,1)S(1)} %get-tuple-element.123), channel_id=1, source_target_pairs={{0,2},{1,3},{2,0},{3,1},{4,6},{5,7},{6,4},{7,5},{8,10},{9,11},{10,... | collective-permute-start | bytes 344072 | tf_op jit(solution)/shard_map/cond/branch_1_fun/ppermute | solution.py:397
  52.7 5.7 %collective-permute-start.36 = (bf16[4,56,256]{2,1,0:T(8,128)(2,1)S(1)}, bf16[4,56,256]{2,1,0:T(8,128)(2,1)S(1)}, u32[]{:S(2)}, u32[]{:S(2)}) collective-permute-start(bf16[4,56,256]{2,1,0:T(8,128)(2,1)S(1)} %get-tuple-element.124), channel_id=1, source_target_pairs={{0,3},{1,2},{2,1},{3,0},{4,7},{5,6},{6,5},{7,4},{8,11},{9,10},{10,... | collective-permute-start | bytes 344072 | tf_op jit(solution)/shard_map/cond/branch_1_fun/ppermute | solution.py:397
  59.1 7.6 %collective-permute-start.37 = (bf16[128,256]{1,0:T(8,128)(2,1)S(1)}, bf16[128,256]{1,0:T(8,128)(2,1)S(1)}, u32[]{:S(2)}, u32[]{:S(2)}) collective-permute-start(bf16[128,256]{1,0:T(8,128)(2,1)S(1)} %get-tuple-element.125), channel_id=1, source_target_pairs={{0,4},{1,5},{2,6},{3,7},{4,0},{5,1},{6,2},{7,3},{8,12},{9,13},{10,... | collective-permute-start | bytes 196616 | tf_op jit(solution)/shard_map/cond/branch_1_fun/ppermute | solution.py:397
  59.2 5.8 %collective-permute-start.38 = (bf16[128,256]{1,0:T(8,128)(2,1)S(1)}, bf16[128,256]{1,0:T(8,128)(2,1)S(1)}, u32[]{:S(2)}, u32[]{:S(2)}) collective-permute-start(bf16[128,256]{1,0:T(8,128)(2,1)S(1)} %get-tuple-element.126), channel_id=1, source_target_pairs={{0,28},{1,29},{2,30},{3,31},{4,8},{5,9},{6,10},{7,11},{8,4},{9,5},... | collective-permute-start | bytes 196616 | tf_op jit(solution)/shard_map/cond/branch_1_fun/ppermute | solution.py:397
  59.3 7.5 %collective-permute-start.39 = (bf16[128,256]{1,0:T(8,128)(2,1)S(1)}, bf16[128,256]{1,0:T(8,128)(2,1)S(1)}, u32[]{:S(2)}, u32[]{:S(2)}) collective-permute-start(bf16[128,256]{1,0:T(8,128)(2,1)S(1)} %get-tuple-element.127), channel_id=1, source_target_pairs={{0,16},{1,17},{2,18},{3,19},{4,20},{5,21},{6,22},{7,23},{8,24},{9,... | collective-permute-start | bytes 196616 | tf_op jit(solution)/shard_map/cond/branch_1_fun/ppermute | solution.py:397

commit v3 on v2

--- a/solution.py
+++ b/solution.py
@@ -180,7 +180,7 @@
     return nt(one, high) + nt(one, low)
 
 
-def table_kernel(rec_ref, text_ref, label_ref, out_ref, seen_ref, count_ref, *, recs, owned):
+def table_kernel(rec_ref, text_ref, label_ref, table_ref, most_ref, out_ref, seen_ref, count_ref, *, recs, owned):
     here = lax.axis_index("rec")
     odd = lax.rem(here, 2)
     far, cross = lax.rem(here + 2 * odd + recs - 1, recs), lax.rem(here + recs // 2, recs)
@@ -200,40 +200,50 @@
         owner = lax.div(text, owned)
         which = jnp.where(owner == far, 1, jnp.where(owner == cross, 2, 0))
         at = which * owned + text - owner * owned + (1 - label) * n_cand
-        at = jnp.where(rec == here, at, 4 * n_cand + 1)
+        at = jnp.where(rec == here, at, 2 * n_cand)
         out_ref[at] = out_ref[at] + 1
         return jnp.maximum(most, n)
 
-    out_ref[4 * n_cand + 1] = 0
-    out_ref[4 * n_cand] = lax.fori_loop(0, text_ref.shape[0], pair, jnp.int32(0))
-    for s in range(n_cand):
-        out_ref[3 * n_cand + s] = -1
+    out_ref[2 * n_cand] = 0
+    most_ref[0] = lax.fori_loop(0, text_ref.shape[0], pair, jnp.int32(0))
+    row = lax.broadcasted_iota(jnp.int32, table_ref.shape, 0)
+    lane = lax.broadcasted_iota(jnp.int32, table_ref.shape, 1)
+    table = jnp.zeros(table_ref.shape, F32)
     at = jnp.int32(0)
     for c in range(n_cand):
-        used = (out_ref[c] + out_ref[n_cand + c]) > 0
-        out_ref[2 * n_cand + c] = jnp.where(used, at, -1)
-
-        @pl.when(used)
-        def _(at=at, c=c):
-            out_ref[3 * n_cand + at] = c
-
+        pos, neg = out_ref[c], out_ref[n_cand + c]
+        used = (pos + neg) > 0
+        here = row == jnp.where(used, at, -1)
+        for k, value in ((c, 1.0), (n_cand, pos.astype(F32)), (n_cand + 1, neg.astype(F32))):
+            table = jnp.where(here & (lane == k), value, table)
         at = at + jnp.where(used, 1, 0)
-
-
-def select_kernel(table_ref, a_ref, b_ref, c_ref, out_ref, *, slots, n_cand):
-    owned, _, _ = a_ref.shape
+    table_ref[...] = table
+
+
+def select_kernel(table_ref, *refs, slots):
+    cand_refs, out_ref = refs[:-1], refs[-1]
+    owned = cand_refs[0].shape[0]
+    cands = [ref[j].astype(F32) for ref in cand_refs for j in range(owned)]
     for s in range(slots):
-        c = table_ref[3 * n_cand + s]
-        out_ref[s] = jnp.zeros(out_ref.shape[1:], out_ref.dtype)
-        for i, ref in enumerate((a_ref, b_ref, c_ref)):
-
-            @pl.when((c >= i * owned) & (c < (i + 1) * owned))
-            def _(ref=ref, i=i, s=s, c=c):
-                out_ref[s] = ref[c - i * owned]
+        picked = [table_ref[s : s + 1, c : c + 1] * cand for c, cand in enumerate(cands)]
+        out_ref[s] = functools.reduce(jnp.add, picked).astype(out_ref.dtype)
 
 
 def prepare_kernel(f_ref, out_ref):
     out_ref[...] = nt(eye(f_ref.shape[1]), f_ref[...]).astype(BF16)
+
+
+def if_slot(slot, slots, group, work, idle):
+    if slots % group == 0:
+        work()
+    else:
+        pl.when(slot < slots)(work)
+        pl.when(slot >= slots)(idle)
+
+
+def clear(*refs):
+    for ref in refs:
+        ref[...] = jnp.zeros(ref.shape, ref.dtype)
 
 
 def forward_kernel(f_ref, ft_ref, *refs, unit, first, group, scale):
@@ -242,21 +252,24 @@
     held, w, width = q_refs[0].shape
     slot = first + (me ^ unit)
     rows = group * w
-    for j in range(group):
-        block = q_refs[j][jnp.minimum(slot, held - 1)].astype(F32)
-        q_ref[me ^ j] = jnp.where(slot < held, block, 0.0)
-    q = q_ref[...].reshape(rows, width).astype(BF16)
-    q_out_ref[...] = q
-    s = nt(f_ref[...], q) * scale
-    top = jnp.max(s, axis=0, keepdims=True)
-    weights = jnp.exp(s - top)
-    weights_ref[...] = weights
-    top_ref[...] = top
-    out_ref[:rows] = turned(nn(ft_ref[...], weights.astype(BF16)), eye(rows))
-    out_ref[rows:] = stack([top], LINES, width)
-
-
-def token_kernel(table_ref, q_ref, *refs, first, group, tokens, n_cand):
+
+    def work():
+        for j in range(group):
+            q_ref[me ^ j] = q_refs[j][jnp.minimum(slot, held - 1)].astype(F32)
+        q = q_ref[...].reshape(rows, width).astype(BF16)
+        q_out_ref[...] = q
+        s = nt(f_ref[...], q) * scale
+        top = jnp.max(s, axis=0, keepdims=True)
+        weights = jnp.exp(s - top)
+        weights_ref[...] = weights
+        top_ref[...] = top
+        out_ref[:rows] = turned(nn(ft_ref[...], weights.astype(BF16)), eye(rows))
+        out_ref[rows:] = stack([top], LINES, width)
+
+    if_slot(slot, held if first else group, group, work, lambda: clear(q_out_ref, out_ref))
+
+
+def token_kernel(table_ref, q_ref, *refs, first, slots, group, tokens, n_cand):
     in_refs, (out_ref, direct_ref) = refs[:group], refs[group:]
     rows, width = q_ref.shape
     one = eye(rows)
@@ -273,11 +286,10 @@
     cos = jnp.sum(q_unit * c_unit, axis=1, keepdims=True)
     score = jnp.sum(cos, axis=0, keepdims=True) / tokens
     logit = TEMP * score + BIAS
-    slot = first + lax.axis_index("frame")
-    c = jnp.where(slot < n_cand, table_ref[3 * n_cand + jnp.minimum(slot, n_cand - 1)], -1)
-    used = jnp.where(c >= 0, 1, 0)
-    pos = (used * table_ref[jnp.maximum(c, 0)]).astype(F32)
-    neg = (used * table_ref[n_cand + jnp.maximum(c, 0)]).astype(F32)
+    table = table_ref[...]
+    mine = lax.broadcasted_iota(jnp.int32, table.shape, 0) == first + lax.axis_index("frame")
+    counts = jnp.sum(jnp.where(mine, table, 0.0), axis=0, keepdims=True)
+    pos, neg = counts[:, n_cand : n_cand + 1], counts[:, n_cand + 1 : n_cand + 2]
     tail = jnp.log1p(jnp.exp(-jnp.abs(logit)))
     loss = pos * (jnp.maximum(-logit, 0.0) + tail) + neg * (jnp.maximum(logit, 0.0) + tail)
     grad_pos = (-LOSS_SCALE * TEMP / tokens) * jax.nn.sigmoid(-logit)
@@ -291,20 +303,25 @@
     direct_ref[...] = (pos * grad_pos + neg * grad_neg) * (c_unit - cos * q_unit) * q_norm
 
 
-def backward_kernel(f_ref, ft_ref, weights_ref, top_ref, d_ref, *refs, unit, group, scale):
+def backward_kernel(f_ref, ft_ref, weights_ref, top_ref, d_ref, *refs, unit, first, slots, group, scale):
     if unit == 0:
         direct_ref, refs = refs[0], refs[1:]
     dq_ref, ds_ref, w_ref = refs
     width = f_ref.shape[1]
     rows = top_ref.shape[1]
-    m = unpack(d_ref[rows:].astype(F32), 0, rows)
-    weights = weights_ref[...] * jnp.exp(top_ref[...] - m)
-    w_ref[...] = weights.astype(BF16)
-    ds = (weights * nt(f_ref[...], d_ref[:rows]) * scale).astype(BF16)
-    ds_ref[...] = ds
-    dqt = nn(ft_ref[...], ds)
-    dq = turned(dqt, eye(rows)) + direct_ref[...] if unit == 0 else nt(eye(rows), dqt.astype(BF16))
-    dq_ref[...] = dq.reshape(group, rows // group, width)
+    slot = first + (lax.axis_index("frame") ^ unit)
+
+    def work():
+        m = unpack(d_ref[rows:].astype(F32), 0, rows)
+        weights = weights_ref[...] * jnp.exp(top_ref[...] - m)
+        w_ref[...] = weights.astype(BF16)
+        ds = (weights * nt(f_ref[...], d_ref[:rows]) * scale).astype(BF16)
+        ds_ref[...] = ds
+        dqt = nn(ft_ref[...], ds)
+        dq = turned(dqt, eye(rows)) + direct_ref[...] if unit == 0 else nt(eye(rows), dqt.astype(BF16))
+        dq_ref[...] = dq.reshape(group, rows // group, width)
+
+    if_slot(slot, slots if first else group, group, work, lambda: clear(dq_ref, ds_ref, w_ref))
 
 
 def spread_kernel(*refs, units, group):
@@ -347,16 +364,15 @@
         copy.wait()
 
 
-def finish_kernel(table_ref, pair_ref, across_ref, *refs, n_cand):
+def finish_kernel(table_ref, pair_ref, across_ref, *refs):
     in_refs, outs = refs[:-3], refs[-3:]
-    owned = n_cand // 3
-    w, width = in_refs[0].shape[1:]
-    for c in range(n_cand):
-        s = table_ref[2 * n_cand + c]
+    slots, w, width = in_refs[0].shape
+    owned = (outs[0].shape[0] - EXTRA) // w
+    totals = [functools.reduce(jnp.add, [x[s].astype(F32) for x in in_refs]) for s in range(slots)]
+    for c in range(3 * owned):
+        picked = [table_ref[s : s + 1, c : c + 1] * total for s, total in enumerate(totals)]
         j = c % owned
-        at = jnp.maximum(s, 0)
-        total = functools.reduce(jnp.add, [x[at].astype(F32) for x in in_refs])
-        outs[c // owned][j * w : (j + 1) * w] = jnp.where(s >= 0, total, 0.0).astype(BF16)
+        outs[c // owned][j * w : (j + 1) * w] = functools.reduce(jnp.add, picked).astype(BF16)
     for ref, loss_ref in zip(outs, (across_ref, across_ref, pair_ref)):
         pieces = [x.astype(F32) for x in split(loss_ref[...])]
         ref[owned * w :] = stack(pieces, EXTRA, width).astype(BF16)
@@ -424,9 +440,9 @@
     order = [3, 1, 2, 0]
 
     q = call(
-        functools.partial(select_kernel, slots=slots, n_cand=n_cand),
+        functools.partial(select_kernel, slots=slots),
         shape((slots, w, width), BF16),
-        [SMEM, VMEM, VMEM, VMEM],
+        [VMEM] * 4,
         table, near, far, cross,
     )
     qs = [q] + [permute(q, recs, group, xor[j]) for j in range(1, group)]
@@ -455,9 +471,11 @@
     ds, directs = {}, {}
     for r in range(rounds):
         d, directs[r] = call(
-            functools.partial(token_kernel, first=r * group, group=group, tokens=tokens, n_cand=n_cand),
+            functools.partial(
+                token_kernel, first=r * group, slots=slots, group=group, tokens=tokens, n_cand=n_cand
+            ),
             [shape((rows + EXTRA, width), BF16), shape((rows, width), F32)],
-            [SMEM] + [VMEM] * (1 + group),
+            [VMEM] * (2 + group),
             table, made[r, 0][3], *[sent[r, i] for i in range(group)],
         )
         for i in order:
@@ -468,7 +486,9 @@
     for r in range(rounds):
         for i in order:
             back[r, i] = call(
-                functools.partial(backward_kernel, unit=i, group=group, scale=scale),
+                functools.partial(
+                    backward_kernel, unit=i, first=r * group, slots=slots, group=group, scale=scale
+                ),
                 [shape((group, w, width), F32), shape((depth, rows), BF16), shape((depth, rows), BF16)],
                 [VMEM] * (6 if i == 0 else 5),
                 f, ft, made[r, i][1], made[r, i][2], ds[r, i], *([directs[r]] if i == 0 else []),
@@ -485,9 +505,9 @@
     pair = loss + permute(loss, recs, group, lambda r, g: (r ^ 2, g))
     across = loss + permute(loss, recs, group, lambda r, g: (cross_of(r, recs), g))
     home = call(
-        functools.partial(finish_kernel, n_cand=n_cand),
+        finish_kernel,
         [shape((owned * w + EXTRA, width), BF16)] * 3,
-        [SMEM] + [VMEM] * (2 + group),
+        [VMEM] * (3 + group),
         table, pair, across, *dqs,
     )
     got = []
@@ -525,13 +545,13 @@
         fetched.append(permute(texts, recs, group, lambda r, g: (to(r, recs), g)))
     near, far, cross = fetched
     n_cand = 3 * owned
-    table = pl.pallas_call(
+    table, most = pl.pallas_call(
         functools.partial(table_kernel, recs=recs, owned=owned),
         name="table",
-        out_shape=jax.ShapeDtypeStruct((4 * n_cand + 2,), jnp.int32),
+        out_shape=[jax.ShapeDtypeStruct((8, 128), F32), jax.ShapeDtypeStruct((1,), jnp.int32)],
         in_specs=[SMEM] * 3,
-        out_specs=SMEM,
-        scratch_shapes=[pltpu.SMEM((recs,), jnp.int32)] * 2,
+        out_specs=[VMEM, SMEM],
+        scratch_shapes=[pltpu.SMEM((n,), jnp.int32) for n in (2 * n_cand + 1, recs, recs)],
     )(pair_rec[:, 0], pair_text, pair_label)
 
     def run(slots, *args):
@@ -539,7 +559,7 @@
 
     args = (frames, near, far, cross, table)
     return lax.cond(
-        table[4 * n_cand] <= group, functools.partial(run, group), functools.partial(run, n_cand), *args
+        most[0] <= group, functools.partial(run, group), functools.partial(run, n_cand), *args
     )
 
 

time: 67.6 us -> 66.3 us (0.981)
  Pallas kernels: 19.3 us -> 17.9 us
  starting transfers between devices: 27.2 us -> 28.5 us
    pallas_call x15, Pallas kernels: 17.7 us -> 16.4 us  [call(): pl.pallas_call(kernel, out_shape=out_shape, in_specs=in_specs, out_specs=...]
    ppermute x20, starting transfers between devices: 27.2 us -> 28.5 us  [permute(): return lax.ppermute(x, AXES, pairs)]
  transfers between devices with their start and end apart: 20 -> 20, of which waited for: 15 -> 13; matrix products, arithmetic and copies ran while one was open for 1% -> 0% of each run, Pallas kernels for 20% -> 20%
where the time goes in v3:
time: 66.3 us; the launch traced here: 66.1 us
  starting transfers between devices  28.5 us (43%)
  waiting for transfers between devices  18.3 us (28%)
  Pallas kernels  17.9 us (27%)
  between operations  1.3 us (2%)
    ppermute x20, starting transfers between devices, permute(): return lax.ppermute(x, AXES, pairs)  28.5 us
    ppermute x20, waiting for transfers between devices, permute(): return lax.ppermute(x, AXES, pairs)  18.3 us
    pallas_call x15, Pallas kernels, call(): pl.pallas_call(kernel, out_shape=out_shape, in_specs=in_specs, out_specs=...  16.4 us
    pallas_call x1, Pallas kernels, body(): pl.pallas_call(functools.partial(table_kernel, recs=recs, owned=owned), n...  1.53 us
  transfers between devices with their start and end apart: 20, of which 13 were waited for; matrix products, arithmetic and copies ran while one was open for 0% of the time, Pallas kernels for 20%

profile of v3, /device:TPU:0, one launch (start us, length us, event | category | flops | bytes accessed | tf_op | source)
XLA Modules:
  0.0 66.1 jit_solution(4617211484476849543)
XLA Ops:
  0.6 0.6 collective-permute-start.40
  1.2 3.6 %collective-permute-start.42 = (bf16[2,56,256]{2,1,0:T(8,128)(2,1)}, bf16[2,56,256]{2,1,0:T(8,128)(2,1)S(1)}, u32[]{:S(2)}, u32[]{:S(2)}) collective-permute-start(bf16[2,56,256]{2,1,0:T(8,128)(2,1)} %param.8), channel_id=1, source_target_pairs={{0,16},{1,17},{2,18},{3,19},{4,20},{5,21},{6,22},{7,23},{8,24},{9,... | collective-permute-start | bytes 172040 | tf_op jit(solution)/shard_map/ppermute | solution.py:413
  4.8 1.1 %collective-permute-start.41 = (bf16[2,56,256]{2,1,0:T(8,128)(2,1)}, bf16[2,56,256]{2,1,0:T(8,128)(2,1)S(1)}, u32[]{:S(2)}, u32[]{:S(2)}) collective-permute-start(bf16[2,56,256]{2,1,0:T(8,128)(2,1)} %param.8), channel_id=1, source_target_pairs={{0,28},{1,29},{2,30},{3,31},{4,8},{5,9},{6,10},{7,11},{8,4},{9,5},... | collective-permute-start | bytes 172040 | tf_op jit(solution)/shard_map/ppermute | solution.py:413
  5.9 1.5 %table.1 = (f32[8,128]{1,0:T(8,128)S(1)}, s32[1]{0:T(128)}) custom-call(s32[16]{0:T(128)} %bitcast.34, s32[16]{0:T(128)} %text_ref.1, s32[16]{0:T(128)} %label_ref.1), custom_call_target="tpu_custom_call" | custom-call | tf_op jit(solution)/shard_map/table/pallas_call | solution.py:548
  8.1 0.0 collective-permute-done.40
  8.1 0.8 %collective-permute-done.42 = bf16[2,56,256]{2,1,0:T(8,128)(2,1)S(1)} collective-permute-done((bf16[2,56,256]{2,1,0:T(8,128)(2,1)}, bf16[2,56,256]{2,1,0:T(8,128)(2,1)S(1)}, u32[]{:S(2)}, u32[]{:S(2)}) %collective-permute-start.42) | collective-permute-done | bytes 57376 | tf_op jit(solution)/shard_map/ppermute | solution.py:413
  8.9 1.7 %collective-permute-done.41 = bf16[2,56,256]{2,1,0:T(8,128)(2,1)S(1)} collective-permute-done((bf16[2,56,256]{2,1,0:T(8,128)(2,1)}, bf16[2,56,256]{2,1,0:T(8,128)(2,1)S(1)}, u32[]{:S(2)}, u32[]{:S(2)}) %collective-permute-start.41) | collective-permute-done | bytes 57376 | tf_op jit(solution)/shard_map/ppermute | solution.py:413
  10.6 55.5 %conditional.1 = (bf16[2,56,256]{2,1,0:T(8,128)(2,1)}, f32[]{:T(128)}, bf16[1,1536,256]{2,1,0:T(8,128)(2,1)}) conditional(s32[]{:T(128)} %bitcast.5, (bf16[1,1536,256]{2,1,0:T(8,128)(2,1)}, f32[8,128]{1,0:T(8,128)S(1)}, bf16[2,56,256]{2,1,0:T(8,128)(2,1)S(1)}, bf16[2,56,256]{2,1,0:T(8,128)(2,1)S(1)}, bf16[2,56,256]{2,1,0:T(8,128)(2,1)S(1)}) %tuple.17, ...), branch_computations={%region_0.0_spmd, %region_1.0_spmd} | conditional | flops 8631877632 | bytes 41885132 | solution.py:561
  10.6 0.0 copy-start.1
  10.6 0.2 branch_1_fun.16.refs_0_
  10.8 2.5 %collective-permute-start.25 = (bf16[4,56,256]{2,1,0:T(8,128)(2,1)S(1)}, bf16[4,56,256]{2,1,0:T(8,128)(2,1)S(1)}, u32[]{:S(2)}, u32[]{:S(2)}) collective-permute-start(bf16[4,56,256]{2,1,0:T(8,128)(2,1)S(1)} %branch_1_fun.16.refs_0_), channel_id=1, source_target_pairs={{0,3},{1,2},{2,1},{3,0},{4,7},{5,6},{6,5},{7,4},{8,11},{9,10},{10,... | collective-permute-start | bytes 344072 | tf_op jit(solution)/shard_map/cond/branch_1_fun/ppermute | solution.py:413
  13.3 0.5 collective-permute-start.24
  13.8 0.5 collective-permute-start.23
  14.3 1.5 %branch_1_fun.15.ft_ref = bf16[256,1536]{1,0:T(8,128)(2,1)S(1)} custom-call(bf16[1536,256]{1,0:T(8,128)(2,1)} %bitcast.25), custom_call_target="tpu_custom_call" | custom-call | flops 176160768 | bytes 1048576 | tf_op jit(solution)/shard_map/cond/branch_1_fun/pallas_call | solution.py:395
  15.9 1.9 %collective-permute-done.25.refs_3_ = bf16[4,56,256]{2,1,0:T(8,128)(2,1)S(1)} collective-permute-done((bf16[4,56,256]{2,1,0:T(8,128)(2,1)S(1)}, bf16[4,56,256]{2,1,0:T(8,128)(2,1)S(1)}, u32[]{:S(2)}, u32[]{:S(2)}) %collective-permute-start.25) | collective-permute-done | bytes 114720 | tf_op jit(solution)/shard_map/cond/branch_1_fun/ppermute | solution.py:413
  17.8 0.7 %collective-permute-done.24.refs_2_ = bf16[4,56,256]{2,1,0:T(8,128)(2,1)S(1)} collective-permute-done((bf16[4,56,256]{2,1,0:T(8,128)(2,1)S(1)}, bf16[4,56,256]{2,1,0:T(8,128)(2,1)S(1)}, u32[]{:S(2)}, u32[]{:S(2)}) %collective-permute-start.24) | collective-permute-done | bytes 114720 | tf_op jit(solution)/shard_map/cond/branch_1_fun/ppermute | solution.py:413
  18.5 0.1 collective-permute-done.23.refs_1_
  18.6 0.0 copy-done.1
  18.6 1.6 %branch_1_fun.20 = (f32[232,256]{1,0:T(8,128)S(1)}, f32[1536,224]{1,0:T(8,128)S(1)}, f32[1,224]{1,0:T(1,128)S(1)}, bf16[224,256]{1,0:T(8,128)(2,1)S(1)}) custom-call(bf16[1536,256]{1,0:T(8,128)(2,1)S(1)} %bitcast.26, bf16[256,1536]{1,0:T(8,128)(2,1)S(1)} %branch_1_fun.15.ft_ref, bf16[4,56,256]{2,1,0:T(8,128)(2,1)S(1)} %branch_1_fun.16.refs_0_, ...), custom_call_target="tpu_custom_call" | custom-call | flops 352321536 | bytes 1048576 | tf_op jit(solution)/shard_map/cond/branch_1_fun/pallas_call | solution.py:395
  20.1 1.5 %collective-permute-start.28 = (f32[232,256]{1,0:T(8,128)S(1)}, f32[232,256]{1,0:T(8,128)S(1)}, u32[]{:S(2)}, u32[]{:S(2)}) collective-permute-start(f32[232,256]{1,0:T(8,128)S(1)} %get-tuple-element.107), channel_id=1, source_target_pairs={{0,3},{1,2},{2,1},{3,0},{4,7},{5,6},{6,5},{7,4},{8,11},{9,10},{10,... | collective-permute-start | bytes 712712 | tf_op jit(solution)/shard_map/cond/branch_1_fun/ppermute | solution.py:413
  21.7 1.6 %branch_1_fun.19 = (f32[232,256]{1,0:T(8,128)S(1)}, f32[1536,224]{1,0:T(8,128)S(1)}, f32[1,224]{1,0:T(1,128)S(1)}, bf16[224,256]{1,0:T(8,128)(2,1)S(1)}) custom-call(bf16[1536,256]{1,0:T(8,128)(2,1)S(1)} %bitcast.27, bf16[256,1536]{1,0:T(8,128)(2,1)S(1)} %branch_1_fun.15.ft_ref, bf16[4,56,256]{2,1,0:T(8,128)(2,1)S(1)} %branch_1_fun.16.refs_0_, ...), custom_call_target="tpu_custom_call" | custom-call | flops 352321536 | bytes 1048576 | tf_op jit(solution)/shard_map/cond/branch_1_fun/pallas_call | solution.py:395
  23.3 0.9 %collective-permute-start.27 = (f32[232,256]{1,0:T(8,128)S(1)}, f32[232,256]{1,0:T(8,128)S(1)}, u32[]{:S(2)}, u32[]{:S(2)}) collective-permute-start(f32[232,256]{1,0:T(8,128)S(1)} %get-tuple-element.106), channel_id=1, source_target_pairs={{0,2},{1,3},{2,0},{3,1},{4,6},{5,7},{6,4},{7,5},{8,10},{9,11},{10,... | collective-permute-start | bytes 712712 | tf_op jit(solution)/shard_map/cond/branch_1_fun/ppermute | solution.py:413
  24.1 1.6 %branch_1_fun.18 = (f32[232,256]{1,0:T(8,128)S(1)}, f32[1536,224]{1,0:T(8,128)S(1)}, f32[1,224]{1,0:T(1,128)S(1)}, bf16[224,256]{1,0:T(8,128)(2,1)S(1)}) custom-call(bf16[1536,256]{1,0:T(8,128)(2,1)S(1)} %bitcast.28, bf16[256,1536]{1,0:T(8,128)(2,1)S(1)} %branch_1_fun.15.ft_ref, bf16[4,56,256]{2,1,0:T(8,128)(2,1)S(1)} %branch_1_fun.16.refs_0_, ...), custom_call_target="tpu_custom_call" | custom-call | flops 352321536 | bytes 1048576 | tf_op jit(solution)/shard_map/cond/branch_1_fun/pallas_call | solution.py:395
  25.7 1.2 %collective-permute-start.26 = (f32[232,256]{1,0:T(8,128)S(1)}, f32[232,256]{1,0:T(8,128)S(1)}, u32[]{:S(2)}, u32[]{:S(2)}) collective-permute-start(f32[232,256]{1,0:T(8,128)S(1)} %get-tuple-element.105), channel_id=1, source_target_pairs={{0,1},{1,0},{2,3},{3,2},{4,5},{5,4},{6,7},{7,6},{8,9},{9,8},{10,11... | collective-permute-start | bytes 712712 | tf_op jit(solution)/shard_map/cond/branch_1_fun/ppermute | solution.py:413
  26.9 1.6 %branch_1_fun.17 = (f32[232,256]{1,0:T(8,128)S(1)}, f32[1536,224]{1,0:T(8,128)S(1)}, f32[1,224]{1,0:T(1,128)S(1)}, bf16[224,256]{1,0:T(8,128)(2,1)S(1)}) custom-call(bf16[1536,256]{1,0:T(8,128)(2,1)S(1)} %bitcast.29, bf16[256,1536]{1,0:T(8,128)(2,1)S(1)} %branch_1_fun.15.ft_ref, bf16[4,56,256]{2,1,0:T(8,128)(2,1)S(1)} %branch_1_fun.16.refs_0_, ...), custom_call_target="tpu_custom_call" | custom-call | flops 352321536 | bytes 1048576 | tf_op jit(solution)/shard_map/cond/branch_1_fun/pallas_call | solution.py:395
  28.5 0.0 collective-permute-done.28.refs_3_
  28.5 2.6 %collective-permute-done.27.refs_2_ = f32[232,256]{1,0:T(8,128)S(1)} collective-permute-done((f32[232,256]{1,0:T(8,128)S(1)}, f32[232,256]{1,0:T(8,128)S(1)}, u32[]{:S(2)}, u32[]{:S(2)}) %collective-permute-start.27) | collective-permute-done | bytes 237600 | tf_op jit(solution)/shard_map/cond/branch_1_fun/ppermute | solution.py:413
  31.1 1.3 %collective-permute-done.26.refs_1_ = f32[232,256]{1,0:T(8,128)S(1)} collective-permute-done((f32[232,256]{1,0:T(8,128)S(1)}, f32[232,256]{1,0:T(8,128)S(1)}, u32[]{:S(2)}, u32[]{:S(2)}) %collective-permute-start.26) | collective-permute-done | bytes 237600 | tf_op jit(solution)/shard_map/cond/branch_1_fun/ppermute | solution.py:413
  32.4 1.0 %branch_1_fun.21 = (bf16[240,256]{1,0:T(8,128)(2,1)S(1)}, f32[224,256]{1,0:T(8,128)S(1)}) custom-call(f32[8,128]{1,0:T(8,128)S(1)} %get-tuple-element.97.table_ref, bf16[224,256]{1,0:T(8,128)(2,1)S(1)} %get-tuple-element.103.q_ref.refs_4_, f32[232,256]{1,0:T(8,128)S(1)} %get-tuple-element.104.refs_0_, f32[232,256]{1,0:T(8,128)S(1)} %collective-permute-done.26.refs_1_, ...), custom_call_target="tpu_custom_call" | custom-call | bytes 1048576 | tf_op jit(solution)/shard_map/cond/branch_1_fun/pallas_call | solution.py:395
  33.4 0.7 %collective-permute-start.29 = (bf16[240,256]{1,0:T(8,128)(2,1)S(1)}, bf16[240,256]{1,0:T(8,128)(2,1)S(1)}, u32[]{:S(2)}, u32[]{:S(2)}) collective-permute-start(bf16[240,256]{1,0:T(8,128)(2,1)S(1)} %get-tuple-element.108.d_ref.refs_4_.refs_12_), channel_id=1, source_target_pairs={{0,1},{1,0},{2,3},{3,2},{4,5},{5,4},{6,7},{7,6},{8,9},{9,8},{10,11... | collective-permute-start | bytes 368648 | tf_op jit(solution)/shard_map/cond/branch_1_fun/ppermute | solution.py:413
  34.1 1.5 %collective-permute-start.30 = (bf16[240,256]{1,0:T(8,128)(2,1)S(1)}, bf16[240,256]{1,0:T(8,128)(2,1)S(1)}, u32[]{:S(2)}, u32[]{:S(2)}) collective-permute-start(bf16[240,256]{1,0:T(8,128)(2,1)S(1)} %get-tuple-element.108.d_ref.refs_4_.refs_12_), channel_id=1, source_target_pairs={{0,2},{1,3},{2,0},{3,1},{4,6},{5,7},{6,4},{7,5},{8,10},{9,11},{10,... | collective-permute-start | bytes 368648 | tf_op jit(solution)/shard_map/cond/branch_1_fun/ppermute | solution.py:413
  35.6 1.3 %collective-permute-start.31 = (bf16[240,256]{1,0:T(8,128)(2,1)S(1)}, bf16[240,256]{1,0:T(8,128)(2,1)S(1)}, u32[]{:S(2)}, u32[]{:S(2)}) collective-permute-start(bf16[240,256]{1,0:T(8,128)(2,1)S(1)} %get-tuple-element.108.d_ref.refs_4_.refs_12_), channel_id=1, source_target_pairs={{0,3},{1,2},{2,1},{3,0},{4,7},{5,6},{6,5},{7,4},{8,11},{9,10},{10,... | collective-permute-start | bytes 368648 | tf_op jit(solution)/shard_map/cond/branch_1_fun/ppermute | solution.py:413
  36.9 1.0 %branch_1_fun.22 = (f32[4,56,256]{2,1,0:T(8,128)S(1)}, bf16[1536,224]{1,0:T(8,128)(2,1)S(1)}, bf16[1536,224]{1,0:T(8,128)(2,1)S(1)}) custom-call(bf16[1536,256]{1,0:T(8,128)(2,1)S(1)} %bitcast.30, bf16[256,1536]{1,0:T(8,128)(2,1)S(1)} %branch_1_fun.15.ft_ref, f32[1536,224]{1,0:T(8,128)S(1)} %get-tuple-element.101.weights_ref, ...), custom_call_target="tpu_custom_call" | custom-call | flops 352321536 | bytes 1048576 | tf_op jit(solution)/shard_map/cond/branch_1_fun/pallas_call | solution.py:395
  37.9 1.6 %collective-permute-done.29.d_ref.refs_5_.refs_13_ = bf16[240,256]{1,0:T(8,128)(2,1)S(1)} collective-permute-done((bf16[240,256]{1,0:T(8,128)(2,1)S(1)}, bf16[240,256]{1,0:T(8,128)(2,1)S(1)}, u32[]{:S(2)}, u32[]{:S(2)}) %collective-permute-start.29) | collective-permute-done | bytes 122912 | tf_op jit(solution)/shard_map/cond/branch_1_fun/ppermute | solution.py:413
  39.5 1.0 %branch_1_fun.23 = (f32[4,56,256]{2,1,0:T(8,128)S(1)}, bf16[1536,224]{1,0:T(8,128)(2,1)S(1)}, bf16[1536,224]{1,0:T(8,128)(2,1)S(1)}) custom-call(bf16[1536,256]{1,0:T(8,128)(2,1)S(1)} %bitcast.31, bf16[256,1536]{1,0:T(8,128)(2,1)S(1)} %branch_1_fun.15.ft_ref, f32[1536,224]{1,0:T(8,128)S(1)} %get-tuple-element.111.weights_ref, ...), custom_call_target="tpu_custom_call" | custom-call | flops 352321536 | bytes 1048576 | tf_op jit(solution)/shard_map/cond/branch_1_fun/pallas_call | solution.py:395
  40.5 0.0 collective-permute-done.30.d_ref.refs_6_.refs_14_
  40.5 1.0 %branch_1_fun.24 = (f32[4,56,256]{2,1,0:T(8,128)S(1)}, bf16[1536,224]{1,0:T(8,128)(2,1)S(1)}, bf16[1536,224]{1,0:T(8,128)(2,1)S(1)}) custom-call(bf16[1536,256]{1,0:T(8,128)(2,1)S(1)} %bitcast.32, bf16[256,1536]{1,0:T(8,128)(2,1)S(1)} %branch_1_fun.15.ft_ref, f32[1536,224]{1,0:T(8,128)S(1)} %get-tuple-element.114.weights_ref, ...), custom_call_target="tpu_custom_call" | custom-call | flops 352321536 | bytes 1048576 | tf_op jit(solution)/shard_map/cond/branch_1_fun/pallas_call | solution.py:395
  41.5 0.0 collective-permute-done.31.d_ref.refs_7_.refs_15_
  41.5 1.0 %branch_1_fun.25 = (f32[4,56,256]{2,1,0:T(8,128)S(1)}, bf16[1536,224]{1,0:T(8,128)(2,1)S(1)}, bf16[1536,224]{1,0:T(8,128)(2,1)S(1)}) custom-call(bf16[1536,256]{1,0:T(8,128)(2,1)S(1)} %bitcast.33, bf16[256,1536]{1,0:T(8,128)(2,1)S(1)} %branch_1_fun.15.ft_ref, f32[1536,224]{1,0:T(8,128)S(1)} %get-tuple-element.117.weights_ref, ...), custom_call_target="tpu_custom_call" | custom-call | flops 352321536 | bytes 1048576 | tf_op jit(solution)/shard_map/cond/branch_1_fun/pallas_call | solution.py:395
  42.4 0.1 branch_1_fun.26
  42.5 2.4 %collective-permute-start.33 = (f32[1,128]{1,0:T(1,128)S(1)}, f32[1,128]{1,0:T(1,128)S(1)}, u32[]{:S(2)}, u32[]{:S(2)}) collective-permute-start(f32[1,128]{1,0:T(1,128)S(1)} %get-tuple-element.120), channel_id=1, source_target_pairs={{0,16},{1,17},{2,18},{3,19},{4,20},{5,21},{6,22},{7,23},{8,24},{9,... | collective-permute-start | bytes 1544 | tf_op jit(solution)/shard_map/cond/branch_1_fun/ppermute | solution.py:413
  44.9 5.0 %collective-permute-start.32 = (f32[1,128]{1,0:T(1,128)S(1)}, f32[1,128]{1,0:T(1,128)S(1)}, u32[]{:S(2)}, u32[]{:S(2)}) collective-permute-start(f32[1,128]{1,0:T(1,128)S(1)} %get-tuple-element.120), channel_id=1, source_target_pairs={{0,8},{1,9},{2,10},{3,11},{4,12},{5,13},{6,14},{7,15},{8,0},{9,1},... | collective-permute-start | bytes 1544 | tf_op jit(solution)/shard_map/cond/branch_1_fun/ppermute | solution.py:413
  49.9 0.5 collective-permute-start.34
  50.4 1.5 %collective-permute-start.35 = (bf16[4,56,256]{2,1,0:T(8,128)(2,1)S(1)}, bf16[4,56,256]{2,1,0:T(8,128)(2,1)S(1)}, u32[]{:S(2)}, u32[]{:S(2)}) collective-permute-start(bf16[4,56,256]{2,1,0:T(8,128)(2,1)S(1)} %get-tuple-element.123), channel_id=1, source_target_pairs={{0,2},{1,3},{2,0},{3,1},{4,6},{5,7},{6,4},{7,5},{8,10},{9,11},{10,... | collective-permute-start | bytes 344072 | tf_op jit(solution)/shard_map/cond/branch_1_fun/ppermute | solution.py:413
  51.9 1.4 %collective-permute-start.36 = (bf16[4,56,256]{2,1,0:T(8,128)(2,1)S(1)}, bf16[4,56,256]{2,1,0:T(8,128)(2,1)S(1)}, u32[]{:S(2)}, u32[]{:S(2)}) collective-permute-start(bf16[4,56,256]{2,1,0:T(8,128)(2,1)S(1)} %get-tuple-element.124), channel_id=1, source_target_pairs={{0,3},{1,2},{2,1},{3,0},{4,7},{5,6},{6,5},{7,4},{8,11},{9,10},{10,... | collective-permute-start | bytes 344072 | tf_op jit(solution)/shard_map/cond/branch_1_fun/ppermute | solution.py:413
  53.3 0.0 collective-permute-done.33
  53.3 0.0 collective-permute-done.32
  53.4 1.3 %collective-permute-done.34.refs_1_ = bf16[4,56,256]{2,1,0:T(8,128)(2,1)S(1)} collective-permute-done((bf16[4,56,256]{2,1,0:T(8,128)(2,1)S(1)}, bf16[4,56,256]{2,1,0:T(8,128)(2,1)S(1)}, u32[]{:S(2)}, u32[]{:S(2)}) %collective-permute-start.34) | collective-permute-done | bytes 114720 | tf_op jit(solution)/shard_map/cond/branch_1_fun/ppermute | solution.py:413
  54.6 0.5 collective-permute-done.35.refs_2_
  55.2 2.4 %collective-permute-done.36.refs_3_ = bf16[4,56,256]{2,1,0:T(8,128)(2,1)S(1)} collective-permute-done((bf16[4,56,256]{2,1,0:T(8,128)(2,1)S(1)}, bf16[4,56,256]{2,1,0:T(8,128)(2,1)S(1)}, u32[]{:S(2)}, u32[]{:S(2)}) %collective-permute-start.36) | collective-permute-done | bytes 114720 | tf_op jit(solution)/shard_map/cond/branch_1_fun/ppermute | solution.py:413
  57.6 0.2 branch_1_fun.27
  57.8 0.1 collective-permute-start.37
  57.9 0.1 collective-permute-start.38
  58.0 1.5 %collective-permute-start.39 = (bf16[128,256]{1,0:T(8,128)(2,1)S(1)}, bf16[128,256]{1,0:T(8,128)(2,1)S(1)}, u32[]{:S(2)}, u32[]{:S(2)}) collective-permute-start(bf16[128,256]{1,0:T(8,128)(2,1)S(1)} %get-tuple-element.127), channel_id=1, source_target_pairs={{0,16},{1,17},{2,18},{3,19},{4,20},{5,21},{6,22},{7,23},{8,24},{9,... | collective-permute-start | bytes 196616 | tf_op jit(solution)/shard_map/cond/branch_1_fun/ppermute | solution.py:413
  59.4 2.6 %branch_1_fun.29 = bf16[1,1536,256]{2,1,0:T(8,128)(2,1)} custom-call(bf16[1536,224]{1,0:T(8,128)(2,1)S(1)} %get-tuple-element.130.refs_0_, bf16[1536,224]{1,0:T(8,128)(2,1)S(1)} %get-tuple-element.131.refs_1_, bf16[1536,224]{1,0:T(8,128)(2,1)S(1)} %get-tuple-element.132.refs_2_, bf16[1536,224]{1,0:T(8,128)(2,1)S(1)} %get-tuple-element.133.refs_3_, ...), custom_call_target="tpu_custom_call" | custom-call | flops 1409286144 | bytes 1048576 | tf_op jit(solution)/shard_map/cond/branch_1_fun/pallas_call | solution.py:395
  62.0 1.6 %collective-permute-done.38.far_ref = bf16[128,256]{1,0:T(8,128)(2,1)S(1)} collective-permute-done((bf16[128,256]{1,0:T(8,128)(2,1)S(1)}, bf16[128,256]{1,0:T(8,128)(2,1)S(1)}, u32[]{:S(2)}, u32[]{:S(2)}) %collective-permute-start.38) | collective-permute-done | bytes 65568 | tf_op jit(solution)/shard_map/cond/branch_1_fun/ppermute | solution.py:413
  63.6 1.8 %collective-permute-done.39.cross_ref = bf16[128,256]{1,0:T(8,128)(2,1)S(1)} collective-permute-done((bf16[128,256]{1,0:T(8,128)(2,1)S(1)}, bf16[128,256]{1,0:T(8,128)(2,1)S(1)}, u32[]{:S(2)}, u32[]{:S(2)}) %collective-permute-start.39) | collective-permute-done | bytes 65568 | tf_op jit(solution)/shard_map/cond/branch_1_fun/ppermute | solution.py:413
  65.4 0.0 collective-permute-done.37.near_ref
  65.4 0.7 branch_1_fun.28
  (1 shorter events, 0.0 us)
Async XLA Ops:
  0.6 7.5 %collective-permute-start.40 = (bf16[2,56,256]{2,1,0:T(8,128)(2,1)}, bf16[2,56,256]{2,1,0:T(8,128)(2,1)S(1)}, u32[]{:S(2)}, u32[]{:S(2)}) collective-permute-start(bf16[2,56,256]{2,1,0:T(8,128)(2,1)} %param.8), channel_id=1, source_target_pairs={{0,4},{1,5},{2,6},{3,7},{4,0},{5,1},{6,2},{7,3},{8,12},{9,13},{10,... | collective-permute-start | bytes 172040 | tf_op jit(solution)/shard_map/ppermute | solution.py:413
  1.2 7.7 %collective-permute-start.42 = (bf16[2,56,256]{2,1,0:T(8,128)(2,1)}, bf16[2,56,256]{2,1,0:T(8,128)(2,1)S(1)}, u32[]{:S(2)}, u32[]{:S(2)}) collective-permute-start(bf16[2,56,256]{2,1,0:T(8,128)(2,1)} %param.8), channel_id=1, source_target_pairs={{0,16},{1,17},{2,18},{3,19},{4,20},{5,21},{6,22},{7,23},{8,24},{9,... | collective-permute-start | bytes 172040 | tf_op jit(solution)/shard_map/ppermute | solution.py:413
  4.8 5.7 %collective-permute-start.41 = (bf16[2,56,256]{2,1,0:T(8,128)(2,1)}, bf16[2,56,256]{2,1,0:T(8,128)(2,1)S(1)}, u32[]{:S(2)}, u32[]{:S(2)}) collective-permute-start(bf16[2,56,256]{2,1,0:T(8,128)(2,1)} %param.8), channel_id=1, source_target_pairs={{0,28},{1,29},{2,30},{3,31},{4,8},{5,9},{6,10},{7,11},{8,4},{9,5},... | collective-permute-start | bytes 172040 | tf_op jit(solution)/shard_map/ppermute | solution.py:413
  10.6 8.0 %copy-start.1 = (bf16[1,1536,256]{2,1,0:T(8,128)(2,1)S(1)}, bf16[1,1536,256]{2,1,0:T(8,128)(2,1)}, u32[]{:S(2)}) copy-start(bf16[1,1536,256]{2,1,0:T(8,128)(2,1)} %get-tuple-element.154) | copy-start | bytes 2359300 | tf_op jit(solution)/shard_map/cond
  10.8 7.0 %collective-permute-start.25 = (bf16[4,56,256]{2,1,0:T(8,128)(2,1)S(1)}, bf16[4,56,256]{2,1,0:T(8,128)(2,1)S(1)}, u32[]{:S(2)}, u32[]{:S(2)}) collective-permute-start(bf16[4,56,256]{2,1,0:T(8,128)(2,1)S(1)} %branch_1_fun.16.refs_0_), channel_id=1, source_target_pairs={{0,3},{1,2},{2,1},{3,0},{4,7},{5,6},{6,5},{7,4},{8,11},{9,10},{10,... | collective-permute-start | bytes 344072 | tf_op jit(solution)/shard_map/cond/branch_1_fun/ppermute | solution.py:413
  13.3 5.2 %collective-permute-start.24 = (bf16[4,56,256]{2,1,0:T(8,128)(2,1)S(1)}, bf16[4,56,256]{2,1,0:T(8,128)(2,1)S(1)}, u32[]{:S(2)}, u32[]{:S(2)}) collective-permute-start(bf16[4,56,256]{2,1,0:T(8,128)(2,1)S(1)} %branch_1_fun.16.refs_0_), channel_id=1, source_target_pairs={{0,2},{1,3},{2,0},{3,1},{4,6},{5,7},{6,4},{7,5},{8,10},{9,11},{10,... | collective-permute-start | bytes 344072 | tf_op jit(solution)/shard_map/cond/branch_1_fun/ppermute | solution.py:413
  13.8 4.8 %collective-permute-start.23 = (bf16[4,56,256]{2,1,0:T(8,128)(2,1)S(1)}, bf16[4,56,256]{2,1,0:T(8,128)(2,1)S(1)}, u32[]{:S(2)}, u32[]{:S(2)}) collective-permute-start(bf16[4,56,256]{2,1,0:T(8,128)(2,1)S(1)} %branch_1_fun.16.refs_0_), channel_id=1, source_target_pairs={{0,1},{1,0},{2,3},{3,2},{4,5},{5,4},{6,7},{7,6},{8,9},{9,8},{10,11... | collective-permute-start | bytes 344072 | tf_op jit(solution)/shard_map/cond/branch_1_fun/ppermute | solution.py:413
  20.1 8.4 %collective-permute-start.28 = (f32[232,256]{1,0:T(8,128)S(1)}, f32[232,256]{1,0:T(8,128)S(1)}, u32[]{:S(2)}, u32[]{:S(2)}) collective-permute-start(f32[232,256]{1,0:T(8,128)S(1)} %get-tuple-element.107), channel_id=1, source_target_pairs={{0,3},{1,2},{2,1},{3,0},{4,7},{5,6},{6,5},{7,4},{8,11},{9,10},{10,... | collective-permute-start | bytes 712712 | tf_op jit(solution)/shard_map/cond/branch_1_fun/ppermute | solution.py:413
  23.3 7.8 %collective-permute-start.27 = (f32[232,256]{1,0:T(8,128)S(1)}, f32[232,256]{1,0:T(8,128)S(1)}, u32[]{:S(2)}, u32[]{:S(2)}) collective-permute-start(f32[232,256]{1,0:T(8,128)S(1)} %get-tuple-element.106), channel_id=1, source_target_pairs={{0,2},{1,3},{2,0},{3,1},{4,6},{5,7},{6,4},{7,5},{8,10},{9,11},{10,... | collective-permute-start | bytes 712712 | tf_op jit(solution)/shard_map/cond/branch_1_fun/ppermute | solution.py:413
  25.7 6.6 %collective-permute-start.26 = (f32[232,256]{1,0:T(8,128)S(1)}, f32[232,256]{1,0:T(8,128)S(1)}, u32[]{:S(2)}, u32[]{:S(2)}) collective-permute-start(f32[232,256]{1,0:T(8,128)S(1)} %get-tuple-element.105), channel_id=1, source_target_pairs={{0,1},{1,0},{2,3},{3,2},{4,5},{5,4},{6,7},{7,6},{8,9},{9,8},{10,11... | collective-permute-start | bytes 712712 | tf_op jit(solution)/shard_map/cond/branch_1_fun/ppermute | solution.py:413
  33.4 6.1 %collective-permute-start.29 = (bf16[240,256]{1,0:T(8,128)(2,1)S(1)}, bf16[240,256]{1,0:T(8,128)(2,1)S(1)}, u32[]{:S(2)}, u32[]{:S(2)}) collective-permute-start(bf16[240,256]{1,0:T(8,128)(2,1)S(1)} %get-tuple-element.108.d_ref.refs_4_.refs_12_), channel_id=1, source_target_pairs={{0,1},{1,0},{2,3},{3,2},{4,5},{5,4},{6,7},{7,6},{8,9},{9,8},{10,11... | collective-permute-start | bytes 368648 | tf_op jit(solution)/shard_map/cond/branch_1_fun/ppermute | solution.py:413
  34.1 6.4 %collective-permute-start.30 = (bf16[240,256]{1,0:T(8,128)(2,1)S(1)}, bf16[240,256]{1,0:T(8,128)(2,1)S(1)}, u32[]{:S(2)}, u32[]{:S(2)}) collective-permute-start(bf16[240,256]{1,0:T(8,128)(2,1)S(1)} %get-tuple-element.108.d_ref.refs_4_.refs_12_), channel_id=1, source_target_pairs={{0,2},{1,3},{2,0},{3,1},{4,6},{5,7},{6,4},{7,5},{8,10},{9,11},{10,... | collective-permute-start | bytes 368648 | tf_op jit(solution)/shard_map/cond/branch_1_fun/ppermute | solution.py:413
  35.6 5.8 %collective-permute-start.31 = (bf16[240,256]{1,0:T(8,128)(2,1)S(1)}, bf16[240,256]{1,0:T(8,128)(2,1)S(1)}, u32[]{:S(2)}, u32[]{:S(2)}) collective-permute-start(bf16[240,256]{1,0:T(8,128)(2,1)S(1)} %get-tuple-element.108.d_ref.refs_4_.refs_12_), channel_id=1, source_target_pairs={{0,3},{1,2},{2,1},{3,0},{4,7},{5,6},{6,5},{7,4},{8,11},{9,10},{10,... | collective-permute-start | bytes 368648 | tf_op jit(solution)/shard_map/cond/branch_1_fun/ppermute | solution.py:413
  42.5 10.8 %collective-permute-start.33 = (f32[1,128]{1,0:T(1,128)S(1)}, f32[1,128]{1,0:T(1,128)S(1)}, u32[]{:S(2)}, u32[]{:S(2)}) collective-permute-start(f32[1,128]{1,0:T(1,128)S(1)} %get-tuple-element.120), channel_id=1, source_target_pairs={{0,16},{1,17},{2,18},{3,19},{4,20},{5,21},{6,22},{7,23},{8,24},{9,... | collective-permute-start | bytes 1544 | tf_op jit(solution)/shard_map/cond/branch_1_fun/ppermute | solution.py:413
  44.9 8.5 %collective-permute-start.32 = (f32[1,128]{1,0:T(1,128)S(1)}, f32[1,128]{1,0:T(1,128)S(1)}, u32[]{:S(2)}, u32[]{:S(2)}) collective-permute-start(f32[1,128]{1,0:T(1,128)S(1)} %get-tuple-element.120), channel_id=1, source_target_pairs={{0,8},{1,9},{2,10},{3,11},{4,12},{5,13},{6,14},{7,15},{8,0},{9,1},... | collective-permute-start | bytes 1544 | tf_op jit(solution)/shard_map/cond/branch_1_fun/ppermute | solution.py:413
  49.9 4.8 %collective-permute-start.34 = (bf16[4,56,256]{2,1,0:T(8,128)(2,1)S(1)}, bf16[4,56,256]{2,1,0:T(8,128)(2,1)S(1)}, u32[]{:S(2)}, u32[]{:S(2)}) collective-permute-start(bf16[4,56,256]{2,1,0:T(8,128)(2,1)S(1)} %get-tuple-element.122), channel_id=1, source_target_pairs={{0,1},{1,0},{2,3},{3,2},{4,5},{5,4},{6,7},{7,6},{8,9},{9,8},{10,11... | collective-permute-start | bytes 344072 | tf_op jit(solution)/shard_map/cond/branch_1_fun/ppermute | solution.py:413
  50.4 4.8 %collective-permute-start.35 = (bf16[4,56,256]{2,1,0:T(8,128)(2,1)S(1)}, bf16[4,56,256]{2,1,0:T(8,128)(2,1)S(1)}, u32[]{:S(2)}, u32[]{:S(2)}) collective-permute-start(bf16[4,56,256]{2,1,0:T(8,128)(2,1)S(1)} %get-tuple-element.123), channel_id=1, source_target_pairs={{0,2},{1,3},{2,0},{3,1},{4,6},{5,7},{6,4},{7,5},{8,10},{9,11},{10,... | collective-permute-start | bytes 344072 | tf_op jit(solution)/shard_map/cond/branch_1_fun/ppermute | solution.py:413
  51.9 5.7 %collective-permute-start.36 = (bf16[4,56,256]{2,1,0:T(8,128)(2,1)S(1)}, bf16[4,56,256]{2,1,0:T(8,128)(2,1)S(1)}, u32[]{:S(2)}, u32[]{:S(2)}) collective-permute-start(bf16[4,56,256]{2,1,0:T(8,128)(2,1)S(1)} %get-tuple-element.124), channel_id=1, source_target_pairs={{0,3},{1,2},{2,1},{3,0},{4,7},{5,6},{6,5},{7,4},{8,11},{9,10},{10,... | collective-permute-start | bytes 344072 | tf_op jit(solution)/shard_map/cond/branch_1_fun/ppermute | solution.py:413
  57.8 7.6 %collective-permute-start.37 = (bf16[128,256]{1,0:T(8,128)(2,1)S(1)}, bf16[128,256]{1,0:T(8,128)(2,1)S(1)}, u32[]{:S(2)}, u32[]{:S(2)}) collective-permute-start(bf16[128,256]{1,0:T(8,128)(2,1)S(1)} %get-tuple-element.125), channel_id=1, source_target_pairs={{0,4},{1,5},{2,6},{3,7},{4,0},{5,1},{6,2},{7,3},{8,12},{9,13},{10,... | collective-permute-start | bytes 196616 | tf_op jit(solution)/shard_map/cond/branch_1_fun/ppermute | solution.py:413
  57.9 5.8 %collective-permute-start.38 = (bf16[128,256]{1,0:T(8,128)(2,1)S(1)}, bf16[128,256]{1,0:T(8,128)(2,1)S(1)}, u32[]{:S(2)}, u32[]{:S(2)}) collective-permute-start(bf16[128,256]{1,0:T(8,128)(2,1)S(1)} %get-tuple-element.126), channel_id=1, source_target_pairs={{0,28},{1,29},{2,30},{3,31},{4,8},{5,9},{6,10},{7,11},{8,4},{9,5},... | collective-permute-start | bytes 196616 | tf_op jit(solution)/shard_map/cond/branch_1_fun/ppermute | solution.py:413
  58.0 7.5 %collective-permute-start.39 = (bf16[128,256]{1,0:T(8,128)(2,1)S(1)}, bf16[128,256]{1,0:T(8,128)(2,1)S(1)}, u32[]{:S(2)}, u32[]{:S(2)}) collective-permute-start(bf16[128,256]{1,0:T(8,128)(2,1)S(1)} %get-tuple-element.127), channel_id=1, source_target_pairs={{0,16},{1,17},{2,18},{3,19},{4,20},{5,21},{6,22},{7,23},{8,24},{9,... | collective-permute-start | bytes 196616 | tf_op jit(solution)/shard_map/cond/branch_1_fun/ppermute | solution.py:413

commit v4 on v3

--- a/solution.py
+++ b/solution.py
@@ -344,19 +344,53 @@
     loss_ref[...] = loss
 
 
-def frames_kernel(*refs, units):
+def first_frames_kernel(*refs, units, blocks):
     ds_refs, q_refs, w_refs, d_refs = [refs[k * units : (k + 1) * units] for k in range(4)]
-    out_ref, held_ref, sems = refs[4 * units :]
-    rows, depth = q_refs[0].shape[0], held_ref.shape[0]
-    blocks = sems.shape[0]
-    size = depth // blocks
-    copies = []
-    for b in range(blocks):
-        at = pl.ds(b * size, size)
+    out_ref = refs[-1]
+    rows = q_refs[0].shape[0]
+    size = out_ref.shape[0] // blocks
+
+    def block(b, carry):
+        at = pl.ds(pl.multiple_of(b * size, size), size)
         total = None
         for i in range(units):
             term = nn(ds_refs[i][at], q_refs[i][...]) + nn(w_refs[i][at], d_refs[i][:rows])
             total = term if total is None else total + term
+        out_ref[at] = total
+        return carry
+
+    lax.fori_loop(0, blocks, block, 0)
+
+
+def frames_kernel(*refs, units, spare):
+    ds_refs, q_refs, w_refs, d_refs = [refs[k * units : (k + 1) * units] for k in range(4)]
+    out_ref, held_ref, sum_ref, sems = refs[-4:]
+    before = refs[4 * units : -4]
+    rows, depth = q_refs[0].shape[0], held_ref.shape[0]
+    blocks = sems.shape[0]
+    size = depth // blocks
+    me = lax.axis_index("frame")
+    copies = []
+    for b in range(blocks):
+        at = pl.ds(b * size, size)
+        total = before[0][at] if before else None
+        if spare is not None:
+            sum_ref[...] = total
+        for i in range(units):
+
+            def term(i=i, at=at):
+                return nn(ds_refs[i][at], q_refs[i][...]) + nn(w_refs[i][at], d_refs[i][:rows])
+
+            if spare is not None:
+
+                @pl.when((me ^ i) < spare)
+                def _(term=term):
+                    sum_ref[...] = sum_ref[...] + term()
+
+            else:
+                total = term() if total is None else total + term()
+        if spare is not None:
+            total = sum_ref[...]
         held_ref[at] = total.astype(BF16)
         copies.append(pltpu.make_async_copy(held_ref.at[at], out_ref.at[0, at], sems.at[b]))
         copies[-1].start()
@@ -510,21 +544,41 @@
         [VMEM] * (3 + group),
         table, pair, across, *dqs,
     )
+
+    def frame_args(n, some):
+        return [(back[k][1], made[k][3], back[k][2], ds[k])[n] for k in some]
+
     got = []
     for x, where in zip(home, (near_of, far_of, cross_of)):
         got.append(permute(x, recs, group, lambda r, g: (where(r, recs), g)))
-    args = [back[k][1] for k in keys]
+    total = []
+    blocks = 6 if depth % 768 == 0 else 1
+    if rounds > 1:
+        args = [x for n in range(4) for x in frame_args(n, keys[:group])]
+        total = [
+            call(
+                functools.partial(first_frames_kernel, units=group, blocks=blocks // 2 or 1),
+                shape(frames.shape[1:], F32),
+                [VMEM] * len(args),
+                *args,
+                flops=2 * group * cost,
+            )
+        ]
+    args = [x for n in range(4) for x in frame_args(n, keys[-group:])]
     args[0], _ = lax.optimization_barrier((args[0], home[0]))
-    args += [made[k][3] for k in keys] + [back[k][2] for k in keys] + [ds[k] for k in keys]
-    blocks = 6 if depth % 768 == 0 else 1
+    args += total
     total = call(
-        functools.partial(frames_kernel, units=units),
+        functools.partial(frames_kernel, units=group, spare=slots % group or None),
         pltpu.HBM(frames.shape, BF16),
         [VMEM] * len(args),
         *args,
         out_specs=pl.BlockSpec(memory_space=pltpu.HBM),
-        scratch=[pltpu.VMEM((depth, width), BF16), pltpu.SemaphoreType.DMA((blocks,))],
-        flops=2 * units * cost,
+        scratch=[
+            pltpu.VMEM((depth, width), BF16),
+            pltpu.VMEM((depth // blocks, width), F32),
+            pltpu.SemaphoreType.DMA((blocks,)),
+        ],
+        flops=2 * group * cost,
     )
     texts, loss = call(
         close_kernel,

time: 66.3 us -> 66.4 us (level)
  waiting for transfers between devices: 18.3 us -> 20.7 us
  starting transfers between devices: 28.5 us -> 26.2 us
    ppermute x20, waiting for transfers between devices: 18.3 us -> 20.7 us  [permute(): return lax.ppermute(x, AXES, pairs)]
    ppermute x20, starting transfers between devices: 28.5 us -> 26.2 us  [permute(): return lax.ppermute(x, AXES, pairs)]
  transfers between devices with their start and end apart: 20 -> 20, of which waited for: 13 -> 14; matrix products, arithmetic and copies ran while one was open for 0% -> 0% of each run, Pallas kernels for 20% -> 20%
where the time goes in v4:
time: 66.4 us; the launch traced here: 66.3 us
  starting transfers between devices  26.2 us (39%)
  waiting for transfers between devices  20.7 us (31%)
  Pallas kernels  17.9 us (27%)
  between operations  1.3 us (2%)
    ppermute x20, starting transfers between devices, permute(): return lax.ppermute(x, AXES, pairs)  26.2 us
    ppermute x20, waiting for transfers between devices, permute(): return lax.ppermute(x, AXES, pairs)  20.7 us
    pallas_call x15, Pallas kernels, call(): pl.pallas_call(kernel, out_shape=out_shape, in_specs=in_specs, out_specs=...  16.4 us
    pallas_call x1, Pallas kernels, body(): pl.pallas_call(functools.partial(table_kernel, recs=recs, owned=owned), n...  1.53 us
  transfers between devices with their start and end apart: 20, of which 14 were waited for; matrix products, arithmetic and copies ran while one was open for 0% of the time, Pallas kernels for 20%

profile of v4, /device:TPU:0, one launch (start us, length us, event | category | flops | bytes accessed | tf_op | source)
XLA Modules:
  0.0 66.3 jit_solution(12269961697621159836)
XLA Ops:
  0.6 0.6 collective-permute-start.40
  1.2 4.7 %collective-permute-start.41 = (bf16[2,56,256]{2,1,0:T(8,128)(2,1)}, bf16[2,56,256]{2,1,0:T(8,128)(2,1)S(1)}, u32[]{:S(2)}, u32[]{:S(2)}) collective-permute-start(bf16[2,56,256]{2,1,0:T(8,128)(2,1)} %param.8), channel_id=1, source_target_pairs={{0,28},{1,29},{2,30},{3,31},{4,8},{5,9},{6,10},{7,11},{8,4},{9,5},... | collective-permute-start | bytes 172040 | tf_op jit(solution)/shard_map/ppermute | solution.py:447
  5.9 0.0 collective-permute-start.42
  5.9 1.5 %table.1 = (f32[8,128]{1,0:T(8,128)S(1)}, s32[1]{0:T(128)}) custom-call(s32[16]{0:T(128)} %bitcast.34, s32[16]{0:T(128)} %text_ref.1, s32[16]{0:T(128)} %label_ref.1), custom_call_target="tpu_custom_call" | custom-call | tf_op jit(solution)/shard_map/table/pallas_call | solution.py:602
  8.1 0.0 collective-permute-done.40
  8.1 0.1 collective-permute-done.41
  8.2 2.9 %collective-permute-done.42 = bf16[2,56,256]{2,1,0:T(8,128)(2,1)S(1)} collective-permute-done((bf16[2,56,256]{2,1,0:T(8,128)(2,1)}, bf16[2,56,256]{2,1,0:T(8,128)(2,1)S(1)}, u32[]{:S(2)}, u32[]{:S(2)}) %collective-permute-start.42) | collective-permute-done | bytes 57376 | tf_op jit(solution)/shard_map/ppermute | solution.py:447
  11.2 55.1 %conditional.1 = (bf16[2,56,256]{2,1,0:T(8,128)(2,1)}, f32[]{:T(128)}, bf16[1,1536,256]{2,1,0:T(8,128)(2,1)}) conditional(s32[]{:T(128)} %bitcast.5, (bf16[1,1536,256]{2,1,0:T(8,128)(2,1)}, f32[8,128]{1,0:T(8,128)S(1)}, bf16[2,56,256]{2,1,0:T(8,128)(2,1)S(1)}, bf16[2,56,256]{2,1,0:T(8,128)(2,1)S(1)}, bf16[2,56,256]{2,1,0:T(8,128)(2,1)S(1)}) %tuple.17, ...), branch_computations={%region_0.0_spmd, %region_1.0_spmd} | conditional | flops 8631877632 | bytes 42933708 | solution.py:615
  11.2 0.0 copy-start.1
  11.2 0.2 branch_1_fun.16.refs_0_
  11.4 1.6 %collective-permute-start.23 = (bf16[4,56,256]{2,1,0:T(8,128)(2,1)S(1)}, bf16[4,56,256]{2,1,0:T(8,128)(2,1)S(1)}, u32[]{:S(2)}, u32[]{:S(2)}) collective-permute-start(bf16[4,56,256]{2,1,0:T(8,128)(2,1)S(1)} %branch_1_fun.16.refs_0_), channel_id=1, source_target_pairs={{0,1},{1,0},{2,3},{3,2},{4,5},{5,4},{6,7},{7,6},{8,9},{9,8},{10,11... | collective-permute-start | bytes 344072 | tf_op jit(solution)/shard_map/cond/branch_1_fun/ppermute | solution.py:447
  12.9 1.5 %collective-permute-start.24 = (bf16[4,56,256]{2,1,0:T(8,128)(2,1)S(1)}, bf16[4,56,256]{2,1,0:T(8,128)(2,1)S(1)}, u32[]{:S(2)}, u32[]{:S(2)}) collective-permute-start(bf16[4,56,256]{2,1,0:T(8,128)(2,1)S(1)} %branch_1_fun.16.refs_0_), channel_id=1, source_target_pairs={{0,2},{1,3},{2,0},{3,1},{4,6},{5,7},{6,4},{7,5},{8,10},{9,11},{10,... | collective-permute-start | bytes 344072 | tf_op jit(solution)/shard_map/cond/branch_1_fun/ppermute | solution.py:447
  14.5 0.5 collective-permute-start.25
  14.9 1.5 %branch_1_fun.15.ft_ref = bf16[256,1536]{1,0:T(8,128)(2,1)S(1)} custom-call(bf16[1536,256]{1,0:T(8,128)(2,1)} %bitcast.25), custom_call_target="tpu_custom_call" | custom-call | flops 176160768 | bytes 1048576 | tf_op jit(solution)/shard_map/cond/branch_1_fun/pallas_call | solution.py:429
  16.5 0.8 %collective-permute-done.23.refs_1_ = bf16[4,56,256]{2,1,0:T(8,128)(2,1)S(1)} collective-permute-done((bf16[4,56,256]{2,1,0:T(8,128)(2,1)S(1)}, bf16[4,56,256]{2,1,0:T(8,128)(2,1)S(1)}, u32[]{:S(2)}, u32[]{:S(2)}) %collective-permute-start.23) | collective-permute-done | bytes 114720 | tf_op jit(solution)/shard_map/cond/branch_1_fun/ppermute | solution.py:447
  17.2 1.6 %collective-permute-done.24.refs_2_ = bf16[4,56,256]{2,1,0:T(8,128)(2,1)S(1)} collective-permute-done((bf16[4,56,256]{2,1,0:T(8,128)(2,1)S(1)}, bf16[4,56,256]{2,1,0:T(8,128)(2,1)S(1)}, u32[]{:S(2)}, u32[]{:S(2)}) %collective-permute-start.24) | collective-permute-done | bytes 114720 | tf_op jit(solution)/shard_map/cond/branch_1_fun/ppermute | solution.py:447
  18.8 1.3 %collective-permute-done.25.refs_3_ = bf16[4,56,256]{2,1,0:T(8,128)(2,1)S(1)} collective-permute-done((bf16[4,56,256]{2,1,0:T(8,128)(2,1)S(1)}, bf16[4,56,256]{2,1,0:T(8,128)(2,1)S(1)}, u32[]{:S(2)}, u32[]{:S(2)}) %collective-permute-start.25) | collective-permute-done | bytes 114720 | tf_op jit(solution)/shard_map/cond/branch_1_fun/ppermute | solution.py:447
  20.1 0.0 copy-done.1
  20.2 1.6 %branch_1_fun.18 = (f32[232,256]{1,0:T(8,128)S(1)}, f32[1536,224]{1,0:T(8,128)S(1)}, f32[1,224]{1,0:T(1,128)S(1)}, bf16[224,256]{1,0:T(8,128)(2,1)S(1)}) custom-call(bf16[1536,256]{1,0:T(8,128)(2,1)S(1)} %bitcast.26, bf16[256,1536]{1,0:T(8,128)(2,1)S(1)} %branch_1_fun.15.ft_ref, bf16[4,56,256]{2,1,0:T(8,128)(2,1)S(1)} %branch_1_fun.16.refs_0_, ...), custom_call_target="tpu_custom_call" | custom-call | flops 352321536 | bytes 1048576 | tf_op jit(solution)/shard_map/cond/branch_1_fun/pallas_call | solution.py:429
  21.7 0.6 collective-permute-start.26
  22.3 1.6 %branch_1_fun.19 = (f32[232,256]{1,0:T(8,128)S(1)}, f32[1536,224]{1,0:T(8,128)S(1)}, f32[1,224]{1,0:T(1,128)S(1)}, bf16[224,256]{1,0:T(8,128)(2,1)S(1)}) custom-call(bf16[1536,256]{1,0:T(8,128)(2,1)S(1)} %bitcast.27, bf16[256,1536]{1,0:T(8,128)(2,1)S(1)} %branch_1_fun.15.ft_ref, bf16[4,56,256]{2,1,0:T(8,128)(2,1)S(1)} %branch_1_fun.16.refs_0_, ...), custom_call_target="tpu_custom_call" | custom-call | flops 352321536 | bytes 1048576 | tf_op jit(solution)/shard_map/cond/branch_1_fun/pallas_call | solution.py:429
  23.9 0.6 collective-permute-start.27
  24.5 1.6 %branch_1_fun.20 = (f32[232,256]{1,0:T(8,128)S(1)}, f32[1536,224]{1,0:T(8,128)S(1)}, f32[1,224]{1,0:T(1,128)S(1)}, bf16[224,256]{1,0:T(8,128)(2,1)S(1)}) custom-call(bf16[1536,256]{1,0:T(8,128)(2,1)S(1)} %bitcast.28, bf16[256,1536]{1,0:T(8,128)(2,1)S(1)} %branch_1_fun.15.ft_ref, bf16[4,56,256]{2,1,0:T(8,128)(2,1)S(1)} %branch_1_fun.16.refs_0_, ...), custom_call_target="tpu_custom_call" | custom-call | flops 352321536 | bytes 1048576 | tf_op jit(solution)/shard_map/cond/branch_1_fun/pallas_call | solution.py:429
  26.0 2.5 %collective-permute-start.28 = (f32[232,256]{1,0:T(8,128)S(1)}, f32[232,256]{1,0:T(8,128)S(1)}, u32[]{:S(2)}, u32[]{:S(2)}) collective-permute-start(f32[232,256]{1,0:T(8,128)S(1)} %get-tuple-element.107), channel_id=1, source_target_pairs={{0,3},{1,2},{2,1},{3,0},{4,7},{5,6},{6,5},{7,4},{8,11},{9,10},{10,... | collective-permute-start | bytes 712712 | tf_op jit(solution)/shard_map/cond/branch_1_fun/ppermute | solution.py:447
  28.5 1.6 %branch_1_fun.17 = (f32[232,256]{1,0:T(8,128)S(1)}, f32[1536,224]{1,0:T(8,128)S(1)}, f32[1,224]{1,0:T(1,128)S(1)}, bf16[224,256]{1,0:T(8,128)(2,1)S(1)}) custom-call(bf16[1536,256]{1,0:T(8,128)(2,1)S(1)} %bitcast.29, bf16[256,1536]{1,0:T(8,128)(2,1)S(1)} %branch_1_fun.15.ft_ref, bf16[4,56,256]{2,1,0:T(8,128)(2,1)S(1)} %branch_1_fun.16.refs_0_, ...), custom_call_target="tpu_custom_call" | custom-call | flops 352321536 | bytes 1048576 | tf_op jit(solution)/shard_map/cond/branch_1_fun/pallas_call | solution.py:429
  30.1 0.0 collective-permute-done.26.refs_1_
  30.1 4.8 %collective-permute-done.27.refs_2_ = f32[232,256]{1,0:T(8,128)S(1)} collective-permute-done((f32[232,256]{1,0:T(8,128)S(1)}, f32[232,256]{1,0:T(8,128)S(1)}, u32[]{:S(2)}, u32[]{:S(2)}) %collective-permute-start.27) | collective-permute-done | bytes 237600 | tf_op jit(solution)/shard_map/cond/branch_1_fun/ppermute | solution.py:447
  34.9 0.0 collective-permute-done.28.refs_3_
  34.9 1.0 %branch_1_fun.21 = (bf16[240,256]{1,0:T(8,128)(2,1)S(1)}, f32[224,256]{1,0:T(8,128)S(1)}) custom-call(f32[8,128]{1,0:T(8,128)S(1)} %get-tuple-element.97.table_ref, bf16[224,256]{1,0:T(8,128)(2,1)S(1)} %get-tuple-element.103.q_ref.refs_4_, f32[232,256]{1,0:T(8,128)S(1)} %get-tuple-element.104.refs_0_, f32[232,256]{1,0:T(8,128)S(1)} %collective-permute-done.26.refs_1_, ...), custom_call_target="tpu_custom_call" | custom-call | bytes 1048576 | tf_op jit(solution)/shard_map/cond/branch_1_fun/pallas_call | solution.py:429
  35.9 3.6 %collective-permute-start.31 = (bf16[240,256]{1,0:T(8,128)(2,1)S(1)}, bf16[240,256]{1,0:T(8,128)(2,1)S(1)}, u32[]{:S(2)}, u32[]{:S(2)}) collective-permute-start(bf16[240,256]{1,0:T(8,128)(2,1)S(1)} %get-tuple-element.108.d_ref.refs_4_.refs_12_), channel_id=1, source_target_pairs={{0,3},{1,2},{2,1},{3,0},{4,7},{5,6},{6,5},{7,4},{8,11},{9,10},{10,... | collective-permute-start | bytes 368648 | tf_op jit(solution)/shard_map/cond/branch_1_fun/ppermute | solution.py:447
  39.5 1.1 %collective-permute-start.30 = (bf16[240,256]{1,0:T(8,128)(2,1)S(1)}, bf16[240,256]{1,0:T(8,128)(2,1)S(1)}, u32[]{:S(2)}, u32[]{:S(2)}) collective-permute-start(bf16[240,256]{1,0:T(8,128)(2,1)S(1)} %get-tuple-element.108.d_ref.refs_4_.refs_12_), channel_id=1, source_target_pairs={{0,2},{1,3},{2,0},{3,1},{4,6},{5,7},{6,4},{7,5},{8,10},{9,11},{10,... | collective-permute-start | bytes 368648 | tf_op jit(solution)/shard_map/cond/branch_1_fun/ppermute | solution.py:447
  40.7 0.0 collective-permute-start.29
  40.7 1.0 %branch_1_fun.22 = (f32[4,56,256]{2,1,0:T(8,128)S(1)}, bf16[1536,224]{1,0:T(8,128)(2,1)S(1)}, bf16[1536,224]{1,0:T(8,128)(2,1)S(1)}) custom-call(bf16[1536,256]{1,0:T(8,128)(2,1)S(1)} %bitcast.30, bf16[256,1536]{1,0:T(8,128)(2,1)S(1)} %branch_1_fun.15.ft_ref, f32[1536,224]{1,0:T(8,128)S(1)} %get-tuple-element.101.weights_ref, ...), custom_call_target="tpu_custom_call" | custom-call | flops 352321536 | bytes 1048576 | tf_op jit(solution)/shard_map/cond/branch_1_fun/pallas_call | solution.py:429
  41.7 0.7 %collective-permute-done.31.d_ref.refs_7_.refs_15_ = bf16[240,256]{1,0:T(8,128)(2,1)S(1)} collective-permute-done((bf16[240,256]{1,0:T(8,128)(2,1)S(1)}, bf16[240,256]{1,0:T(8,128)(2,1)S(1)}, u32[]{:S(2)}, u32[]{:S(2)}) %collective-permute-start.31) | collective-permute-done | bytes 122912 | tf_op jit(solution)/shard_map/cond/branch_1_fun/ppermute | solution.py:447
  42.4 1.0 %branch_1_fun.25 = (f32[4,56,256]{2,1,0:T(8,128)S(1)}, bf16[1536,224]{1,0:T(8,128)(2,1)S(1)}, bf16[1536,224]{1,0:T(8,128)(2,1)S(1)}) custom-call(bf16[1536,256]{1,0:T(8,128)(2,1)S(1)} %bitcast.31, bf16[256,1536]{1,0:T(8,128)(2,1)S(1)} %branch_1_fun.15.ft_ref, f32[1536,224]{1,0:T(8,128)S(1)} %get-tuple-element.117.weights_ref, ...), custom_call_target="tpu_custom_call" | custom-call | flops 352321536 | bytes 1048576 | tf_op jit(solution)/shard_map/cond/branch_1_fun/pallas_call | solution.py:429
  43.4 1.0 %collective-permute-done.30.d_ref.refs_6_.refs_14_ = bf16[240,256]{1,0:T(8,128)(2,1)S(1)} collective-permute-done((bf16[240,256]{1,0:T(8,128)(2,1)S(1)}, bf16[240,256]{1,0:T(8,128)(2,1)S(1)}, u32[]{:S(2)}, u32[]{:S(2)}) %collective-permute-start.30) | collective-permute-done | bytes 122912 | tf_op jit(solution)/shard_map/cond/branch_1_fun/ppermute | solution.py:447
  44.4 1.0 %branch_1_fun.24 = (f32[4,56,256]{2,1,0:T(8,128)S(1)}, bf16[1536,224]{1,0:T(8,128)(2,1)S(1)}, bf16[1536,224]{1,0:T(8,128)(2,1)S(1)}) custom-call(bf16[1536,256]{1,0:T(8,128)(2,1)S(1)} %bitcast.32, bf16[256,1536]{1,0:T(8,128)(2,1)S(1)} %branch_1_fun.15.ft_ref, f32[1536,224]{1,0:T(8,128)S(1)} %get-tuple-element.114.weights_ref, ...), custom_call_target="tpu_custom_call" | custom-call | flops 352321536 | bytes 1048576 | tf_op jit(solution)/shard_map/cond/branch_1_fun/pallas_call | solution.py:429
  45.4 0.8 %collective-permute-done.29.d_ref.refs_5_.refs_13_ = bf16[240,256]{1,0:T(8,128)(2,1)S(1)} collective-permute-done((bf16[240,256]{1,0:T(8,128)(2,1)S(1)}, bf16[240,256]{1,0:T(8,128)(2,1)S(1)}, u32[]{:S(2)}, u32[]{:S(2)}) %collective-permute-start.29) | collective-permute-done | bytes 122912 | tf_op jit(solution)/shard_map/cond/branch_1_fun/ppermute | solution.py:447
  46.2 1.0 %branch_1_fun.23 = (f32[4,56,256]{2,1,0:T(8,128)S(1)}, bf16[1536,224]{1,0:T(8,128)(2,1)S(1)}, bf16[1536,224]{1,0:T(8,128)(2,1)S(1)}) custom-call(bf16[1536,256]{1,0:T(8,128)(2,1)S(1)} %bitcast.33, bf16[256,1536]{1,0:T(8,128)(2,1)S(1)} %branch_1_fun.15.ft_ref, f32[1536,224]{1,0:T(8,128)S(1)} %get-tuple-element.111.weights_ref, ...), custom_call_target="tpu_custom_call" | custom-call | flops 352321536 | bytes 1048576 | tf_op jit(solution)/shard_map/cond/branch_1_fun/pallas_call | solution.py:429
  47.1 0.1 branch_1_fun.26
  47.2 0.1 collective-permute-start.32
  47.3 3.6 %collective-permute-start.33 = (f32[1,128]{1,0:T(1,128)S(1)}, f32[1,128]{1,0:T(1,128)S(1)}, u32[]{:S(2)}, u32[]{:S(2)}) collective-permute-start(f32[1,128]{1,0:T(1,128)S(1)} %get-tuple-element.120), channel_id=1, source_target_pairs={{0,16},{1,17},{2,18},{3,19},{4,20},{5,21},{6,22},{7,23},{8,24},{9,... | collective-permute-start | bytes 1544 | tf_op jit(solution)/shard_map/cond/branch_1_fun/ppermute | solution.py:447
  50.8 0.2 collective-permute-start.34
  51.0 0.9 %collective-permute-start.35 = (bf16[4,56,256]{2,1,0:T(8,128)(2,1)S(1)}, bf16[4,56,256]{2,1,0:T(8,128)(2,1)S(1)}, u32[]{:S(2)}, u32[]{:S(2)}) collective-permute-start(bf16[4,56,256]{2,1,0:T(8,128)(2,1)S(1)} %get-tuple-element.123), channel_id=1, source_target_pairs={{0,2},{1,3},{2,0},{3,1},{4,6},{5,7},{6,4},{7,5},{8,10},{9,11},{10,... | collective-permute-start | bytes 344072 | tf_op jit(solution)/shard_map/cond/branch_1_fun/ppermute | solution.py:447
  52.0 2.4 %collective-permute-start.36 = (bf16[4,56,256]{2,1,0:T(8,128)(2,1)S(1)}, bf16[4,56,256]{2,1,0:T(8,128)(2,1)S(1)}, u32[]{:S(2)}, u32[]{:S(2)}) collective-permute-start(bf16[4,56,256]{2,1,0:T(8,128)(2,1)S(1)} %get-tuple-element.124), channel_id=1, source_target_pairs={{0,3},{1,2},{2,1},{3,0},{4,7},{5,6},{6,5},{7,4},{8,11},{9,10},{10,... | collective-permute-start | bytes 344072 | tf_op jit(solution)/shard_map/cond/branch_1_fun/ppermute | solution.py:447
  54.3 0.0 collective-permute-done.32
  54.3 0.0 collective-permute-done.33
  54.3 1.3 %collective-permute-done.34.refs_1_ = bf16[4,56,256]{2,1,0:T(8,128)(2,1)S(1)} collective-permute-done((bf16[4,56,256]{2,1,0:T(8,128)(2,1)S(1)}, bf16[4,56,256]{2,1,0:T(8,128)(2,1)S(1)}, u32[]{:S(2)}, u32[]{:S(2)}) %collective-permute-start.34) | collective-permute-done | bytes 114720 | tf_op jit(solution)/shard_map/cond/branch_1_fun/ppermute | solution.py:447
  55.6 0.2 collective-permute-done.35.refs_2_
  55.8 1.8 %collective-permute-done.36.refs_3_ = bf16[4,56,256]{2,1,0:T(8,128)(2,1)S(1)} collective-permute-done((bf16[4,56,256]{2,1,0:T(8,128)(2,1)S(1)}, bf16[4,56,256]{2,1,0:T(8,128)(2,1)S(1)}, u32[]{:S(2)}, u32[]{:S(2)}) %collective-permute-start.36) | collective-permute-done | bytes 114720 | tf_op jit(solution)/shard_map/cond/branch_1_fun/ppermute | solution.py:447
  57.7 0.2 branch_1_fun.27
  57.9 0.1 collective-permute-start.37
  57.9 1.6 %collective-permute-start.38 = (bf16[128,256]{1,0:T(8,128)(2,1)S(1)}, bf16[128,256]{1,0:T(8,128)(2,1)S(1)}, u32[]{:S(2)}, u32[]{:S(2)}) collective-permute-start(bf16[128,256]{1,0:T(8,128)(2,1)S(1)} %get-tuple-element.126), channel_id=1, source_target_pairs={{0,28},{1,29},{2,30},{3,31},{4,8},{5,9},{6,10},{7,11},{8,4},{9,5},... | collective-permute-start | bytes 196616 | tf_op jit(solution)/shard_map/cond/branch_1_fun/ppermute | solution.py:447
  59.5 0.2 collective-permute-start.39
  59.7 2.6 %branch_1_fun.29 = bf16[1,1536,256]{2,1,0:T(8,128)(2,1)} custom-call(bf16[1536,224]{1,0:T(8,128)(2,1)S(1)} %get-tuple-element.130.refs_0_, bf16[1536,224]{1,0:T(8,128)(2,1)S(1)} %get-tuple-element.131.refs_1_, bf16[1536,224]{1,0:T(8,128)(2,1)S(1)} %get-tuple-element.132.refs_2_, bf16[1536,224]{1,0:T(8,128)(2,1)S(1)} %get-tuple-element.133.refs_3_, ...), custom_call_target="tpu_custom_call" | custom-call | flops 1409286144 | bytes 1048576 | tf_op jit(solution)/shard_map/cond/branch_1_fun/pallas_call | solution.py:429
  62.3 0.0 collective-permute-done.37.near_ref
  62.3 1.2 %collective-permute-done.38.far_ref = bf16[128,256]{1,0:T(8,128)(2,1)S(1)} collective-permute-done((bf16[128,256]{1,0:T(8,128)(2,1)S(1)}, bf16[128,256]{1,0:T(8,128)(2,1)S(1)}, u32[]{:S(2)}, u32[]{:S(2)}) %collective-permute-start.38) | collective-permute-done | bytes 65568 | tf_op jit(solution)/shard_map/cond/branch_1_fun/ppermute | solution.py:447
  63.5 2.1 %collective-permute-done.39.cross_ref = bf16[128,256]{1,0:T(8,128)(2,1)S(1)} collective-permute-done((bf16[128,256]{1,0:T(8,128)(2,1)S(1)}, bf16[128,256]{1,0:T(8,128)(2,1)S(1)}, u32[]{:S(2)}, u32[]{:S(2)}) %collective-permute-start.39) | collective-permute-done | bytes 65568 | tf_op jit(solution)/shard_map/cond/branch_1_fun/ppermute | solution.py:447
  65.6 0.7 branch_1_fun.28
  (1 shorter events, 0.0 us)
Async XLA Ops:
  0.6 7.4 %collective-permute-start.40 = (bf16[2,56,256]{2,1,0:T(8,128)(2,1)}, bf16[2,56,256]{2,1,0:T(8,128)(2,1)S(1)}, u32[]{:S(2)}, u32[]{:S(2)}) collective-permute-start(bf16[2,56,256]{2,1,0:T(8,128)(2,1)} %param.8), channel_id=1, source_target_pairs={{0,4},{1,5},{2,6},{3,7},{4,0},{5,1},{6,2},{7,3},{8,12},{9,13},{10,... | collective-permute-start | bytes 172040 | tf_op jit(solution)/shard_map/ppermute | solution.py:447
  1.2 7.0 %collective-permute-start.41 = (bf16[2,56,256]{2,1,0:T(8,128)(2,1)}, bf16[2,56,256]{2,1,0:T(8,128)(2,1)S(1)}, u32[]{:S(2)}, u32[]{:S(2)}) collective-permute-start(bf16[2,56,256]{2,1,0:T(8,128)(2,1)} %param.8), channel_id=1, source_target_pairs={{0,28},{1,29},{2,30},{3,31},{4,8},{5,9},{6,10},{7,11},{8,4},{9,5},... | collective-permute-start | bytes 172040 | tf_op jit(solution)/shard_map/ppermute | solution.py:447
  5.9 5.3 %collective-permute-start.42 = (bf16[2,56,256]{2,1,0:T(8,128)(2,1)}, bf16[2,56,256]{2,1,0:T(8,128)(2,1)S(1)}, u32[]{:S(2)}, u32[]{:S(2)}) collective-permute-start(bf16[2,56,256]{2,1,0:T(8,128)(2,1)} %param.8), channel_id=1, source_target_pairs={{0,16},{1,17},{2,18},{3,19},{4,20},{5,21},{6,22},{7,23},{8,24},{9,... | collective-permute-start | bytes 172040 | tf_op jit(solution)/shard_map/ppermute | solution.py:447
  11.2 9.0 %copy-start.1 = (bf16[1,1536,256]{2,1,0:T(8,128)(2,1)S(1)}, bf16[1,1536,256]{2,1,0:T(8,128)(2,1)}, u32[]{:S(2)}) copy-start(bf16[1,1536,256]{2,1,0:T(8,128)(2,1)} %get-tuple-element.154) | copy-start | bytes 2359300 | tf_op jit(solution)/shard_map/cond
  11.4 5.9 %collective-permute-start.23 = (bf16[4,56,256]{2,1,0:T(8,128)(2,1)S(1)}, bf16[4,56,256]{2,1,0:T(8,128)(2,1)S(1)}, u32[]{:S(2)}, u32[]{:S(2)}) collective-permute-start(bf16[4,56,256]{2,1,0:T(8,128)(2,1)S(1)} %branch_1_fun.16.refs_0_), channel_id=1, source_target_pairs={{0,1},{1,0},{2,3},{3,2},{4,5},{5,4},{6,7},{7,6},{8,9},{9,8},{10,11... | collective-permute-start | bytes 344072 | tf_op jit(solution)/shard_map/cond/branch_1_fun/ppermute | solution.py:447
  12.9 5.9 %collective-permute-start.24 = (bf16[4,56,256]{2,1,0:T(8,128)(2,1)S(1)}, bf16[4,56,256]{2,1,0:T(8,128)(2,1)S(1)}, u32[]{:S(2)}, u32[]{:S(2)}) collective-permute-start(bf16[4,56,256]{2,1,0:T(8,128)(2,1)S(1)} %branch_1_fun.16.refs_0_), channel_id=1, source_target_pairs={{0,2},{1,3},{2,0},{3,1},{4,6},{5,7},{6,4},{7,5},{8,10},{9,11},{10,... | collective-permute-start | bytes 344072 | tf_op jit(solution)/shard_map/cond/branch_1_fun/ppermute | solution.py:447
  14.5 5.7 %collective-permute-start.25 = (bf16[4,56,256]{2,1,0:T(8,128)(2,1)S(1)}, bf16[4,56,256]{2,1,0:T(8,128)(2,1)S(1)}, u32[]{:S(2)}, u32[]{:S(2)}) collective-permute-start(bf16[4,56,256]{2,1,0:T(8,128)(2,1)S(1)} %branch_1_fun.16.refs_0_), channel_id=1, source_target_pairs={{0,3},{1,2},{2,1},{3,0},{4,7},{5,6},{6,5},{7,4},{8,11},{9,10},{10,... | collective-permute-start | bytes 344072 | tf_op jit(solution)/shard_map/cond/branch_1_fun/ppermute | solution.py:447
  21.7 8.4 %collective-permute-start.26 = (f32[232,256]{1,0:T(8,128)S(1)}, f32[232,256]{1,0:T(8,128)S(1)}, u32[]{:S(2)}, u32[]{:S(2)}) collective-permute-start(f32[232,256]{1,0:T(8,128)S(1)} %get-tuple-element.105), channel_id=1, source_target_pairs={{0,1},{1,0},{2,3},{3,2},{4,5},{5,4},{6,7},{7,6},{8,9},{9,8},{10,11... | collective-permute-start | bytes 712712 | tf_op jit(solution)/shard_map/cond/branch_1_fun/ppermute | solution.py:447
  23.9 11.0 %collective-permute-start.27 = (f32[232,256]{1,0:T(8,128)S(1)}, f32[232,256]{1,0:T(8,128)S(1)}, u32[]{:S(2)}, u32[]{:S(2)}) collective-permute-start(f32[232,256]{1,0:T(8,128)S(1)} %get-tuple-element.106), channel_id=1, source_target_pairs={{0,2},{1,3},{2,0},{3,1},{4,6},{5,7},{6,4},{7,5},{8,10},{9,11},{10,... | collective-permute-start | bytes 712712 | tf_op jit(solution)/shard_map/cond/branch_1_fun/ppermute | solution.py:447
  26.0 8.9 %collective-permute-start.28 = (f32[232,256]{1,0:T(8,128)S(1)}, f32[232,256]{1,0:T(8,128)S(1)}, u32[]{:S(2)}, u32[]{:S(2)}) collective-permute-start(f32[232,256]{1,0:T(8,128)S(1)} %get-tuple-element.107), channel_id=1, source_target_pairs={{0,3},{1,2},{2,1},{3,0},{4,7},{5,6},{6,5},{7,4},{8,11},{9,10},{10,... | collective-permute-start | bytes 712712 | tf_op jit(solution)/shard_map/cond/branch_1_fun/ppermute | solution.py:447
  35.9 6.5 %collective-permute-start.31 = (bf16[240,256]{1,0:T(8,128)(2,1)S(1)}, bf16[240,256]{1,0:T(8,128)(2,1)S(1)}, u32[]{:S(2)}, u32[]{:S(2)}) collective-permute-start(bf16[240,256]{1,0:T(8,128)(2,1)S(1)} %get-tuple-element.108.d_ref.refs_4_.refs_12_), channel_id=1, source_target_pairs={{0,3},{1,2},{2,1},{3,0},{4,7},{5,6},{6,5},{7,4},{8,11},{9,10},{10,... | collective-permute-start | bytes 368648 | tf_op jit(solution)/shard_map/cond/branch_1_fun/ppermute | solution.py:447
  39.5 4.9 %collective-permute-start.30 = (bf16[240,256]{1,0:T(8,128)(2,1)S(1)}, bf16[240,256]{1,0:T(8,128)(2,1)S(1)}, u32[]{:S(2)}, u32[]{:S(2)}) collective-permute-start(bf16[240,256]{1,0:T(8,128)(2,1)S(1)} %get-tuple-element.108.d_ref.refs_4_.refs_12_), channel_id=1, source_target_pairs={{0,2},{1,3},{2,0},{3,1},{4,6},{5,7},{6,4},{7,5},{8,10},{9,11},{10,... | collective-permute-start | bytes 368648 | tf_op jit(solution)/shard_map/cond/branch_1_fun/ppermute | solution.py:447
  40.7 5.5 %collective-permute-start.29 = (bf16[240,256]{1,0:T(8,128)(2,1)S(1)}, bf16[240,256]{1,0:T(8,128)(2,1)S(1)}, u32[]{:S(2)}, u32[]{:S(2)}) collective-permute-start(bf16[240,256]{1,0:T(8,128)(2,1)S(1)} %get-tuple-element.108.d_ref.refs_4_.refs_12_), channel_id=1, source_target_pairs={{0,1},{1,0},{2,3},{3,2},{4,5},{5,4},{6,7},{7,6},{8,9},{9,8},{10,11... | collective-permute-start | bytes 368648 | tf_op jit(solution)/shard_map/cond/branch_1_fun/ppermute | solution.py:447
  47.2 7.1 %collective-permute-start.32 = (f32[1,128]{1,0:T(1,128)S(1)}, f32[1,128]{1,0:T(1,128)S(1)}, u32[]{:S(2)}, u32[]{:S(2)}) collective-permute-start(f32[1,128]{1,0:T(1,128)S(1)} %get-tuple-element.120), channel_id=1, source_target_pairs={{0,8},{1,9},{2,10},{3,11},{4,12},{5,13},{6,14},{7,15},{8,0},{9,1},... | collective-permute-start | bytes 1544 | tf_op jit(solution)/shard_map/cond/branch_1_fun/ppermute | solution.py:447
  47.3 7.0 %collective-permute-start.33 = (f32[1,128]{1,0:T(1,128)S(1)}, f32[1,128]{1,0:T(1,128)S(1)}, u32[]{:S(2)}, u32[]{:S(2)}) collective-permute-start(f32[1,128]{1,0:T(1,128)S(1)} %get-tuple-element.120), channel_id=1, source_target_pairs={{0,16},{1,17},{2,18},{3,19},{4,20},{5,21},{6,22},{7,23},{8,24},{9,... | collective-permute-start | bytes 1544 | tf_op jit(solution)/shard_map/cond/branch_1_fun/ppermute | solution.py:447
  50.8 4.8 %collective-permute-start.34 = (bf16[4,56,256]{2,1,0:T(8,128)(2,1)S(1)}, bf16[4,56,256]{2,1,0:T(8,128)(2,1)S(1)}, u32[]{:S(2)}, u32[]{:S(2)}) collective-permute-start(bf16[4,56,256]{2,1,0:T(8,128)(2,1)S(1)} %get-tuple-element.122), channel_id=1, source_target_pairs={{0,1},{1,0},{2,3},{3,2},{4,5},{5,4},{6,7},{7,6},{8,9},{9,8},{10,11... | collective-permute-start | bytes 344072 | tf_op jit(solution)/shard_map/cond/branch_1_fun/ppermute | solution.py:447
  51.0 4.8 %collective-permute-start.35 = (bf16[4,56,256]{2,1,0:T(8,128)(2,1)S(1)}, bf16[4,56,256]{2,1,0:T(8,128)(2,1)S(1)}, u32[]{:S(2)}, u32[]{:S(2)}) collective-permute-start(bf16[4,56,256]{2,1,0:T(8,128)(2,1)S(1)} %get-tuple-element.123), channel_id=1, source_target_pairs={{0,2},{1,3},{2,0},{3,1},{4,6},{5,7},{6,4},{7,5},{8,10},{9,11},{10,... | collective-permute-start | bytes 344072 | tf_op jit(solution)/shard_map/cond/branch_1_fun/ppermute | solution.py:447
  52.0 5.7 %collective-permute-start.36 = (bf16[4,56,256]{2,1,0:T(8,128)(2,1)S(1)}, bf16[4,56,256]{2,1,0:T(8,128)(2,1)S(1)}, u32[]{:S(2)}, u32[]{:S(2)}) collective-permute-start(bf16[4,56,256]{2,1,0:T(8,128)(2,1)S(1)} %get-tuple-element.124), channel_id=1, source_target_pairs={{0,3},{1,2},{2,1},{3,0},{4,7},{5,6},{6,5},{7,4},{8,11},{9,10},{10,... | collective-permute-start | bytes 344072 | tf_op jit(solution)/shard_map/cond/branch_1_fun/ppermute | solution.py:447
  57.9 4.4 %collective-permute-start.37 = (bf16[128,256]{1,0:T(8,128)(2,1)S(1)}, bf16[128,256]{1,0:T(8,128)(2,1)S(1)}, u32[]{:S(2)}, u32[]{:S(2)}) collective-permute-start(bf16[128,256]{1,0:T(8,128)(2,1)S(1)} %get-tuple-element.125), channel_id=1, source_target_pairs={{0,4},{1,5},{2,6},{3,7},{4,0},{5,1},{6,2},{7,3},{8,12},{9,13},{10,... | collective-permute-start | bytes 196616 | tf_op jit(solution)/shard_map/cond/branch_1_fun/ppermute | solution.py:447
  57.9 5.6 %collective-permute-start.38 = (bf16[128,256]{1,0:T(8,128)(2,1)S(1)}, bf16[128,256]{1,0:T(8,128)(2,1)S(1)}, u32[]{:S(2)}, u32[]{:S(2)}) collective-permute-start(bf16[128,256]{1,0:T(8,128)(2,1)S(1)} %get-tuple-element.126), channel_id=1, source_target_pairs={{0,28},{1,29},{2,30},{3,31},{4,8},{5,9},{6,10},{7,11},{8,4},{9,5},... | collective-permute-start | bytes 196616 | tf_op jit(solution)/shard_map/cond/branch_1_fun/ppermute | solution.py:447
  59.5 6.1 %collective-permute-start.39 = (bf16[128,256]{1,0:T(8,128)(2,1)S(1)}, bf16[128,256]{1,0:T(8,128)(2,1)S(1)}, u32[]{:S(2)}, u32[]{:S(2)}) collective-permute-start(bf16[128,256]{1,0:T(8,128)(2,1)S(1)} %get-tuple-element.127), channel_id=1, source_target_pairs={{0,16},{1,17},{2,18},{3,19},{4,20},{5,21},{6,22},{7,23},{8,24},{9,... | collective-permute-start | bytes 196616 | tf_op jit(solution)/shard_map/cond/branch_1_fun/ppermute | solution.py:447

commit v5 on v4

--- a/solution.py
+++ b/solution.py
@@ -479,7 +479,9 @@
         [VMEM] * 4,
         table, near, far, cross,
     )
-    qs = [q] + [permute(q, recs, group, xor[j]) for j in range(1, group)]
+    qs = [q]
+    for j in range(1, group):
+        qs.append(permute(q, recs, group, xor[j]))
     ft = call(prepare_kernel, shape((width, depth), BF16), [VMEM], f, flops=cost)
     made, sent = {}, {}
     for r in range(rounds):
@@ -535,7 +537,8 @@
         [VMEM] * (2 * units),
         *[back[k][0] for k in keys], *[ds[k] for k in keys],
     )
-    dqs = [dqs[0]] + [permute(dqs[j], recs, group, xor[j]) for j in range(1, group)]
+    for j in range(1, group):
+        dqs[j] = permute(dqs[j], recs, group, xor[j])
     pair = loss + permute(loss, recs, group, lambda r, g: (r ^ 2, g))
     across = loss + permute(loss, recs, group, lambda r, g: (cross_of(r, recs), g))
     home = call(

time: 66.4 us -> 66.4 us (level)
  no operation moved by 1% of the time
where the time goes in v5:
time: 66.4 us; the launch traced here: 66.3 us
  starting transfers between devices  26.2 us (39%)
  waiting for transfers between devices  20.7 us (31%)
  Pallas kernels  17.9 us (27%)
  between operations  1.3 us (2%)
    ppermute x20, starting transfers between devices, permute(): return lax.ppermute(x, AXES, pairs)  26.2 us
    ppermute x20, waiting for transfers between devices, permute(): return lax.ppermute(x, AXES, pairs)  20.7 us
    pallas_call x15, Pallas kernels, call(): pl.pallas_call(kernel, out_shape=out_shape, in_specs=in_specs, out_specs=...  16.4 us
    pallas_call x1, Pallas kernels, body(): pl.pallas_call(functools.partial(table_kernel, recs=recs, owned=owned), n...  1.53 us
  transfers between devices with their start and end apart: 20, of which 14 were waited for; matrix products, arithmetic and copies ran while one was open for 0% of the time, Pallas kernels for 20%

profile of v5, /device:TPU:0, one launch (start us, length us, event | category | flops | bytes accessed | tf_op | source)
XLA Modules:
  0.0 66.3 jit_solution(12269961697621159836)
XLA Ops:
  0.6 0.6 collective-permute-start.40
  1.2 4.7 %collective-permute-start.41 = (bf16[2,56,256]{2,1,0:T(8,128)(2,1)}, bf16[2,56,256]{2,1,0:T(8,128)(2,1)S(1)}, u32[]{:S(2)}, u32[]{:S(2)}) collective-permute-start(bf16[2,56,256]{2,1,0:T(8,128)(2,1)} %param.8), channel_id=1, source_target_pairs={{0,28},{1,29},{2,30},{3,31},{4,8},{5,9},{6,10},{7,11},{8,4},{9,5},... | collective-permute-start | bytes 172040 | tf_op jit(solution)/shard_map/ppermute | solution.py:447
  5.9 0.0 collective-permute-start.42
  5.9 1.5 %table.1 = (f32[8,128]{1,0:T(8,128)S(1)}, s32[1]{0:T(128)}) custom-call(s32[16]{0:T(128)} %bitcast.34, s32[16]{0:T(128)} %text_ref.1, s32[16]{0:T(128)} %label_ref.1), custom_call_target="tpu_custom_call" | custom-call | tf_op jit(solution)/shard_map/table/pallas_call | solution.py:605
  8.1 0.0 collective-permute-done.40
  8.1 0.1 collective-permute-done.41
  8.2 2.9 %collective-permute-done.42 = bf16[2,56,256]{2,1,0:T(8,128)(2,1)S(1)} collective-permute-done((bf16[2,56,256]{2,1,0:T(8,128)(2,1)}, bf16[2,56,256]{2,1,0:T(8,128)(2,1)S(1)}, u32[]{:S(2)}, u32[]{:S(2)}) %collective-permute-start.42) | collective-permute-done | bytes 57376 | tf_op jit(solution)/shard_map/ppermute | solution.py:447
  11.2 55.1 %conditional.1 = (bf16[2,56,256]{2,1,0:T(8,128)(2,1)}, f32[]{:T(128)}, bf16[1,1536,256]{2,1,0:T(8,128)(2,1)}) conditional(s32[]{:T(128)} %bitcast.5, (bf16[1,1536,256]{2,1,0:T(8,128)(2,1)}, f32[8,128]{1,0:T(8,128)S(1)}, bf16[2,56,256]{2,1,0:T(8,128)(2,1)S(1)}, bf16[2,56,256]{2,1,0:T(8,128)(2,1)S(1)}, bf16[2,56,256]{2,1,0:T(8,128)(2,1)S(1)}) %tuple.17, ...), branch_computations={%region_0.0_spmd, %region_1.0_spmd} | conditional | flops 8631877632 | bytes 42933708 | solution.py:618
  11.2 0.0 copy-start.1
  11.2 0.2 branch_1_fun.16.refs_0_
  11.4 1.6 %collective-permute-start.23 = (bf16[4,56,256]{2,1,0:T(8,128)(2,1)S(1)}, bf16[4,56,256]{2,1,0:T(8,128)(2,1)S(1)}, u32[]{:S(2)}, u32[]{:S(2)}) collective-permute-start(bf16[4,56,256]{2,1,0:T(8,128)(2,1)S(1)} %branch_1_fun.16.refs_0_), channel_id=1, source_target_pairs={{0,1},{1,0},{2,3},{3,2},{4,5},{5,4},{6,7},{7,6},{8,9},{9,8},{10,11... | collective-permute-start | bytes 344072 | tf_op jit(solution)/shard_map/cond/branch_1_fun/ppermute | solution.py:447
  12.9 1.5 %collective-permute-start.24 = (bf16[4,56,256]{2,1,0:T(8,128)(2,1)S(1)}, bf16[4,56,256]{2,1,0:T(8,128)(2,1)S(1)}, u32[]{:S(2)}, u32[]{:S(2)}) collective-permute-start(bf16[4,56,256]{2,1,0:T(8,128)(2,1)S(1)} %branch_1_fun.16.refs_0_), channel_id=1, source_target_pairs={{0,2},{1,3},{2,0},{3,1},{4,6},{5,7},{6,4},{7,5},{8,10},{9,11},{10,... | collective-permute-start | bytes 344072 | tf_op jit(solution)/shard_map/cond/branch_1_fun/ppermute | solution.py:447
  14.5 0.5 collective-permute-start.25
  14.9 1.5 %branch_1_fun.15.ft_ref = bf16[256,1536]{1,0:T(8,128)(2,1)S(1)} custom-call(bf16[1536,256]{1,0:T(8,128)(2,1)} %bitcast.25), custom_call_target="tpu_custom_call" | custom-call | flops 176160768 | bytes 1048576 | tf_op jit(solution)/shard_map/cond/branch_1_fun/pallas_call | solution.py:429
  16.5 0.8 %collective-permute-done.23.refs_1_ = bf16[4,56,256]{2,1,0:T(8,128)(2,1)S(1)} collective-permute-done((bf16[4,56,256]{2,1,0:T(8,128)(2,1)S(1)}, bf16[4,56,256]{2,1,0:T(8,128)(2,1)S(1)}, u32[]{:S(2)}, u32[]{:S(2)}) %collective-permute-start.23) | collective-permute-done | bytes 114720 | tf_op jit(solution)/shard_map/cond/branch_1_fun/ppermute | solution.py:447
  17.2 1.6 %collective-permute-done.24.refs_2_ = bf16[4,56,256]{2,1,0:T(8,128)(2,1)S(1)} collective-permute-done((bf16[4,56,256]{2,1,0:T(8,128)(2,1)S(1)}, bf16[4,56,256]{2,1,0:T(8,128)(2,1)S(1)}, u32[]{:S(2)}, u32[]{:S(2)}) %collective-permute-start.24) | collective-permute-done | bytes 114720 | tf_op jit(solution)/shard_map/cond/branch_1_fun/ppermute | solution.py:447
  18.8 1.3 %collective-permute-done.25.refs_3_ = bf16[4,56,256]{2,1,0:T(8,128)(2,1)S(1)} collective-permute-done((bf16[4,56,256]{2,1,0:T(8,128)(2,1)S(1)}, bf16[4,56,256]{2,1,0:T(8,128)(2,1)S(1)}, u32[]{:S(2)}, u32[]{:S(2)}) %collective-permute-start.25) | collective-permute-done | bytes 114720 | tf_op jit(solution)/shard_map/cond/branch_1_fun/ppermute | solution.py:447
  20.1 0.0 copy-done.1
  20.2 1.6 %branch_1_fun.18 = (f32[232,256]{1,0:T(8,128)S(1)}, f32[1536,224]{1,0:T(8,128)S(1)}, f32[1,224]{1,0:T(1,128)S(1)}, bf16[224,256]{1,0:T(8,128)(2,1)S(1)}) custom-call(bf16[1536,256]{1,0:T(8,128)(2,1)S(1)} %bitcast.26, bf16[256,1536]{1,0:T(8,128)(2,1)S(1)} %branch_1_fun.15.ft_ref, bf16[4,56,256]{2,1,0:T(8,128)(2,1)S(1)} %branch_1_fun.16.refs_0_, ...), custom_call_target="tpu_custom_call" | custom-call | flops 352321536 | bytes 1048576 | tf_op jit(solution)/shard_map/cond/branch_1_fun/pallas_call | solution.py:429
  21.7 0.6 collective-permute-start.26
  22.3 1.6 %branch_1_fun.19 = (f32[232,256]{1,0:T(8,128)S(1)}, f32[1536,224]{1,0:T(8,128)S(1)}, f32[1,224]{1,0:T(1,128)S(1)}, bf16[224,256]{1,0:T(8,128)(2,1)S(1)}) custom-call(bf16[1536,256]{1,0:T(8,128)(2,1)S(1)} %bitcast.27, bf16[256,1536]{1,0:T(8,128)(2,1)S(1)} %branch_1_fun.15.ft_ref, bf16[4,56,256]{2,1,0:T(8,128)(2,1)S(1)} %branch_1_fun.16.refs_0_, ...), custom_call_target="tpu_custom_call" | custom-call | flops 352321536 | bytes 1048576 | tf_op jit(solution)/shard_map/cond/branch_1_fun/pallas_call | solution.py:429
  23.9 0.6 collective-permute-start.27
  24.5 1.6 %branch_1_fun.20 = (f32[232,256]{1,0:T(8,128)S(1)}, f32[1536,224]{1,0:T(8,128)S(1)}, f32[1,224]{1,0:T(1,128)S(1)}, bf16[224,256]{1,0:T(8,128)(2,1)S(1)}) custom-call(bf16[1536,256]{1,0:T(8,128)(2,1)S(1)} %bitcast.28, bf16[256,1536]{1,0:T(8,128)(2,1)S(1)} %branch_1_fun.15.ft_ref, bf16[4,56,256]{2,1,0:T(8,128)(2,1)S(1)} %branch_1_fun.16.refs_0_, ...), custom_call_target="tpu_custom_call" | custom-call | flops 352321536 | bytes 1048576 | tf_op jit(solution)/shard_map/cond/branch_1_fun/pallas_call | solution.py:429
  26.0 2.5 %collective-permute-start.28 = (f32[232,256]{1,0:T(8,128)S(1)}, f32[232,256]{1,0:T(8,128)S(1)}, u32[]{:S(2)}, u32[]{:S(2)}) collective-permute-start(f32[232,256]{1,0:T(8,128)S(1)} %get-tuple-element.107), channel_id=1, source_target_pairs={{0,3},{1,2},{2,1},{3,0},{4,7},{5,6},{6,5},{7,4},{8,11},{9,10},{10,... | collective-permute-start | bytes 712712 | tf_op jit(solution)/shard_map/cond/branch_1_fun/ppermute | solution.py:447
  28.5 1.6 %branch_1_fun.17 = (f32[232,256]{1,0:T(8,128)S(1)}, f32[1536,224]{1,0:T(8,128)S(1)}, f32[1,224]{1,0:T(1,128)S(1)}, bf16[224,256]{1,0:T(8,128)(2,1)S(1)}) custom-call(bf16[1536,256]{1,0:T(8,128)(2,1)S(1)} %bitcast.29, bf16[256,1536]{1,0:T(8,128)(2,1)S(1)} %branch_1_fun.15.ft_ref, bf16[4,56,256]{2,1,0:T(8,128)(2,1)S(1)} %branch_1_fun.16.refs_0_, ...), custom_call_target="tpu_custom_call" | custom-call | flops 352321536 | bytes 1048576 | tf_op jit(solution)/shard_map/cond/branch_1_fun/pallas_call | solution.py:429
  30.1 0.0 collective-permute-done.26.refs_1_
  30.1 4.8 %collective-permute-done.27.refs_2_ = f32[232,256]{1,0:T(8,128)S(1)} collective-permute-done((f32[232,256]{1,0:T(8,128)S(1)}, f32[232,256]{1,0:T(8,128)S(1)}, u32[]{:S(2)}, u32[]{:S(2)}) %collective-permute-start.27) | collective-permute-done | bytes 237600 | tf_op jit(solution)/shard_map/cond/branch_1_fun/ppermute | solution.py:447
  34.9 0.0 collective-permute-done.28.refs_3_
  34.9 1.0 %branch_1_fun.21 = (bf16[240,256]{1,0:T(8,128)(2,1)S(1)}, f32[224,256]{1,0:T(8,128)S(1)}) custom-call(f32[8,128]{1,0:T(8,128)S(1)} %get-tuple-element.97.table_ref, bf16[224,256]{1,0:T(8,128)(2,1)S(1)} %get-tuple-element.103.q_ref.refs_4_, f32[232,256]{1,0:T(8,128)S(1)} %get-tuple-element.104.refs_0_, f32[232,256]{1,0:T(8,128)S(1)} %collective-permute-done.26.refs_1_, ...), custom_call_target="tpu_custom_call" | custom-call | bytes 1048576 | tf_op jit(solution)/shard_map/cond/branch_1_fun/pallas_call | solution.py:429
  35.9 3.6 %collective-permute-start.31 = (bf16[240,256]{1,0:T(8,128)(2,1)S(1)}, bf16[240,256]{1,0:T(8,128)(2,1)S(1)}, u32[]{:S(2)}, u32[]{:S(2)}) collective-permute-start(bf16[240,256]{1,0:T(8,128)(2,1)S(1)} %get-tuple-element.108.d_ref.refs_4_.refs_12_), channel_id=1, source_target_pairs={{0,3},{1,2},{2,1},{3,0},{4,7},{5,6},{6,5},{7,4},{8,11},{9,10},{10,... | collective-permute-start | bytes 368648 | tf_op jit(solution)/shard_map/cond/branch_1_fun/ppermute | solution.py:447
  39.5 1.1 %collective-permute-start.30 = (bf16[240,256]{1,0:T(8,128)(2,1)S(1)}, bf16[240,256]{1,0:T(8,128)(2,1)S(1)}, u32[]{:S(2)}, u32[]{:S(2)}) collective-permute-start(bf16[240,256]{1,0:T(8,128)(2,1)S(1)} %get-tuple-element.108.d_ref.refs_4_.refs_12_), channel_id=1, source_target_pairs={{0,2},{1,3},{2,0},{3,1},{4,6},{5,7},{6,4},{7,5},{8,10},{9,11},{10,... | collective-permute-start | bytes 368648 | tf_op jit(solution)/shard_map/cond/branch_1_fun/ppermute | solution.py:447
  40.7 0.0 collective-permute-start.29
  40.7 1.0 %branch_1_fun.22 = (f32[4,56,256]{2,1,0:T(8,128)S(1)}, bf16[1536,224]{1,0:T(8,128)(2,1)S(1)}, bf16[1536,224]{1,0:T(8,128)(2,1)S(1)}) custom-call(bf16[1536,256]{1,0:T(8,128)(2,1)S(1)} %bitcast.30, bf16[256,1536]{1,0:T(8,128)(2,1)S(1)} %branch_1_fun.15.ft_ref, f32[1536,224]{1,0:T(8,128)S(1)} %get-tuple-element.101.weights_ref, ...), custom_call_target="tpu_custom_call" | custom-call | flops 352321536 | bytes 1048576 | tf_op jit(solution)/shard_map/cond/branch_1_fun/pallas_call | solution.py:429
  41.7 0.7 %collective-permute-done.31.d_ref.refs_7_.refs_15_ = bf16[240,256]{1,0:T(8,128)(2,1)S(1)} collective-permute-done((bf16[240,256]{1,0:T(8,128)(2,1)S(1)}, bf16[240,256]{1,0:T(8,128)(2,1)S(1)}, u32[]{:S(2)}, u32[]{:S(2)}) %collective-permute-start.31) | collective-permute-done | bytes 122912 | tf_op jit(solution)/shard_map/cond/branch_1_fun/ppermute | solution.py:447
  42.4 1.0 %branch_1_fun.25 = (f32[4,56,256]{2,1,0:T(8,128)S(1)}, bf16[1536,224]{1,0:T(8,128)(2,1)S(1)}, bf16[1536,224]{1,0:T(8,128)(2,1)S(1)}) custom-call(bf16[1536,256]{1,0:T(8,128)(2,1)S(1)} %bitcast.31, bf16[256,1536]{1,0:T(8,128)(2,1)S(1)} %branch_1_fun.15.ft_ref, f32[1536,224]{1,0:T(8,128)S(1)} %get-tuple-element.117.weights_ref, ...), custom_call_target="tpu_custom_call" | custom-call | flops 352321536 | bytes 1048576 | tf_op jit(solution)/shard_map/cond/branch_1_fun/pallas_call | solution.py:429
  43.4 1.0 %collective-permute-done.30.d_ref.refs_6_.refs_14_ = bf16[240,256]{1,0:T(8,128)(2,1)S(1)} collective-permute-done((bf16[240,256]{1,0:T(8,128)(2,1)S(1)}, bf16[240,256]{1,0:T(8,128)(2,1)S(1)}, u32[]{:S(2)}, u32[]{:S(2)}) %collective-permute-start.30) | collective-permute-done | bytes 122912 | tf_op jit(solution)/shard_map/cond/branch_1_fun/ppermute | solution.py:447
  44.4 1.0 %branch_1_fun.24 = (f32[4,56,256]{2,1,0:T(8,128)S(1)}, bf16[1536,224]{1,0:T(8,128)(2,1)S(1)}, bf16[1536,224]{1,0:T(8,128)(2,1)S(1)}) custom-call(bf16[1536,256]{1,0:T(8,128)(2,1)S(1)} %bitcast.32, bf16[256,1536]{1,0:T(8,128)(2,1)S(1)} %branch_1_fun.15.ft_ref, f32[1536,224]{1,0:T(8,128)S(1)} %get-tuple-element.114.weights_ref, ...), custom_call_target="tpu_custom_call" | custom-call | flops 352321536 | bytes 1048576 | tf_op jit(solution)/shard_map/cond/branch_1_fun/pallas_call | solution.py:429
  45.4 0.8 %collective-permute-done.29.d_ref.refs_5_.refs_13_ = bf16[240,256]{1,0:T(8,128)(2,1)S(1)} collective-permute-done((bf16[240,256]{1,0:T(8,128)(2,1)S(1)}, bf16[240,256]{1,0:T(8,128)(2,1)S(1)}, u32[]{:S(2)}, u32[]{:S(2)}) %collective-permute-start.29) | collective-permute-done | bytes 122912 | tf_op jit(solution)/shard_map/cond/branch_1_fun/ppermute | solution.py:447
  46.2 1.0 %branch_1_fun.23 = (f32[4,56,256]{2,1,0:T(8,128)S(1)}, bf16[1536,224]{1,0:T(8,128)(2,1)S(1)}, bf16[1536,224]{1,0:T(8,128)(2,1)S(1)}) custom-call(bf16[1536,256]{1,0:T(8,128)(2,1)S(1)} %bitcast.33, bf16[256,1536]{1,0:T(8,128)(2,1)S(1)} %branch_1_fun.15.ft_ref, f32[1536,224]{1,0:T(8,128)S(1)} %get-tuple-element.111.weights_ref, ...), custom_call_target="tpu_custom_call" | custom-call | flops 352321536 | bytes 1048576 | tf_op jit(solution)/shard_map/cond/branch_1_fun/pallas_call | solution.py:429
  47.1 0.1 branch_1_fun.26
  47.2 0.1 collective-permute-start.32
  47.3 3.6 %collective-permute-start.33 = (f32[1,128]{1,0:T(1,128)S(1)}, f32[1,128]{1,0:T(1,128)S(1)}, u32[]{:S(2)}, u32[]{:S(2)}) collective-permute-start(f32[1,128]{1,0:T(1,128)S(1)} %get-tuple-element.120), channel_id=1, source_target_pairs={{0,16},{1,17},{2,18},{3,19},{4,20},{5,21},{6,22},{7,23},{8,24},{9,... | collective-permute-start | bytes 1544 | tf_op jit(solution)/shard_map/cond/branch_1_fun/ppermute | solution.py:447
  50.8 0.2 collective-permute-start.34
  51.0 0.9 %collective-permute-start.35 = (bf16[4,56,256]{2,1,0:T(8,128)(2,1)S(1)}, bf16[4,56,256]{2,1,0:T(8,128)(2,1)S(1)}, u32[]{:S(2)}, u32[]{:S(2)}) collective-permute-start(bf16[4,56,256]{2,1,0:T(8,128)(2,1)S(1)} %get-tuple-element.123), channel_id=1, source_target_pairs={{0,2},{1,3},{2,0},{3,1},{4,6},{5,7},{6,4},{7,5},{8,10},{9,11},{10,... | collective-permute-start | bytes 344072 | tf_op jit(solution)/shard_map/cond/branch_1_fun/ppermute | solution.py:447
  52.0 2.4 %collective-permute-start.36 = (bf16[4,56,256]{2,1,0:T(8,128)(2,1)S(1)}, bf16[4,56,256]{2,1,0:T(8,128)(2,1)S(1)}, u32[]{:S(2)}, u32[]{:S(2)}) collective-permute-start(bf16[4,56,256]{2,1,0:T(8,128)(2,1)S(1)} %get-tuple-element.124), channel_id=1, source_target_pairs={{0,3},{1,2},{2,1},{3,0},{4,7},{5,6},{6,5},{7,4},{8,11},{9,10},{10,... | collective-permute-start | bytes 344072 | tf_op jit(solution)/shard_map/cond/branch_1_fun/ppermute | solution.py:447
  54.3 0.0 collective-permute-done.32
  54.3 0.0 collective-permute-done.33
  54.3 1.3 %collective-permute-done.34.refs_1_ = bf16[4,56,256]{2,1,0:T(8,128)(2,1)S(1)} collective-permute-done((bf16[4,56,256]{2,1,0:T(8,128)(2,1)S(1)}, bf16[4,56,256]{2,1,0:T(8,128)(2,1)S(1)}, u32[]{:S(2)}, u32[]{:S(2)}) %collective-permute-start.34) | collective-permute-done | bytes 114720 | tf_op jit(solution)/shard_map/cond/branch_1_fun/ppermute | solution.py:447
  55.6 0.2 collective-permute-done.35.refs_2_
  55.8 1.8 %collective-permute-done.36.refs_3_ = bf16[4,56,256]{2,1,0:T(8,128)(2,1)S(1)} collective-permute-done((bf16[4,56,256]{2,1,0:T(8,128)(2,1)S(1)}, bf16[4,56,256]{2,1,0:T(8,128)(2,1)S(1)}, u32[]{:S(2)}, u32[]{:S(2)}) %collective-permute-start.36) | collective-permute-done | bytes 114720 | tf_op jit(solution)/shard_map/cond/branch_1_fun/ppermute | solution.py:447
  57.7 0.2 branch_1_fun.27
  57.9 0.1 collective-permute-start.37
  57.9 1.6 %collective-permute-start.38 = (bf16[128,256]{1,0:T(8,128)(2,1)S(1)}, bf16[128,256]{1,0:T(8,128)(2,1)S(1)}, u32[]{:S(2)}, u32[]{:S(2)}) collective-permute-start(bf16[128,256]{1,0:T(8,128)(2,1)S(1)} %get-tuple-element.126), channel_id=1, source_target_pairs={{0,28},{1,29},{2,30},{3,31},{4,8},{5,9},{6,10},{7,11},{8,4},{9,5},... | collective-permute-start | bytes 196616 | tf_op jit(solution)/shard_map/cond/branch_1_fun/ppermute | solution.py:447
  59.5 0.2 collective-permute-start.39
  59.7 2.6 %branch_1_fun.29 = bf16[1,1536,256]{2,1,0:T(8,128)(2,1)} custom-call(bf16[1536,224]{1,0:T(8,128)(2,1)S(1)} %get-tuple-element.130.refs_0_, bf16[1536,224]{1,0:T(8,128)(2,1)S(1)} %get-tuple-element.131.refs_1_, bf16[1536,224]{1,0:T(8,128)(2,1)S(1)} %get-tuple-element.132.refs_2_, bf16[1536,224]{1,0:T(8,128)(2,1)S(1)} %get-tuple-element.133.refs_3_, ...), custom_call_target="tpu_custom_call" | custom-call | flops 1409286144 | bytes 1048576 | tf_op jit(solution)/shard_map/cond/branch_1_fun/pallas_call | solution.py:429
  62.3 0.0 collective-permute-done.37.near_ref
  62.3 1.2 %collective-permute-done.38.far_ref = bf16[128,256]{1,0:T(8,128)(2,1)S(1)} collective-permute-done((bf16[128,256]{1,0:T(8,128)(2,1)S(1)}, bf16[128,256]{1,0:T(8,128)(2,1)S(1)}, u32[]{:S(2)}, u32[]{:S(2)}) %collective-permute-start.38) | collective-permute-done | bytes 65568 | tf_op jit(solution)/shard_map/cond/branch_1_fun/ppermute | solution.py:447
  63.5 2.1 %collective-permute-done.39.cross_ref = bf16[128,256]{1,0:T(8,128)(2,1)S(1)} collective-permute-done((bf16[128,256]{1,0:T(8,128)(2,1)S(1)}, bf16[128,256]{1,0:T(8,128)(2,1)S(1)}, u32[]{:S(2)}, u32[]{:S(2)}) %collective-permute-start.39) | collective-permute-done | bytes 65568 | tf_op jit(solution)/shard_map/cond/branch_1_fun/ppermute | solution.py:447
  65.6 0.7 branch_1_fun.28
  (1 shorter events, 0.0 us)
Async XLA Ops:
  0.6 7.4 %collective-permute-start.40 = (bf16[2,56,256]{2,1,0:T(8,128)(2,1)}, bf16[2,56,256]{2,1,0:T(8,128)(2,1)S(1)}, u32[]{:S(2)}, u32[]{:S(2)}) collective-permute-start(bf16[2,56,256]{2,1,0:T(8,128)(2,1)} %param.8), channel_id=1, source_target_pairs={{0,4},{1,5},{2,6},{3,7},{4,0},{5,1},{6,2},{7,3},{8,12},{9,13},{10,... | collective-permute-start | bytes 172040 | tf_op jit(solution)/shard_map/ppermute | solution.py:447
  1.2 7.0 %collective-permute-start.41 = (bf16[2,56,256]{2,1,0:T(8,128)(2,1)}, bf16[2,56,256]{2,1,0:T(8,128)(2,1)S(1)}, u32[]{:S(2)}, u32[]{:S(2)}) collective-permute-start(bf16[2,56,256]{2,1,0:T(8,128)(2,1)} %param.8), channel_id=1, source_target_pairs={{0,28},{1,29},{2,30},{3,31},{4,8},{5,9},{6,10},{7,11},{8,4},{9,5},... | collective-permute-start | bytes 172040 | tf_op jit(solution)/shard_map/ppermute | solution.py:447
  5.9 5.3 %collective-permute-start.42 = (bf16[2,56,256]{2,1,0:T(8,128)(2,1)}, bf16[2,56,256]{2,1,0:T(8,128)(2,1)S(1)}, u32[]{:S(2)}, u32[]{:S(2)}) collective-permute-start(bf16[2,56,256]{2,1,0:T(8,128)(2,1)} %param.8), channel_id=1, source_target_pairs={{0,16},{1,17},{2,18},{3,19},{4,20},{5,21},{6,22},{7,23},{8,24},{9,... | collective-permute-start | bytes 172040 | tf_op jit(solution)/shard_map/ppermute | solution.py:447
  11.2 9.0 %copy-start.1 = (bf16[1,1536,256]{2,1,0:T(8,128)(2,1)S(1)}, bf16[1,1536,256]{2,1,0:T(8,128)(2,1)}, u32[]{:S(2)}) copy-start(bf16[1,1536,256]{2,1,0:T(8,128)(2,1)} %get-tuple-element.154) | copy-start | bytes 2359300 | tf_op jit(solution)/shard_map/cond
  11.4 5.9 %collective-permute-start.23 = (bf16[4,56,256]{2,1,0:T(8,128)(2,1)S(1)}, bf16[4,56,256]{2,1,0:T(8,128)(2,1)S(1)}, u32[]{:S(2)}, u32[]{:S(2)}) collective-permute-start(bf16[4,56,256]{2,1,0:T(8,128)(2,1)S(1)} %branch_1_fun.16.refs_0_), channel_id=1, source_target_pairs={{0,1},{1,0},{2,3},{3,2},{4,5},{5,4},{6,7},{7,6},{8,9},{9,8},{10,11... | collective-permute-start | bytes 344072 | tf_op jit(solution)/shard_map/cond/branch_1_fun/ppermute | solution.py:447
  12.9 5.9 %collective-permute-start.24 = (bf16[4,56,256]{2,1,0:T(8,128)(2,1)S(1)}, bf16[4,56,256]{2,1,0:T(8,128)(2,1)S(1)}, u32[]{:S(2)}, u32[]{:S(2)}) collective-permute-start(bf16[4,56,256]{2,1,0:T(8,128)(2,1)S(1)} %branch_1_fun.16.refs_0_), channel_id=1, source_target_pairs={{0,2},{1,3},{2,0},{3,1},{4,6},{5,7},{6,4},{7,5},{8,10},{9,11},{10,... | collective-permute-start | bytes 344072 | tf_op jit(solution)/shard_map/cond/branch_1_fun/ppermute | solution.py:447
  14.5 5.7 %collective-permute-start.25 = (bf16[4,56,256]{2,1,0:T(8,128)(2,1)S(1)}, bf16[4,56,256]{2,1,0:T(8,128)(2,1)S(1)}, u32[]{:S(2)}, u32[]{:S(2)}) collective-permute-start(bf16[4,56,256]{2,1,0:T(8,128)(2,1)S(1)} %branch_1_fun.16.refs_0_), channel_id=1, source_target_pairs={{0,3},{1,2},{2,1},{3,0},{4,7},{5,6},{6,5},{7,4},{8,11},{9,10},{10,... | collective-permute-start | bytes 344072 | tf_op jit(solution)/shard_map/cond/branch_1_fun/ppermute | solution.py:447
  21.7 8.4 %collective-permute-start.26 = (f32[232,256]{1,0:T(8,128)S(1)}, f32[232,256]{1,0:T(8,128)S(1)}, u32[]{:S(2)}, u32[]{:S(2)}) collective-permute-start(f32[232,256]{1,0:T(8,128)S(1)} %get-tuple-element.105), channel_id=1, source_target_pairs={{0,1},{1,0},{2,3},{3,2},{4,5},{5,4},{6,7},{7,6},{8,9},{9,8},{10,11... | collective-permute-start | bytes 712712 | tf_op jit(solution)/shard_map/cond/branch_1_fun/ppermute | solution.py:447
  23.9 11.0 %collective-permute-start.27 = (f32[232,256]{1,0:T(8,128)S(1)}, f32[232,256]{1,0:T(8,128)S(1)}, u32[]{:S(2)}, u32[]{:S(2)}) collective-permute-start(f32[232,256]{1,0:T(8,128)S(1)} %get-tuple-element.106), channel_id=1, source_target_pairs={{0,2},{1,3},{2,0},{3,1},{4,6},{5,7},{6,4},{7,5},{8,10},{9,11},{10,... | collective-permute-start | bytes 712712 | tf_op jit(solution)/shard_map/cond/branch_1_fun/ppermute | solution.py:447
  26.0 8.9 %collective-permute-start.28 = (f32[232,256]{1,0:T(8,128)S(1)}, f32[232,256]{1,0:T(8,128)S(1)}, u32[]{:S(2)}, u32[]{:S(2)}) collective-permute-start(f32[232,256]{1,0:T(8,128)S(1)} %get-tuple-element.107), channel_id=1, source_target_pairs={{0,3},{1,2},{2,1},{3,0},{4,7},{5,6},{6,5},{7,4},{8,11},{9,10},{10,... | collective-permute-start | bytes 712712 | tf_op jit(solution)/shard_map/cond/branch_1_fun/ppermute | solution.py:447
  35.9 6.5 %collective-permute-start.31 = (bf16[240,256]{1,0:T(8,128)(2,1)S(1)}, bf16[240,256]{1,0:T(8,128)(2,1)S(1)}, u32[]{:S(2)}, u32[]{:S(2)}) collective-permute-start(bf16[240,256]{1,0:T(8,128)(2,1)S(1)} %get-tuple-element.108.d_ref.refs_4_.refs_12_), channel_id=1, source_target_pairs={{0,3},{1,2},{2,1},{3,0},{4,7},{5,6},{6,5},{7,4},{8,11},{9,10},{10,... | collective-permute-start | bytes 368648 | tf_op jit(solution)/shard_map/cond/branch_1_fun/ppermute | solution.py:447
  39.5 4.9 %collective-permute-start.30 = (bf16[240,256]{1,0:T(8,128)(2,1)S(1)}, bf16[240,256]{1,0:T(8,128)(2,1)S(1)}, u32[]{:S(2)}, u32[]{:S(2)}) collective-permute-start(bf16[240,256]{1,0:T(8,128)(2,1)S(1)} %get-tuple-element.108.d_ref.refs_4_.refs_12_), channel_id=1, source_target_pairs={{0,2},{1,3},{2,0},{3,1},{4,6},{5,7},{6,4},{7,5},{8,10},{9,11},{10,... | collective-permute-start | bytes 368648 | tf_op jit(solution)/shard_map/cond/branch_1_fun/ppermute | solution.py:447
  40.7 5.5 %collective-permute-start.29 = (bf16[240,256]{1,0:T(8,128)(2,1)S(1)}, bf16[240,256]{1,0:T(8,128)(2,1)S(1)}, u32[]{:S(2)}, u32[]{:S(2)}) collective-permute-start(bf16[240,256]{1,0:T(8,128)(2,1)S(1)} %get-tuple-element.108.d_ref.refs_4_.refs_12_), channel_id=1, source_target_pairs={{0,1},{1,0},{2,3},{3,2},{4,5},{5,4},{6,7},{7,6},{8,9},{9,8},{10,11... | collective-permute-start | bytes 368648 | tf_op jit(solution)/shard_map/cond/branch_1_fun/ppermute | solution.py:447
  47.2 7.1 %collective-permute-start.32 = (f32[1,128]{1,0:T(1,128)S(1)}, f32[1,128]{1,0:T(1,128)S(1)}, u32[]{:S(2)}, u32[]{:S(2)}) collective-permute-start(f32[1,128]{1,0:T(1,128)S(1)} %get-tuple-element.120), channel_id=1, source_target_pairs={{0,8},{1,9},{2,10},{3,11},{4,12},{5,13},{6,14},{7,15},{8,0},{9,1},... | collective-permute-start | bytes 1544 | tf_op jit(solution)/shard_map/cond/branch_1_fun/ppermute | solution.py:447
  47.3 7.0 %collective-permute-start.33 = (f32[1,128]{1,0:T(1,128)S(1)}, f32[1,128]{1,0:T(1,128)S(1)}, u32[]{:S(2)}, u32[]{:S(2)}) collective-permute-start(f32[1,128]{1,0:T(1,128)S(1)} %get-tuple-element.120), channel_id=1, source_target_pairs={{0,16},{1,17},{2,18},{3,19},{4,20},{5,21},{6,22},{7,23},{8,24},{9,... | collective-permute-start | bytes 1544 | tf_op jit(solution)/shard_map/cond/branch_1_fun/ppermute | solution.py:447
  50.8 4.8 %collective-permute-start.34 = (bf16[4,56,256]{2,1,0:T(8,128)(2,1)S(1)}, bf16[4,56,256]{2,1,0:T(8,128)(2,1)S(1)}, u32[]{:S(2)}, u32[]{:S(2)}) collective-permute-start(bf16[4,56,256]{2,1,0:T(8,128)(2,1)S(1)} %get-tuple-element.122), channel_id=1, source_target_pairs={{0,1},{1,0},{2,3},{3,2},{4,5},{5,4},{6,7},{7,6},{8,9},{9,8},{10,11... | collective-permute-start | bytes 344072 | tf_op jit(solution)/shard_map/cond/branch_1_fun/ppermute | solution.py:447
  51.0 4.8 %collective-permute-start.35 = (bf16[4,56,256]{2,1,0:T(8,128)(2,1)S(1)}, bf16[4,56,256]{2,1,0:T(8,128)(2,1)S(1)}, u32[]{:S(2)}, u32[]{:S(2)}) collective-permute-start(bf16[4,56,256]{2,1,0:T(8,128)(2,1)S(1)} %get-tuple-element.123), channel_id=1, source_target_pairs={{0,2},{1,3},{2,0},{3,1},{4,6},{5,7},{6,4},{7,5},{8,10},{9,11},{10,... | collective-permute-start | bytes 344072 | tf_op jit(solution)/shard_map/cond/branch_1_fun/ppermute | solution.py:447
  52.0 5.7 %collective-permute-start.36 = (bf16[4,56,256]{2,1,0:T(8,128)(2,1)S(1)}, bf16[4,56,256]{2,1,0:T(8,128)(2,1)S(1)}, u32[]{:S(2)}, u32[]{:S(2)}) collective-permute-start(bf16[4,56,256]{2,1,0:T(8,128)(2,1)S(1)} %get-tuple-element.124), channel_id=1, source_target_pairs={{0,3},{1,2},{2,1},{3,0},{4,7},{5,6},{6,5},{7,4},{8,11},{9,10},{10,... | collective-permute-start | bytes 344072 | tf_op jit(solution)/shard_map/cond/branch_1_fun/ppermute | solution.py:447
  57.9 4.4 %collective-permute-start.37 = (bf16[128,256]{1,0:T(8,128)(2,1)S(1)}, bf16[128,256]{1,0:T(8,128)(2,1)S(1)}, u32[]{:S(2)}, u32[]{:S(2)}) collective-permute-start(bf16[128,256]{1,0:T(8,128)(2,1)S(1)} %get-tuple-element.125), channel_id=1, source_target_pairs={{0,4},{1,5},{2,6},{3,7},{4,0},{5,1},{6,2},{7,3},{8,12},{9,13},{10,... | collective-permute-start | bytes 196616 | tf_op jit(solution)/shard_map/cond/branch_1_fun/ppermute | solution.py:447
  57.9 5.6 %collective-permute-start.38 = (bf16[128,256]{1,0:T(8,128)(2,1)S(1)}, bf16[128,256]{1,0:T(8,128)(2,1)S(1)}, u32[]{:S(2)}, u32[]{:S(2)}) collective-permute-start(bf16[128,256]{1,0:T(8,128)(2,1)S(1)} %get-tuple-element.126), channel_id=1, source_target_pairs={{0,28},{1,29},{2,30},{3,31},{4,8},{5,9},{6,10},{7,11},{8,4},{9,5},... | collective-permute-start | bytes 196616 | tf_op jit(solution)/shard_map/cond/branch_1_fun/ppermute | solution.py:447
  59.5 6.1 %collective-permute-start.39 = (bf16[128,256]{1,0:T(8,128)(2,1)S(1)}, bf16[128,256]{1,0:T(8,128)(2,1)S(1)}, u32[]{:S(2)}, u32[]{:S(2)}) collective-permute-start(bf16[128,256]{1,0:T(8,128)(2,1)S(1)} %get-tuple-element.127), channel_id=1, source_target_pairs={{0,16},{1,17},{2,18},{3,19},{4,20},{5,21},{6,22},{7,23},{8,24},{9,... | collective-permute-start | bytes 196616 | tf_op jit(solution)/shard_map/cond/branch_1_fun/ppermute | solution.py:447
